TPU v7x, 32 devices: a whole 2x2x4 slice. The times are simulated.
32 devices in a mesh: gx: 4 (over y, core), gy: 4 (over z), gz: 2 (over x).
Axes of the slice: x: 2, y: 2, z: 4, core: 2. Of those that a mesh axis runs over, the one named last changes fastest.
Arguments:
- field: float32 [64, 64, 16, 512], P(None, 'gz', 'gx', 'gy'), may hold values from 0.01 to 1
- courant_x: float32 [64, 16, 512], P('gz', 'gx', 'gy'), may hold values from -0.45 to 0.45
- courant_y: float32 [64, 16, 512], P('gz', 'gx', 'gy'), may hold values from -0.45 to 0.45
- supersat: float32 [64, 16, 512], P('gz', 'gx', 'gy'), may hold values from -0.5 to 0.5
- cloud_mask: int32 [64, 16, 512], P('gz', 'gx', 'gy'), may hold values 0 or 1
- fall_speed: float32 [64], replicated, may hold values from 0.05 to 40
- growth: float32 [47], replicated, may hold values from 0.2 to 1.6
- activation_threshold: float32 [16], replicated, may hold values from -0.2 to 0.4
- kernel_rate: float32 [48, 8], replicated, may hold values from 0.02 to 0.2
- partner: int32 [48, 8], replicated, may hold values from 0 to 47
- target: int32 [48, 8], replicated, may hold values from 0 to 47
Outputs:
- updated: float32 [64, 64, 16, 512], P(None, 'gz', 'gx', 'gy')
Inputs may be any that keep to these rules, and one draw needn't show every extreme that they name: `partner`: bin indices of drop bins. `target`: bin indices of drop bins.
All inputs are finite; a program needn't handle non-finite values. No bound on the sum of `cloud_mask` on one device may be relied on, other than what follows from the above.
Results may differ from a plain program's by a relative error of at most 0.0003.
Values sent between devices are 32-bit elements; how exact they have to be, the bound alone decides.
A program may use at most 128 MiB of HBM per device.

v0:
```python
import jax
import jax.numpy as jnp
from jax import lax
from jax.sharding import PartitionSpec as P


def padded_2(cells, sides, width):
    for axis, dim in sides:
        count = lax.axis_size(axis)
        head = lax.slice_in_dim(cells, 0, width, axis=dim)
        tail = lax.slice_in_dim(cells, cells.shape[dim] - width, cells.shape[dim], axis=dim)
        cells = jnp.concatenate(
            [
                lax.ppermute(tail, axis, [(i, (i + 1) % count) for i in range(count)]),
                cells,
                lax.ppermute(head, axis, [((i + 1) % count, i) for i in range(count)]),
            ],
            axis=dim,
        )
    return cells


def advect(padded, num_bins):
    mass = padded[:num_bins]
    cour_x = padded[num_bins]
    cour_y = padded[num_bins + 1]
    edge_x = cour_x[:, :-1, 1:-1]
    flux_x = (
        jnp.maximum(edge_x, 0.0) * mass[:, :, :-1, 1:-1]
        + jnp.minimum(edge_x, 0.0) * mass[:, :, 1:, 1:-1]
    )
    edge_y = cour_y[:, 1:-1, :-1]
    flux_y = (
        jnp.maximum(edge_y, 0.0) * mass[:, :, 1:-1, :-1]
        + jnp.minimum(edge_y, 0.0) * mass[:, :, 1:-1, 1:]
    )
    inner = mass[:, :, 1:-1, 1:-1]
    return inner - (flux_x[:, :, 1:] - flux_x[:, :, :-1]) - (flux_y[..., 1:] - flux_y[..., :-1])


def settle(mass, fall_speed, depth):
    ratio = fall_speed / (1.0 + fall_speed)
    level = jnp.arange(depth, dtype=jnp.int32)
    distance = (level[None, :] - level[:, None]).astype(jnp.float32)
    power = jnp.exp(jnp.maximum(distance, 0.0)[None] * jnp.log(ratio)[:, None, None])
    matrix = jnp.where(distance[None] >= 0.0, power / (1.0 + fall_speed)[:, None, None], 0.0)
    return jnp.einsum("bkm,bmxy->bkxy", matrix, mass, precision=lax.Precision.HIGHEST)


def collide(grown, cloudy, select, route, rates, num_slots):
    num_drops = grown.shape[0]
    depth = grown.shape[1]
    block = 8
    while depth % block:
        block = block // 2

    def one_block(number, result):
        start = number * block
        piece = lax.dynamic_slice_in_dim(grown, start, block, 1)
        masked = lax.dynamic_slice_in_dim(cloudy, start, block, 0)
        flat = piece.reshape(num_drops, -1)
        picked = jnp.dot(select, flat, precision=lax.Precision.HIGHEST)
        rate = rates[:, None] * jnp.tile(flat, (num_slots, 1)) * picked
        loss = jnp.sum(rate.reshape(num_slots, num_drops, -1), 0)
        gain = jnp.dot(route, rate, precision=lax.Precision.HIGHEST)
        fresh = flat + masked.reshape(1, -1) * (gain - loss)
        return lax.dynamic_update_slice_in_dim(result, fresh.reshape(piece.shape), start, 1)

    return lax.fori_loop(0, depth // block, one_block, grown)


def microphysics(
    settled, saturation, cloudy, growth, activation_threshold, select, route, rates, num_slots
):
    num_drops = growth.shape[0] + 1
    drop_mass = settled[:num_drops]
    aero_mass = settled[num_drops:]
    face = growth[:, None, None, None] * saturation[None]
    cond_flux = jnp.maximum(face, 0.0) * drop_mass[:-1] + jnp.minimum(face, 0.0) * drop_mass[1:]
    zero_face = jnp.zeros_like(cond_flux[:1])
    grown = (
        drop_mass
        + jnp.concatenate([zero_face, cond_flux], 0)
        - jnp.concatenate([cond_flux, zero_face], 0)
    )
    activated = (
        jnp.maximum(saturation[None] - activation_threshold[:, None, None, None], 0.0) * aero_mass
    )
    grown = jnp.concatenate([grown[:1] + jnp.sum(activated, 0, keepdims=True), grown[1:]], 0)
    drops_after = collide(grown, cloudy, select, route, rates, num_slots)
    return jnp.concatenate([drops_after, aero_mass - activated], 0)


def shards(
    field,
    courant_x,
    courant_y,
    supersat,
    cloud_mask,
    fall_speed,
    growth,
    activation_threshold,
    kernel_rate,
    partner,
    target,
):
    num_bins = field.shape[0]
    num_drops, num_slots = partner.shape
    stacked = jnp.concatenate([field, courant_x[None], courant_y[None]], 0)
    padded = padded_2(stacked, (("gx", 2), ("gy", 3)), 1)
    advected = advect(padded, num_bins)
    mask_float = cloud_mask.astype(jnp.float32)
    drop_ids = jnp.arange(num_drops, dtype=jnp.int32)
    select = (partner.T.reshape(-1)[:, None] == drop_ids[None, :]).astype(jnp.float32)
    route = (drop_ids[:, None] == target.T.reshape(-1)[None, :]).astype(jnp.float32)
    rates = kernel_rate.T.reshape(-1)
    bundle = jnp.concatenate([advected, supersat[None], mask_float[None]], 0)
    column = lax.all_to_all(bundle, "gz", split_axis=2, concat_axis=1, tiled=True)
    mass = column[:num_bins]
    settled = settle(mass, fall_speed, mass.shape[1])
    finished = microphysics(
        settled,
        column[num_bins],
        column[num_bins + 1],
        growth,
        activation_threshold,
        select,
        route,
        rates,
        num_slots,
    )
    return lax.all_to_all(finished, "gz", split_axis=1, concat_axis=2, tiled=True)


def solution(mesh):
    return jax.shard_map(
        shards,
        mesh=mesh,
        in_specs=(
            P(None, "gz", "gx", "gy"),
            P("gz", "gx", "gy"),
            P("gz", "gx", "gy"),
            P("gz", "gx", "gy"),
            P("gz", "gx", "gy"),
            P(),
            P(),
            P(),
            P(),
            P(),
            P(),
        ),
        out_specs=P(None, "gz", "gx", "gy"),
        check_vma=False,
    )
```

profile of v0, /device:TPU:6, one launch (start us, length us, event | category | flops | bytes accessed | tf_op | source)
XLA Modules:
  0.0 326.7 jit_solution(16030387712345461029)
XLA Ops:
  0.0 2.7 copy.25
  3.6 22.9 %collective-permute-done.1 = f32[66,32,1,128]{3,1,2,0:T(8,128)S(1)} collective-permute-done((f32[66,32,1,128]{3,1,2,0:T(8,128)S(1)}, f32[66,32,1,128]{3,1,2,0:T(8,128)S(1)}, u32[]{:S(2)}, u32[]{:S(2)}) %collective-permute-start.1) | collective-permute-done | bytes 1081376 | tf_op jit(solution)/shard_map/ppermute | solution.py:16
  26.4 2.8 collective-permute-done
  29.2 1.0 copy-done.3
  30.2 3.2 pad_maximum_fusion.10
  33.5 11.3 %fusion.39 = (f32[66,32,6,1]{3,1,2,0:T(8,128)}, f32[66,32,6,1]{3,1,2,0:T(8,128)}) fusion(f32[66,32,6,128]{3,1,2,0:T(8,128)} %pad_maximum_fusion.10), kind=kLoop, calls=%fused_computation.96 | loop fusion | bytes 202752 | tf_op jit(solution)/shard_map/slice | solution.py:11
  44.8 5.6 %copy.22 = f32[66,32,6,1]{0,1,3,2:T(8,128)S(1)} copy(f32[66,32,6,1]{3,1,2,0:T(8,128)} %get-tuple-element.180) | data formatting | bytes 101376 | tf_op jit(solution)/shard_map/slice | solution.py:10
  50.4 3.7 %collective-permute-start.3 = (f32[66,32,6,1]{0,1,3,2:T(8,128)S(1)}, f32[66,32,6,1]{0,1,3,2:T(8,128)S(1)}, u32[]{:S(2)}, u32[]{:S(2)}) collective-permute-start(f32[66,32,6,1]{0,1,3,2:T(8,128)S(1)} %copy.22), channel_id=1, source_target_pairs={{2,0},{4,2},{6,4},{0,6},{3,1},{5,3},{7,5},{1,7},{10,8},{12,10},{14... | collective-permute-start | bytes 152072 | tf_op jit(solution)/shard_map/ppermute | solution.py:16
  54.0 5.6 %copy.21 = f32[66,32,6,1]{0,1,3,2:T(8,128)S(1)} copy(f32[66,32,6,1]{3,1,2,0:T(8,128)} %get-tuple-element.179) | data formatting | bytes 101376 | tf_op jit(solution)/shard_map/slice | solution.py:11
  61.1 6.5 %copy.24 = f32[66,32,6,1]{3,1,2,0:T(8,128)} copy(f32[66,32,6,1]{0,1,3,2:T(8,128)S(1)} %collective-permute-done.3) | data formatting | bytes 101376 | tf_op jit(solution)/shard_map/ppermute | solution.py:16
  67.6 7.4 %copy.23 = f32[66,32,6,1]{3,1,2,0:T(8,128)} copy(f32[66,32,6,1]{0,1,3,2:T(8,128)} %collective-permute-done.2) | data formatting | bytes 101376 | tf_op jit(solution)/shard_map/ppermute | solution.py:14
  75.0 1.4 maximum_bitcast_fusion
  77.4 1.3 slice-done.1
  78.7 1.8 copy-done.2
  80.8 10.3 %fusion.12 = f32[64,32,4,129]{3,1,2,0:T(8,128)S(1)} fusion(f32[66,32,6,1]{3,1,2,0:T(8,128)S(1)} %bitcast.76, f32[66,32,1,128]{3,1,2,0:T(8,128)S(1)} %collective-permute-done.1, f32[66,32,1,128]{3,1,2,0:T(8,128)S(1)} %copy-done.4, f32[1,32,4,128]{3,1,2,0:T(8,128)S(1)} %get-tuple-element.193, f32[1,32,4,128]{3,1,2,0:T(8,128)S(1)} %get-tuple-element.194, ...), kind=kLoop, calls=%fused_computation.19 | loop fusion | flops 13737984 | bytes 10948608 | tf_op jit(solution)/shard_map/add | solution.py:34
  91.0 1.4 fusion.15
  93.2 2.0 fusion.17
  95.8 2.7 copy.30
  98.5 6.3 %all-to-all-start = ((f32[66,32,4,128]{3,1,0,2:T(8,128)}), f32[66,32,4,128]{3,1,0,2:T(8,128)}, u32[]{:S(2)}, u32[]{:S(2)}) async-start(f32[66,32,4,128]{3,1,0,2:T(8,128)} %copy.30), calls=%async_computation | async-start | bytes 8650752 | tf_op jit(solution)/shard_map/all_to_all | solution.py:118
  105.1 47.2 %all-to-all-done = f32[66,32,4,128]{3,1,0,2:T(8,128)} async-done(((f32[66,32,4,128]{3,1,0,2:T(8,128)}), f32[66,32,4,128]{3,1,0,2:T(8,128)}, u32[]{:S(2)}, u32[]{:S(2)}) %all-to-all-start) | async-done | bytes 4325408 | tf_op jit(solution)/shard_map/all_to_all | solution.py:118
  152.4 2.9 copy.52
  155.7 4.6 %fusion.23 = f32[64,64,2,128]{3,1,2,0:T(8,128)S(1)} fusion(f32[64,64,2,128]{3,1,2,0:T(8,128)S(1)} %bitcast.80, f32[64]{0:T(128)S(1)} %get-tuple-element.192, f32[64]{0:T(128)S(1)} %get-tuple-element.191, f32[64,64]{1,0:T(8,128)S(1)} %convert_maximum_fusion, pred[64,64]{1,0:T(8,128)(4,1)S(1)} %convert_compare_fusion), kind=kOutput, calls=%fused_computation.55 | convolution fusion | flops 806092800 | bytes 8409600 | tf_op jit(solution)/shard_map/bkm,bmxy->bkxy/dot_general | solution.py:47
  160.7 1.8 copy.36
  163.3 1.0 fusion.19
  164.7 1.9 pad_maximum_fusion.19
  166.6 6.0 %copy.40 = f32[48,64,2,128]{3,2,0,1:T(2,128)} copy(f32[48,64,2,128]{3,1,2,0:T(8,128)} %pad_maximum_fusion.19) | data formatting | bytes 6291456
  173.2 95.6 %while.15 = (s32[]{:T(128)}, f32[48,64,2,128]{3,2,0,1:T(2,128)}, f32[48,64,2,128]{3,1,2,0:T(8,128)}, f32[64,2,128]{2,1,0:T(2,128)}, f32[8,48]{1,0:T(8,128)}, /*i...) while((s32[]{:T(128)}, f32[48,64,2,128]{3,2,0,1:T(2,128)}, ...), condition=%wide.wide.region_3.4_spmd.clone, body=%wide.wide.region_1.3_spmd.clone.sunk | while | flops 908599296 | bytes 15364803 | solution.py:69
  173.2 1.0 constant_dynamic-slice_fusion.6
  174.8 2.7 bitcast_multiply_fusion.4
  177.5 0.9 reduce_sum.27
  179.1 3.8 %fusion.58 = f32[48,2048]{1,0:T(8,128)} fusion(f32[48,2048]{1,0:T(8,128)S(1)} %reshape.83, f32[48,2048]{1,0:T(8,128)} %reduce_sum.27, f32[384,2048]{1,0:T(8,128)S(1)} %bitcast_multiply_fusion.4, f32[2048]{0:T(1024)S(1)} %bitcast.81, s32[384]{0:T(512)S(1)} %get-tuple-element.304), kind=kOutput, calls=%fused_computation.7.clone.clone.1 | convolution fusion | flops 453316608 | bytes 4335104 | tf_op jit(solution)/shard_map/while/body/eval_jaxpr/dot_general | solution.py:65
  182.9 1.3 reshape.84
  185.2 1.0 constant_dynamic-slice_fusion.6
  186.7 2.7 bitcast_multiply_fusion.4
  189.4 0.9 reduce_sum.27
  191.1 3.8 %fusion.58 = f32[48,2048]{1,0:T(8,128)} fusion(f32[48,2048]{1,0:T(8,128)S(1)} %reshape.83, f32[48,2048]{1,0:T(8,128)} %reduce_sum.27, f32[384,2048]{1,0:T(8,128)S(1)} %bitcast_multiply_fusion.4, f32[2048]{0:T(1024)S(1)} %bitcast.81, s32[384]{0:T(512)S(1)} %get-tuple-element.304), kind=kOutput, calls=%fused_computation.7.clone.clone.1 | convolution fusion | flops 453316608 | bytes 4335104 | tf_op jit(solution)/shard_map/while/body/eval_jaxpr/dot_general | solution.py:65
  194.9 1.3 reshape.84
  197.1 1.0 constant_dynamic-slice_fusion.6
  198.7 2.7 bitcast_multiply_fusion.4
  203.0 3.8 %fusion.58 = f32[48,2048]{1,0:T(8,128)} fusion(f32[48,2048]{1,0:T(8,128)S(1)} %reshape.83, f32[48,2048]{1,0:T(8,128)} %reduce_sum.27, f32[384,2048]{1,0:T(8,128)S(1)} %bitcast_multiply_fusion.4, f32[2048]{0:T(1024)S(1)} %bitcast.81, s32[384]{0:T(512)S(1)} %get-tuple-element.304), kind=kOutput, calls=%fused_computation.7.clone.clone.1 | convolution fusion | flops 453316608 | bytes 4335104 | tf_op jit(solution)/shard_map/while/body/eval_jaxpr/dot_general | solution.py:65
  206.8 1.3 reshape.84
  209.1 1.0 constant_dynamic-slice_fusion.6
  210.6 2.7 bitcast_multiply_fusion.4
  215.0 3.8 %fusion.58 = f32[48,2048]{1,0:T(8,128)} fusion(f32[48,2048]{1,0:T(8,128)S(1)} %reshape.83, f32[48,2048]{1,0:T(8,128)} %reduce_sum.27, f32[384,2048]{1,0:T(8,128)S(1)} %bitcast_multiply_fusion.4, f32[2048]{0:T(1024)S(1)} %bitcast.81, s32[384]{0:T(512)S(1)} %get-tuple-element.304), kind=kOutput, calls=%fused_computation.7.clone.clone.1 | convolution fusion | flops 453316608 | bytes 4335104 | tf_op jit(solution)/shard_map/while/body/eval_jaxpr/dot_general | solution.py:65
  218.8 1.3 reshape.84
  221.0 1.0 constant_dynamic-slice_fusion.6
  222.6 2.7 bitcast_multiply_fusion.4
  227.0 3.8 %fusion.58 = f32[48,2048]{1,0:T(8,128)} fusion(f32[48,2048]{1,0:T(8,128)S(1)} %reshape.83, f32[48,2048]{1,0:T(8,128)} %reduce_sum.27, f32[384,2048]{1,0:T(8,128)S(1)} %bitcast_multiply_fusion.4, f32[2048]{0:T(1024)S(1)} %bitcast.81, s32[384]{0:T(512)S(1)} %get-tuple-element.304), kind=kOutput, calls=%fused_computation.7.clone.clone.1 | convolution fusion | flops 453316608 | bytes 4335104 | tf_op jit(solution)/shard_map/while/body/eval_jaxpr/dot_general | solution.py:65
  230.8 1.3 reshape.84
  233.0 1.0 constant_dynamic-slice_fusion.6
  234.5 2.7 bitcast_multiply_fusion.4
  238.9 3.8 %fusion.58 = f32[48,2048]{1,0:T(8,128)} fusion(f32[48,2048]{1,0:T(8,128)S(1)} %reshape.83, f32[48,2048]{1,0:T(8,128)} %reduce_sum.27, f32[384,2048]{1,0:T(8,128)S(1)} %bitcast_multiply_fusion.4, f32[2048]{0:T(1024)S(1)} %bitcast.81, s32[384]{0:T(512)S(1)} %get-tuple-element.304), kind=kOutput, calls=%fused_computation.7.clone.clone.1 | convolution fusion | flops 453316608 | bytes 4335104 | tf_op jit(solution)/shard_map/while/body/eval_jaxpr/dot_general | solution.py:65
  242.7 1.3 reshape.84
  244.9 1.0 constant_dynamic-slice_fusion.6
  246.5 2.7 bitcast_multiply_fusion.4
  250.9 3.8 %fusion.58 = f32[48,2048]{1,0:T(8,128)} fusion(f32[48,2048]{1,0:T(8,128)S(1)} %reshape.83, f32[48,2048]{1,0:T(8,128)} %reduce_sum.27, f32[384,2048]{1,0:T(8,128)S(1)} %bitcast_multiply_fusion.4, f32[2048]{0:T(1024)S(1)} %bitcast.81, s32[384]{0:T(512)S(1)} %get-tuple-element.304), kind=kOutput, calls=%fused_computation.7.clone.clone.1 | convolution fusion | flops 453316608 | bytes 4335104 | tf_op jit(solution)/shard_map/while/body/eval_jaxpr/dot_general | solution.py:65
  254.7 1.3 reshape.84
  256.9 1.0 constant_dynamic-slice_fusion.6
  258.4 2.7 bitcast_multiply_fusion.4
  262.8 3.8 %fusion.58 = f32[48,2048]{1,0:T(8,128)} fusion(f32[48,2048]{1,0:T(8,128)S(1)} %reshape.83, f32[48,2048]{1,0:T(8,128)} %reduce_sum.27, f32[384,2048]{1,0:T(8,128)S(1)} %bitcast_multiply_fusion.4, f32[2048]{0:T(1024)S(1)} %bitcast.81, s32[384]{0:T(512)S(1)} %get-tuple-element.304), kind=kOutput, calls=%fused_computation.7.clone.clone.1 | convolution fusion | flops 453316608 | bytes 4335104 | tf_op jit(solution)/shard_map/while/body/eval_jaxpr/dot_general | solution.py:65
  266.6 1.3 reshape.84
  268.8 4.4 %pad_maximum_fusion.18 = f32[64,64,2,128]{3,2,0,1:T(2,128)S(1)} fusion(f32[16,64,2,128]{3,2,0,1:T(2,128)} %copy.36, f32[48,64,2,128]{3,2,0,1:T(2,128)} %get-tuple-element.129), kind=kLoop, calls=%fused_computation.48 | loop fusion | flops 1048576 | bytes 8388608 | tf_op jit(solution)/shard_map/concatenate | solution.py:91
  273.2 49.2 %all_to_all.33 = f32[64,64,2,128]{3,2,0,1:T(2,128)S(1)} all-to-all(f32[64,64,2,128]{3,2,0,1:T(2,128)S(1)} %pad_maximum_fusion.18), channel_id=1, replica_groups=mesh['gx'=4,'gy'=4,'gz'=2] {'gz'}, dimensions={1} | all-to-all | bytes 8388608 | tf_op jit(solution)/shard_map/all_to_all | solution.py:132
  322.4 4.4 %copy.37 = f32[64,32,2,2,128]{4,3,2,1,0:T(2,128)} copy(f32[64,32,2,2,128]{4,3,0,1,2:T(2,128)S(1)} %bitcast.79) | data formatting | bytes 8388608 | tf_op jit(solution)/shard_map/all_to_all | solution.py:132
  (101 shorter events, 30.2 us)
Async XLA Ops:
  0.0 2.8 copy-start.10
  0.0 2.8 copy-start.11
  2.8 26.5 %copy-start = (f32[64,32,4,128]{3,1,2,0:T(8,128)}, f32[64,32,4,128]{3,1,2,0:T(8,128)S(1)}, u32[]{:S(2)}) copy-start(f32[64,32,4,128]{3,1,2,0:T(8,128)S(1)} %copy.25) | copy-start | bytes 12582916
  3.0 23.4 %collective-permute-start.1 = (f32[66,32,1,128]{3,1,2,0:T(8,128)S(1)}, f32[66,32,1,128]{3,1,2,0:T(8,128)S(1)}, u32[]{:S(2)}, u32[]{:S(2)}) collective-permute-start(f32[66,32,1,128]{3,1,2,0:T(8,128)S(1)} %get-tuple-element.184), channel_id=1, source_target_pairs={{8,0},{16,8},{24,16},{0,24},{9,1},{17,9},{25,17},{1,25},{10,2},{18... | collective-permute-start | bytes 3244040 | tf_op jit(solution)/shard_map/ppermute | solution.py:16
  3.1 26.2 %collective-permute-start = (f32[66,32,1,128]{3,1,2,0:T(8,128)S(1)}, f32[66,32,1,128]{3,1,2,0:T(8,128)S(1)}, u32[]{:S(2)}, u32[]{:S(2)}) collective-permute-start(f32[66,32,1,128]{3,1,2,0:T(8,128)S(1)} %get-tuple-element.183), channel_id=1, source_target_pairs={{0,8},{8,16},{16,24},{24,0},{1,9},{9,17},{17,25},{25,1},{2,10},{10... | collective-permute-start | bytes 3244040 | tf_op jit(solution)/shard_map/ppermute | solution.py:14
  29.2 1.0 copy-start.3
  50.3 9.5 %copy-start.8 = (s32[32,4,128]{2,1,0:T(4,128)S(1)}, s32[32,4,128]{2,1,0:T(4,128)}, u32[]{:S(2)}) copy-start(s32[32,4,128]{2,1,0:T(4,128)} %param.17) | copy-start | bytes 196612
  50.3 10.1 %copy-start.9 = (f32[32,4,128]{2,1,0:T(4,128)S(1)}, f32[32,4,128]{2,1,0:T(4,128)}, u32[]{:S(2)}) copy-start(f32[32,4,128]{2,1,0:T(4,128)} %param.16) | copy-start | bytes 196612
  50.4 10.7 %collective-permute-start.3 = (f32[66,32,6,1]{0,1,3,2:T(8,128)S(1)}, f32[66,32,6,1]{0,1,3,2:T(8,128)S(1)}, u32[]{:S(2)}, u32[]{:S(2)}) collective-permute-start(f32[66,32,6,1]{0,1,3,2:T(8,128)S(1)} %copy.22), channel_id=1, source_target_pairs={{2,0},{4,2},{6,4},{0,6},{3,1},{5,3},{7,5},{1,7},{10,8},{12,10},{14... | collective-permute-start | bytes 152072 | tf_op jit(solution)/shard_map/ppermute | solution.py:16
  59.6 8.0 %collective-permute-start.2 = (f32[66,32,6,1]{0,1,3,2:T(8,128)S(1)}, f32[66,32,6,1]{0,1,3,2:T(8,128)}, u32[]{:S(2)}, u32[]{:S(2)}) collective-permute-start(f32[66,32,6,1]{0,1,3,2:T(8,128)S(1)} %copy.21), channel_id=1, source_target_pairs={{0,2},{2,4},{4,6},{6,0},{1,3},{3,5},{5,7},{7,1},{8,10},{10,12},{12... | collective-permute-start | bytes 152072 | tf_op jit(solution)/shard_map/ppermute | solution.py:14
  67.6 9.0 %slice-start = ((s8[6488064]{0:T(1024)(128)(4,1)}), s8[2293760]{0:T(1024)(128)(4,1)S(1)}, s32[]{:S(2)}) async-start(s8[6488064]{0:T(1024)(128)(4,1)} %bitcast.75), calls=%async_computation.2 | async-start | bytes 4587520
  75.0 2.4 copy-start.1
  75.0 3.7 %slice-start.1 = ((s8[6488064]{0:T(1024)(128)(4,1)}), s8[4194304]{0:T(1024)(128)(4,1)S(1)}, s32[]{:S(2)}) async-start(s8[6488064]{0:T(1024)(128)(4,1)} %bitcast.75), calls=%async_computation.3 | async-start | bytes 8388608
  75.0 5.5 %copy-start.2 = (f32[66,32,6,1]{3,1,2,0:T(8,128)S(1)}, f32[66,32,6,1]{3,1,2,0:T(8,128)}, u32[]{:S(2)}) copy-start(f32[66,32,6,1]{3,1,2,0:T(8,128)} %copy.23) | copy-start | bytes 152068
  75.0 5.7 %copy-start.4 = (f32[66,32,1,128]{3,1,2,0:T(8,128)S(1)}, f32[66,32,1,128]{3,1,2,0:T(8,128)}, u32[]{:S(2)}) copy-start(f32[66,32,1,128]{3,1,2,0:T(8,128)} %copy-done.3) | copy-start | bytes 3244036
  91.0 2.2 copy-start.5
  93.2 2.1 copy-start.6
  93.2 2.1 copy-start.7
  98.5 6.3 %copy-start.12 = (s32[48,8]{0,1:T(8,128)S(1)}, s32[48,8]{0,1:T(8,128)}, u32[]{:S(2)}) copy-start(s32[48,8]{0,1:T(8,128)} %param.22) | copy-start | bytes 4612
  98.5 6.4 %copy-start.13 = (s32[48,8]{0,1:T(8,128)S(1)}, s32[48,8]{0,1:T(8,128)}, u32[]{:S(2)}) copy-start(s32[48,8]{0,1:T(8,128)} %param.23) | copy-start | bytes 4612
  98.5 6.5 %copy-start.14 = (f32[48,8]{0,1:T(8,128)S(1)}, f32[48,8]{0,1:T(8,128)}, u32[]{:S(2)}) copy-start(f32[48,8]{0,1:T(8,128)} %param.21) | copy-start | bytes 4612
  98.5 6.6 %copy-start.17 = (f32[64]{0:T(128)S(1)}, f32[64]{0:T(128)}, u32[]{:S(2)}) copy-start(f32[64]{0:T(128)} %param.18) | copy-start | bytes 772
  98.5 53.8 %all-to-all-start = ((f32[66,32,4,128]{3,1,0,2:T(8,128)}), f32[66,32,4,128]{3,1,0,2:T(8,128)}, u32[]{:S(2)}, u32[]{:S(2)}) async-start(f32[66,32,4,128]{3,1,0,2:T(8,128)} %copy.30), calls=%async_computation | async-start | bytes 8650752 | tf_op jit(solution)/shard_map/all_to_all | solution.py:118
  155.7 4.7 %copy-start.15 = (f32[16]{0:T(128)S(1)}, f32[16]{0:T(128)}, u32[]{:S(2)}) copy-start(f32[16]{0:T(128)} %param.20) | copy-start | bytes 196
  160.4 2.1 copy-start.16
where the time goes:
time: 330 us; the launch traced here: 327 us
  local copies, waits for them, and re-layouts  101 us (31%)
  waiting for transfers between devices  72.9 us (22%)
  matrix products  56.8 us (17%)
  blocking collectives  49.2 us (15%)
  other arithmetic  35.7 us (11%)
  starting transfers between devices  10.7 us (3%)
    all_to_all x1, blocking collectives, shards(): lax.all_to_all(finished, 'gz', split_axis=1, concat_axis=2, tiled=True)  49.2 us
    all_to_all x1, waiting for transfers between devices, shards(): lax.all_to_all(bundle, 'gz', split_axis=2, concat_axis=1, tiled=True)  47.2 us
    dot_general x8, matrix products, one_block(): gain = jnp.dot(route, rate, precision=lax.Precision.HIGHEST)  30.4 us
    ppermute x2, waiting for transfers between devices, padded_2(): lax.ppermute(head, axis, [((i + 1) % count, i) for i in range(count)])  22.9 us
    dot_general x8, matrix products, one_block(): picked = jnp.dot(select, flat, precision=lax.Precision.HIGHEST)  21.7 us
    slice x2, local copies, waits for them, and re-layouts, padded_2(): lax.slice_in_dim(cells, cells.shape[dim] - width, cells.shape[dim], axis=...  16.9 us
    unnamed x43, local copies, waits for them, and re-layouts  15.3 us
    reshape x8, local copies, waits for them, and re-layouts, one_block(): fresh.reshape(piece.shape)  10.6 us
  transfers between devices with their start and end apart: 5, of which 3 were waited for; matrix products, arithmetic and copies ran while one was open for 4% of the time, Pallas kernels for 0%

commit v1 on v0

v1 whole, which is shorter than its diff:
```python
import functools

import jax
import jax.numpy as jnp
from jax import lax
from jax.experimental import pallas as pl
from jax.experimental.pallas import tpu as pltpu
from jax.sharding import PartitionSpec as P

LANES = 128
SUB = 8
GROUP = 8


def roll_to(value, source, dest):
    shift = (dest - source) % LANES
    return value if shift == 0 else pltpu.roll(value, shift, 1)


def pack_y_kernel(nx, field_ref, cour_ref, right_ref, left_ref):
    bins, rows, _ = field_ref.shape
    per_bin = rows // SUB
    blocks = rows // (SUB * nx)
    lane = lax.broadcasted_iota(jnp.int32, (SUB, LANES), 1)

    def one(load, offset, packed):
        for x in range(nx):
            for q in range(blocks):
                at = offset + x * blocks + q
                value = load(pl.ds(q * SUB * nx + x, SUB, stride=nx))
                hit = lane == at
                packed = (
                    jnp.where(hit, roll_to(value, LANES - 1, at), packed[0]),
                    jnp.where(hit, roll_to(value, 0, at), packed[1]),
                )
        return packed

    zero = jnp.zeros((SUB, LANES), jnp.float32)

    def group(g, _):
        packed = (zero, zero)
        for k in range(GROUP):
            packed = one(lambda r: field_ref[g * GROUP + k, r, :], k * per_bin, packed)
        right_ref[g] = packed[0]
        left_ref[g] = packed[1]
        return 0

    lax.fori_loop(0, bins // GROUP, group, 0)
    right_ref[bins // GROUP] = one(lambda r: cour_ref[r, :], 0, (zero, zero))[0]


def advect_settle_kernel(nx, xs, halos, *refs):
    if halos:
        scal, field, cx, cy, yl, yr, table, xl, xr, out, bottom = refs
    else:
        scal, field, cx, cy, yl, yr, table, out, bottom = refs
        xl = xr = None
    bins, rows, _ = field.shape
    blocks = rows // (SUB * nx)
    per_bin = nx * blocks
    lane = lax.broadcasted_iota(jnp.int32, (SUB, LANES), 1)
    first, last = lane == 0, lane == LANES - 1
    for xi, x in enumerate(xs):
        for q in reversed(range(blocks)):
            span = lambda xx: pl.ds(q * SUB * nx + xx, SUB, stride=nx)
            spot = x * blocks + q
            zrows = pl.ds(q * SUB, SUB)
            c_here = cx[span(x), :]
            c_left = cx[span(x - 1), :] if x > 0 else xl[bins, zrows, :]
            y_here = cy[span(x), :]
            y_left = jnp.where(
                first, roll_to(yl[bins // GROUP], spot, 0), pltpu.roll(y_here, 1, 1)
            )
            stay = (
                1.0
                - jnp.maximum(c_here, 0.0)
                + jnp.minimum(c_left, 0.0)
                - jnp.maximum(y_here, 0.0)
                + jnp.minimum(y_left, 0.0)
            )
            from_right = -jnp.minimum(c_here, 0.0)
            from_left = jnp.maximum(c_left, 0.0)
            from_up = -jnp.minimum(y_here, 0.0)
            from_down = jnp.maximum(y_left, 0.0)

            def group(g, _):
                down_pack = yl[g]
                up_pack = yr[g]
                for k in range(GROUP):
                    b = g * GROUP + k
                    here = field[b, span(x), :]
                    left = field[b, span(x - 1), :] if x > 0 else xl[b, zrows, :]
                    right = field[b, span(x + 1), :] if x < nx - 1 else xr[b, zrows, :]
                    at = k * per_bin + spot
                    down = jnp.where(first, roll_to(down_pack, at, 0), pltpu.roll(here, 1, 1))
                    up = jnp.where(
                        last, roll_to(up_pack, at, LANES - 1), pltpu.roll(here, LANES - 1, 1)
                    )
                    moved = (
                        stay * here
                        + from_right * right
                        + from_left * left
                        + from_up * up
                        + from_down * down
                    )
                    fall = moved * scal[b]
                    fall = fall + table[b, 0] * pltpu.roll(fall, SUB - 1, 0)
                    fall = fall + table[b, 1] * pltpu.roll(fall, SUB - 2, 0)
                    fall = fall + table[b, 2] * pltpu.roll(fall, SUB - 4, 0)
                    if q < blocks - 1:
                        above = out[b, xi * blocks + q + 1, pl.ds(0, 1), :]
                        fall = fall + table[b, 3] * above
                    out[b, xi * blocks + q] = fall
                    if q == 0:
                        bottom[xi, pl.ds(b, 1), :] = fall[0:1, :]
                return 0

            lax.fori_loop(0, bins // GROUP, group, 0)


def micro_kernel(nx, xs, slots, merge, *refs):
    if merge:
        scal, index, settled, carry, table, sat_ref, mask_ref, inner, out, grown, change = refs
    else:
        scal, index, settled, carry, table, sat_ref, mask_ref, out, grown, change = refs
    bins = settled.shape[0]
    drops = grown.shape[0]
    aero = bins - drops
    cells = grown.shape[1]
    blocks = cells // len(xs)
    at_growth = bins + blocks * bins
    at_threshold = at_growth + drops
    at_rate = at_threshold + aero

    def spans(v):
        x, q = xs[v // blocks], v % blocks
        return pl.ds(q * SUB * nx + x, SUB, stride=nx)

    sat = [sat_ref[spans(v), :] for v in range(cells)]

    def full(b):
        values = []
        decay = table[b, 3]
        for v in range(cells):
            xi, q = v // blocks, v % blocks
            values.append(
                settled[b, v]
                + (decay * scal[bins + q * bins + b]) * carry[xi, pl.ds(b, 1), :]
            )
        return values

    def put(b, v, value):
        if merge:
            out[b, spans(v), :] = value
        else:
            out[b, v] = value

    zero = jnp.zeros((SUB, LANES), jnp.float32)

    def activate(j, gained):
        mass = full(drops + j)
        fresh = []
        for v in range(cells):
            active = jnp.maximum(sat[v] - scal[at_threshold + j], 0.0) * mass[v]
            put(drops + j, v, mass[v] - active)
            fresh.append(gained[v] + active)
        return tuple(fresh)

    gained = lax.fori_loop(0, aero, activate, (zero,) * cells)

    def condense(b, state):
        current, below = state
        after = full(b + 1)
        flux = []
        for v in range(cells):
            face = scal[at_growth + b] * sat[v]
            flux.append(jnp.maximum(face, 0.0) * current[v] + jnp.minimum(face, 0.0) * after[v])
            grown[b, v] = current[v] + below[v] - flux[v]
            change[b, v] = zero
        return tuple(after), tuple(flux)

    current, below = lax.fori_loop(
        0, drops - 1, condense, (tuple(full(0)), (zero,) * cells)
    )
    for v in range(cells):
        grown[drops - 1, v] = current[v] + below[v]
        change[drops - 1, v] = zero
        grown[0, v] = grown[0, v] + gained[v]

    def collide(i, _):
        mine = grown[i]
        loss = jnp.zeros_like(mine)
        for m in range(slots):
            pair = i * slots + m
            rate = (mine * scal[at_rate + pair]) * grown[index[pair]]
            loss = loss + rate
            goal = index[drops * slots + pair]
            change[goal] = change[goal] + rate
        change[i] = change[i] - loss
        return 0

    lax.fori_loop(0, drops, collide, 0)

    mask = [mask_ref[spans(v), :].astype(jnp.float32) for v in range(cells)]

    def finish(b, _):
        for v in range(cells):
            put(b, v, grown[b, v] + mask[v] * change[b, v])
        return 0

    lax.fori_loop(0, drops, finish, 0)

    if merge:
        others = [x for x in range(nx) if x not in xs]

        def fill(b, _):
            for xi, x in enumerate(others):
                for q in range(blocks):
                    out[b, pl.ds(q * SUB * nx + x, SUB, stride=nx), :] = inner[b, xi * blocks + q]
            return 0

        lax.fori_loop(0, bins, fill, 0)


VMEM = pl.BlockSpec(memory_space=pltpu.VMEM)
SMEM = pl.BlockSpec(memory_space=pltpu.SMEM)
PARAMS = pltpu.CompilerParams(vmem_limit_bytes=48 * 1024 * 1024)


def cost(flops, bytes_accessed):
    return pl.CostEstimate(flops=flops, bytes_accessed=bytes_accessed, transcendentals=0)


def shift_up(value, axis):
    count = lax.axis_size(axis)
    return lax.ppermute(value, axis, [(i, (i + 1) % count) for i in range(count)])


def shift_down(value, axis):
    count = lax.axis_size(axis)
    return lax.ppermute(value, axis, [((i + 1) % count, i) for i in range(count)])


def shards(
    field,
    courant_x,
    courant_y,
    supersat,
    cloud_mask,
    fall_speed,
    growth,
    activation_threshold,
    kernel_rate,
    partner,
    target,
):
    bins, depth, nx, ny = field.shape
    drops, slots = partner.shape
    f32 = jnp.float32
    blocks = depth // SUB
    flat = field.reshape(bins, depth * nx, ny)
    cx, cy, sat, mask = (
        a.reshape(depth * nx, ny) for a in (courant_x, courant_y, supersat, cloud_mask)
    )

    to_right = jnp.concatenate([field[:, :, nx - 1, :], courant_x[None, :, nx - 1, :]], 0)
    to_left = field[:, :, 0, :]
    x_left = shift_up(to_right, "gx")
    x_right = shift_down(to_left, "gx")

    groups = bins // GROUP
    y_to_right, y_to_left = pl.pallas_call(
        functools.partial(pack_y_kernel, nx),
        out_shape=(
            jax.ShapeDtypeStruct((groups + 1, SUB, LANES), f32),
            jax.ShapeDtypeStruct((groups, SUB, LANES), f32),
        ),
        in_specs=[VMEM, VMEM],
        out_specs=(VMEM, VMEM),
        compiler_params=PARAMS,
        cost_estimate=cost(1 << 22, 1 << 22),
        name="pack_y",
    )(flat, cy)
    y_left = shift_up(y_to_right, "gy")
    y_right = shift_down(y_to_left, "gy")

    ratio = fall_speed / (1.0 + fall_speed)
    log_ratio = jnp.log(ratio)
    sub = jnp.arange(SUB, dtype=f32)
    power = jnp.stack([jnp.full((SUB,), 1.0, f32), jnp.full((SUB,), 2.0, f32), jnp.full((SUB,), 4.0, f32), SUB - sub])
    keep = jnp.stack([sub < SUB - 1, sub < SUB - 2, sub < SUB - 4, sub < SUB])
    table = jnp.where(keep, jnp.exp(log_ratio[:, None, None] * power), 0.0)
    table = jnp.broadcast_to(table[..., None], (bins, 4, SUB, LANES))
    step = jnp.exp(log_ratio[None, :] * (SUB * jnp.arange(blocks - 1, -1, -1, dtype=f32))[:, None])
    scal = jnp.concatenate(
        [
            1.0 / (1.0 + fall_speed),
            step.reshape(-1),
            growth,
            jnp.zeros((1,), f32),
            activation_threshold,
            kernel_rate.reshape(-1),
        ]
    )
    index = jnp.concatenate([partner.reshape(-1), target.reshape(-1)])

    inner_x = tuple(range(1, nx - 1))
    edge_x = (0, nx - 1)

    def settle_part(xs, halos):
        cells = len(xs) * blocks
        args = [scal, flat, cx, cy, y_left, y_right, table] + list(halos)
        return pl.pallas_call(
            functools.partial(advect_settle_kernel, nx, xs, bool(halos)),
            out_shape=(
                jax.ShapeDtypeStruct((bins, cells, SUB, LANES), f32),
                jax.ShapeDtypeStruct((len(xs), bins, LANES), f32),
            ),
            in_specs=[SMEM] + [VMEM] * (len(args) - 1),
            out_specs=(VMEM, VMEM),
            compiler_params=PARAMS,
            cost_estimate=cost(1 << 24, 8 << 20),
            name="settle_edge" if halos else "settle_inner",
        )(*args)

    count = lax.axis_size("gz")
    whole = jnp.exp(log_ratio * depth)[None, :, None]

    def inflow(bottom):
        carry = jnp.zeros_like(bottom)
        for hop in range(count - 1):
            sent = bottom if hop == 0 else bottom + whole * carry
            carry = lax.ppermute(sent, "gz", [(i + 1, i) for i in range(count - 1)])
        return carry

    def micro_part(xs, settled, carry, inner):
        cells = len(xs) * blocks
        args = [scal, index, settled, carry, table, sat, mask] + list(inner)
        if inner:
            out = jax.ShapeDtypeStruct((bins, depth * nx, ny), f32)
        else:
            out = jax.ShapeDtypeStruct((bins, cells, SUB, LANES), f32)
        return pl.pallas_call(
            functools.partial(micro_kernel, nx, xs, slots, bool(inner)),
            out_shape=out,
            in_specs=[SMEM, SMEM] + [VMEM] * (len(args) - 2),
            out_specs=VMEM,
            scratch_shapes=[
                pltpu.VMEM((drops, cells, SUB, LANES), f32),
                pltpu.VMEM((drops, cells, SUB, LANES), f32),
            ],
            compiler_params=PARAMS,
            cost_estimate=cost(1 << 24, 8 << 20),
            name="micro_edge" if inner else "micro_inner",
        )(*args)

    settled, bottom = settle_part(inner_x, ())
    inner = micro_part(inner_x, settled, inflow(bottom), ())
    settled, bottom = settle_part(edge_x, (x_left, x_right))
    out = micro_part(edge_x, settled, inflow(bottom), (inner,))
    return out.reshape(field.shape)


def solution(mesh):
    cells = P("gz", "gx", "gy")
    return jax.shard_map(
        shards,
        mesh=mesh,
        in_specs=(P(None, "gz", "gx", "gy"), cells, cells, cells, cells) + (P(),) * 6,
        out_specs=P(None, "gz", "gx", "gy"),
        check_vma=False,
    )
```

time: 330 us -> 63.6 us (0.19)
  local copies, waits for them, and re-layouts: 101 us -> 7.6 us
  waiting for transfers between devices: 72.9 us -> 9.24 us
  matrix products: 56.8 us -> 0 us
  blocking collectives: 49.2 us -> 0 us
  Pallas kernels: 0 us -> 35.1 us
  other arithmetic: 35.7 us -> 1.14 us
    dot_general x17 -> x0, matrix products: 56.8 us -> none  [the longest x8 30.4 us: one_block(): gain = jnp.dot(route, rate, precision=lax.Precision.HIGHEST)]
    all_to_all x1 -> x0, blocking collectives: 49.2 us -> none  [shards(): lax.all_to_all(finished, 'gz', split_axis=1, concat_axis=2, tiled=True)]
    all_to_all x1 -> x0, waiting for transfers between devices: 47.2 us -> none  [shards(): lax.all_to_all(bundle, 'gz', split_axis=2, concat_axis=1, tiled=True)]
    pallas_call x0 -> x5, Pallas kernels: none -> 35.1 us  [the longest x2 20 us: settle_part(): pl.pallas_call(functools.partial(advect_settle_kernel, nx, xs, bool(halos...]
    slice x7 -> x2, local copies, waits for them, and re-layouts: 24 us -> 2.61 us  [the longest x1 2.59 us: shards(): to_left = field[:, :, 0, :]]
    ppermute x4 -> x6, waiting for transfers between devices: 25.7 us -> 9.24 us  [the longest x2 6.48 us: shift_down(): lax.ppermute(value, axis, [((i + 1) % count, i) for i in range(count)])]
    dynamic_slice x24 -> x0, local copies, waits for them, and re-layouts: 15.4 us -> none  [the longest x16 9.8 us: one_block(): piece = lax.dynamic_slice_in_dim(grown, start, block, 1)]
    ppermute x2 -> x0, local copies, waits for them, and re-layouts: 13.9 us -> none  [the longest x1 7.45 us: padded_2(): lax.ppermute(tail, axis, [(i, (i + 1) % count) for i in range(count)])]
  transfers between devices with their start and end apart: 5 -> 6, of which waited for: 3 -> 3; matrix products, arithmetic and copies ran while one was open for 4% -> 9% of each run, Pallas kernels for 0% -> 40%
where the time goes in v1:
time: 63.6 us; the launch traced here: 62.6 us
  Pallas kernels  35.1 us (55%)
  starting transfers between devices  9.27 us (15%)
  waiting for transfers between devices  9.24 us (15%)
  local copies, waits for them, and re-layouts  7.6 us (12%)
  other arithmetic  1.14 us (2%)
    pallas_call x2, Pallas kernels, settle_part(): pl.pallas_call(functools.partial(advect_settle_kernel, nx, xs, bool(halos...  20 us
    pallas_call x2, Pallas kernels, micro_part(): pl.pallas_call(functools.partial(micro_kernel, nx, xs, slots, bool(inner)...  12.4 us
    ppermute x2, waiting for transfers between devices, shift_down(): lax.ppermute(value, axis, [((i + 1) % count, i) for i in range(count)])  6.48 us
    ppermute x2, starting transfers between devices, inflow(): carry = lax.ppermute(sent, 'gz', [(i + 1, i) for i in range(count - 1)])  5.02 us
    ppermute x2, starting transfers between devices, shift_down(): lax.ppermute(value, axis, [((i + 1) % count, i) for i in range(count)])  3.71 us
    unnamed x28, local copies, waits for them, and re-layouts  3.32 us
    pallas_call x1, Pallas kernels, shards(): pl.pallas_call(functools.partial(pack_y_kernel, nx), out_shape=(jax.Shape...  2.76 us
    ppermute x2, waiting for transfers between devices, shift_up(): lax.ppermute(value, axis, [(i, (i + 1) % count) for i in range(count)])  2.75 us
  transfers between devices with their start and end apart: 6, of which 3 were waited for; matrix products, arithmetic and copies ran while one was open for 9% of the time, Pallas kernels for 40%

profile of v1, /device:TPU:6, one launch (start us, length us, event | category | flops | bytes accessed | tf_op | source)
XLA Modules:
  0.0 62.6 jit_solution(12531196834136868418)
XLA Ops:
  0.0 0.0 copy-start
  0.0 2.2 %copy-done = f32[64,32,4,128]{3,2,1,0:T(4,128)S(1)} copy-done((f32[64,32,4,128]{3,2,1,0:T(4,128)S(1)}, f32[64,32,4,128]{3,2,1,0:T(4,128)}, u32[]{:S(2)}) %copy-start) | copy-done | bytes 4194328
  2.2 0.0 copy-start.1
  2.2 0.8 %copy-done.1 = f32[32,4,128]{2,1,0:T(4,128)S(1)} copy-done((f32[32,4,128]{2,1,0:T(4,128)S(1)}, f32[32,4,128]{2,1,0:T(4,128)}, u32[]{:S(2)}) %copy-start.1) | copy-done | bytes 65560
  3.0 2.8 %pack_y.1 = (f32[9,8,128]{2,1,0:T(8,128)S(1)}, f32[8,8,128]{2,1,0:T(8,128)S(1)}) custom-call(f32[64,128,128]{2,1,0:T(8,128)S(1)} %bitcast.19, f32[128,128]{1,0:T(8,128)S(1)} %bitcast.20), custom_call_target="tpu_custom_call" | custom-call | flops 4194304 | bytes 4194304 | tf_op jit(solution)/shard_map/pack_y/pallas_call | solution.py:272
  5.8 3.7 %collective-permute-start.1 = (f32[8,8,128]{2,1,0:T(8,128)S(1)}, f32[8,8,128]{2,1,0:T(8,128)S(1)}, u32[]{:S(2)}, u32[]{:S(2)}) collective-permute-start(f32[8,8,128]{2,1,0:T(8,128)S(1)} %get-tuple-element.12), channel_id=1, source_target_pairs={{2,0},{4,2},{6,4},{0,6},{3,1},{5,3},{7,5},{1,7},{10,8},{12,10},{14... | collective-permute-start | bytes 98312 | tf_op jit(solution)/shard_map/ppermute | solution.py:241
  9.5 0.0 copy-start.3
  9.5 0.0 collective-permute-start
  9.5 2.6 %fusion.1 = (f32[64,32,1,128]{3,2,1,0:T(1,128)}, f32[64,32,1,128]{3,2,1,0:T(1,128)S(1)}) fusion(f32[64,32,4,128]{3,2,1,0:T(4,128)S(1)} %copy-done), kind=kLoop, calls=%fused_computation.17 | loop fusion | bytes 4194304 | tf_op jit(solution)/shard_map/slice | solution.py:267
  12.0 0.0 copy-start.6
  12.0 0.0 copy-start.11
  12.1 0.0 copy-start.7
  12.1 0.0 copy-start.8
  12.1 0.0 copy-start.9
  12.1 0.0 copy-start.10
  12.1 0.0 copy-start.2
  12.1 0.1 collective-permute-start.3
  12.2 0.0 copy-done.3
  12.2 0.1 pad_maximum_fusion
  12.3 0.5 collective-permute-start.2
  12.9 0.1 pad_maximum_fusion.2
  13.0 0.0 copy-done.6
  13.0 0.1 copy.16
  13.0 0.1 reshape.80
  13.1 0.0 copy-done.11
  13.2 0.1 pad_maximum_fusion.1
  13.2 0.1 multiply_exponential_fusion
  13.3 0.8 %exponential_select_fusion = f32[64,4,8]{2,1,0:T(4,128)} fusion(f32[4,8]{1,0:T(4,128)S(1)} %pad_maximum_fusion.1, f32[64]{0:T(128)S(1)} %get-tuple-element.19, pred[4,8]{1,0:T(4,128)(4,1)S(1)} %pad_add_fusion), kind=kLoop, calls=%fused_computation.1 | loop fusion | flops 4096 | bytes 8608 | tf_op jit(solution)/shard_map/jit(_where)/select_n | solution.py:292
  14.1 0.1 exp.15
  14.2 0.0 copy-done.7
  14.2 0.1 copy.15
  14.3 0.1 reshape.79
  14.4 0.0 copy-done.8
  14.4 0.1 copy.17
  14.5 0.1 reshape.81
  14.5 0.0 copy-done.9
  14.6 0.0 copy-done.10
  14.6 0.1 concatenate.9.refs_0_
  14.7 0.0 collective-permute-done.1.refs_5_
  14.7 0.6 collective-permute-done.refs_4_
  15.2 1.2 %broadcast_in_dim.20.refs_6_.refs_4_ = f32[64,4,8,128]{3,2,1,0:T(8,128)S(1)} broadcast(f32[64,4,8]{2,1,0:T(4,128)} %exponential_select_fusion), dimensions={0,1,2} | broadcast | bytes 1056768 | tf_op jit(solution)/shard_map/broadcast_in_dim | solution.py:293
  16.4 0.0 copy-done.2
  16.5 10.0 %settle_inner.1 = (f32[64,8,8,128]{3,2,1,0:T(8,128)S(1)}, f32[2,64,128]{2,1,0:T(8,128)S(1)}) custom-call(f32[768]{0:T(1024)S(1)} %concatenate.9.refs_0_, f32[64,128,128]{2,1,0:T(8,128)} %bitcast.17, f32[128,128]{1,0:T(8,128)S(1)} %bitcast.23, f32[128,128]{1,0:T(8,128)S(1)} %bitcast.21, f32[9,8,128]{2,1,0:T(8,128)S(1)} %collective-permute-done.refs_4_, ...), custom_call_target="tpu_custom_call" | custom-call | flops 16777216 | bytes 8388608 | tf_op jit(solution)/shard_map/settle_inner/pallas_call | solution.py:313
  26.4 0.0 copy-start.4
  26.5 0.0 copy-start.5
  26.5 2.6 %collective-permute-start.5 = (f32[2,64,128]{2,1,0:T(8,128)S(1)}, f32[2,64,128]{2,1,0:T(8,128)S(1)}, u32[]{:S(2)}, u32[]{:S(2)}) collective-permute-start(f32[2,64,128]{2,1,0:T(8,128)S(1)} %get-tuple-element.16), channel_id=1, source_target_pairs={{1,0},{3,2},{5,4},{7,6},{9,8},{11,10},{13,12},{15,14},{17,16},{19,... | collective-permute-start | bytes 196616 | tf_op jit(solution)/shard_map/ppermute | solution.py:333
  29.1 6.5 %collective-permute-done.3.refs_8_ = f32[64,32,128]{2,1,0:T(8,128)S(1)} collective-permute-done((f32[64,32,128]{2,1,0:T(8,128)}, f32[64,32,128]{2,1,0:T(8,128)S(1)}, u32[]{:S(2)}, u32[]{:S(2)}) %collective-permute-start.3) | collective-permute-done | bytes 1048608 | tf_op jit(solution)/shard_map/ppermute | solution.py:241
  35.5 2.2 %collective-permute-done.2.refs_7_ = f32[65,32,128]{2,1,0:T(8,128)S(1)} collective-permute-done((f32[65,32,128]{2,1,0:T(8,128)S(1)}, f32[65,32,128]{2,1,0:T(8,128)S(1)}, u32[]{:S(2)}, u32[]{:S(2)}) %collective-permute-start.2) | collective-permute-done | bytes 1064992 | tf_op jit(solution)/shard_map/ppermute | solution.py:236
  37.7 10.0 %settle_edge.1 = (f32[64,8,8,128]{3,2,1,0:T(8,128)S(1)}, f32[2,64,128]{2,1,0:T(8,128)S(1)}) custom-call(f32[768]{0:T(1024)S(1)} %concatenate.9.refs_0_, f32[64,128,128]{2,1,0:T(8,128)} %bitcast.18, f32[128,128]{1,0:T(8,128)S(1)} %bitcast.24, f32[128,128]{1,0:T(8,128)S(1)} %bitcast.22, f32[9,8,128]{2,1,0:T(8,128)S(1)} %collective-permute-done.refs_4_, ...), custom_call_target="tpu_custom_call" | custom-call | flops 16777216 | bytes 8388608 | tf_op jit(solution)/shard_map/settle_edge/pallas_call | solution.py:313
  47.7 2.4 %collective-permute-start.4 = (f32[2,64,128]{2,1,0:T(8,128)S(1)}, f32[2,64,128]{2,1,0:T(8,128)S(1)}, u32[]{:S(2)}, u32[]{:S(2)}) collective-permute-start(f32[2,64,128]{2,1,0:T(8,128)S(1)} %get-tuple-element.14), channel_id=1, source_target_pairs={{1,0},{3,2},{5,4},{7,6},{9,8},{11,10},{13,12},{15,14},{17,16},{19,... | collective-permute-start | bytes 196616 | tf_op jit(solution)/shard_map/ppermute | solution.py:333
  50.2 0.0 collective-permute-done.5.refs_3_
  50.2 0.0 copy-done.4
  50.2 0.0 copy-done.5
  50.2 4.9 %micro_inner.1.refs_7_ = f32[64,8,8,128]{3,2,1,0:T(8,128)S(1)} custom-call(f32[768]{0:T(1024)S(1)} %concatenate.9.refs_0_, s32[768]{0:T(1024)S(1)} %constant_dynamic-update-slice_fusion.refs_1_, f32[64,8,8,128]{3,2,1,0:T(8,128)S(1)} %get-tuple-element.15.refs_2_, f32[2,64,128]{2,1,0:T(8,128)S(1)} %collective-permute-done.5.refs_3_, ...), custom_call_target="tpu_custom_call" | custom-call | flops 16777216 | bytes 8388608 | tf_op jit(solution)/shard_map/micro_inner/pallas_call | solution.py:343
  55.2 0.0 collective-permute-done.4.refs_3_
  55.2 7.5 %micro_edge.1 = f32[64,128,128]{2,1,0:T(8,128)} custom-call(f32[768]{0:T(1024)S(1)} %concatenate.9.refs_0_, s32[768]{0:T(1024)S(1)} %constant_dynamic-update-slice_fusion.refs_1_, f32[64,8,8,128]{3,2,1,0:T(8,128)S(1)} %get-tuple-element.13.refs_2_, f32[2,64,128]{2,1,0:T(8,128)S(1)} %collective-permute-done.4.refs_3_, ...), custom_call_target="tpu_custom_call" | custom-call | flops 16777216 | bytes 8388608 | tf_op jit(solution)/shard_map/micro_edge/pallas_call | solution.py:343
  (11 shorter events, 0.1 us)
Async XLA Ops:
  0.0 2.2 %copy-start = (f32[64,32,4,128]{3,2,1,0:T(4,128)S(1)}, f32[64,32,4,128]{3,2,1,0:T(4,128)}, u32[]{:S(2)}) copy-start(f32[64,32,4,128]{3,2,1,0:T(4,128)} %param.11) | copy-start | bytes 12582916
  2.2 0.8 %copy-start.1 = (f32[32,4,128]{2,1,0:T(4,128)S(1)}, f32[32,4,128]{2,1,0:T(4,128)}, u32[]{:S(2)}) copy-start(f32[32,4,128]{2,1,0:T(4,128)} %param.13) | copy-start | bytes 196612
  5.8 8.9 %collective-permute-start.1 = (f32[8,8,128]{2,1,0:T(8,128)S(1)}, f32[8,8,128]{2,1,0:T(8,128)S(1)}, u32[]{:S(2)}, u32[]{:S(2)}) collective-permute-start(f32[8,8,128]{2,1,0:T(8,128)S(1)} %get-tuple-element.12), channel_id=1, source_target_pairs={{2,0},{4,2},{6,4},{0,6},{3,1},{5,3},{7,5},{1,7},{10,8},{12,10},{14... | collective-permute-start | bytes 98312 | tf_op jit(solution)/shard_map/ppermute | solution.py:241
  9.5 2.7 %copy-start.3 = (f32[32,4,128]{2,1,0:T(4,128)S(1)}, f32[32,4,128]{2,1,0:T(4,128)}, u32[]{:S(2)}) copy-start(f32[32,4,128]{2,1,0:T(4,128)} %param.12) | copy-start | bytes 196612
  9.5 5.8 %collective-permute-start = (f32[9,8,128]{2,1,0:T(8,128)S(1)}, f32[9,8,128]{2,1,0:T(8,128)S(1)}, u32[]{:S(2)}, u32[]{:S(2)}) collective-permute-start(f32[9,8,128]{2,1,0:T(8,128)S(1)} %get-tuple-element.11), channel_id=1, source_target_pairs={{0,2},{2,4},{4,6},{6,0},{1,3},{3,5},{5,7},{7,1},{8,10},{10,12},{12... | collective-permute-start | bytes 110600 | tf_op jit(solution)/shard_map/ppermute | solution.py:236
  12.0 0.9 %copy-start.6 = (s32[48,8]{0,1:T(8,128)S(1)}, s32[48,8]{0,1:T(8,128)}, u32[]{:S(2)}) copy-start(s32[48,8]{0,1:T(8,128)} %param.20) | copy-start | bytes 4612
  12.0 1.1 %copy-start.11 = (f32[64]{0:T(128)S(1)}, f32[64]{0:T(128)}, u32[]{:S(2)}) copy-start(f32[64]{0:T(128)} %param.16) | copy-start | bytes 772
  12.1 2.1 %copy-start.7 = (f32[48,8]{0,1:T(8,128)S(1)}, f32[48,8]{0,1:T(8,128)}, u32[]{:S(2)}) copy-start(f32[48,8]{0,1:T(8,128)} %param.19) | copy-start | bytes 4612
  12.1 2.3 %copy-start.8 = (s32[48,8]{0,1:T(8,128)S(1)}, s32[48,8]{0,1:T(8,128)}, u32[]{:S(2)}) copy-start(s32[48,8]{0,1:T(8,128)} %param.21) | copy-start | bytes 4612
  12.1 2.5 %copy-start.9 = (f32[47]{0:T(128)S(1)}, f32[47]{0:T(128)}, u32[]{:S(2)}) copy-start(f32[47]{0:T(128)} %param.17) | copy-start | bytes 568
  12.1 2.5 %copy-start.10 = (f32[16]{0:T(128)S(1)}, f32[16]{0:T(128)}, u32[]{:S(2)}) copy-start(f32[16]{0:T(128)} %param.18) | copy-start | bytes 196
  12.1 4.4 %copy-start.2 = (f32[32,4,128]{2,1,0:T(4,128)S(1)}, f32[32,4,128]{2,1,0:T(4,128)}, u32[]{:S(2)}) copy-start(f32[32,4,128]{2,1,0:T(4,128)} %param.13) | copy-start | bytes 196612
  12.1 23.4 %collective-permute-start.3 = (f32[64,32,128]{2,1,0:T(8,128)}, f32[64,32,128]{2,1,0:T(8,128)S(1)}, u32[]{:S(2)}, u32[]{:S(2)}) collective-permute-start(f32[64,32,128]{2,1,0:T(8,128)} %bitcast.5), channel_id=1, source_target_pairs={{8,0},{16,8},{24,16},{0,24},{9,1},{17,9},{25,17},{1,25},{10,2},{18... | collective-permute-start | bytes 3145736 | tf_op jit(solution)/shard_map/ppermute | solution.py:241
  12.3 25.4 %collective-permute-start.2 = (f32[65,32,128]{2,1,0:T(8,128)S(1)}, f32[65,32,128]{2,1,0:T(8,128)S(1)}, u32[]{:S(2)}, u32[]{:S(2)}) collective-permute-start(f32[65,32,128]{2,1,0:T(8,128)S(1)} %pad_maximum_fusion), channel_id=1, source_target_pairs={{0,8},{8,16},{16,24},{24,0},{1,9},{9,17},{17,25},{25,1},{2,10},{10... | collective-permute-start | bytes 3194888 | tf_op jit(solution)/shard_map/ppermute | solution.py:236
  26.4 23.8 %copy-start.4 = (f32[32,4,128]{2,1,0:T(4,128)S(1)}, f32[32,4,128]{2,1,0:T(4,128)}, u32[]{:S(2)}) copy-start(f32[32,4,128]{2,1,0:T(4,128)} %param.14) | copy-start | bytes 196612
  26.5 23.8 %copy-start.5 = (s32[32,4,128]{2,1,0:T(4,128)S(1)}, s32[32,4,128]{2,1,0:T(4,128)}, u32[]{:S(2)}) copy-start(s32[32,4,128]{2,1,0:T(4,128)} %param.15) | copy-start | bytes 196612
  26.5 23.7 %collective-permute-start.5 = (f32[2,64,128]{2,1,0:T(8,128)S(1)}, f32[2,64,128]{2,1,0:T(8,128)S(1)}, u32[]{:S(2)}, u32[]{:S(2)}) collective-permute-start(f32[2,64,128]{2,1,0:T(8,128)S(1)} %get-tuple-element.16), channel_id=1, source_target_pairs={{1,0},{3,2},{5,4},{7,6},{9,8},{11,10},{13,12},{15,14},{17,16},{19,... | collective-permute-start | bytes 196616 | tf_op jit(solution)/shard_map/ppermute | solution.py:333
  47.7 7.4 %collective-permute-start.4 = (f32[2,64,128]{2,1,0:T(8,128)S(1)}, f32[2,64,128]{2,1,0:T(8,128)S(1)}, u32[]{:S(2)}, u32[]{:S(2)}) collective-permute-start(f32[2,64,128]{2,1,0:T(8,128)S(1)} %get-tuple-element.14), channel_id=1, source_target_pairs={{1,0},{3,2},{5,4},{7,6},{9,8},{11,10},{13,12},{15,14},{17,16},{19,... | collective-permute-start | bytes 196616 | tf_op jit(solution)/shard_map/ppermute | solution.py:333

commit v2 on v1

--- a/solution.py
+++ b/solution.py
@@ -17,8 +17,15 @@
     return value if shift == 0 else pltpu.roll(value, shift, 1)
 
 
+def pack_x_kernel(nx, field_ref, right_ref, left_ref):
+    rows = field_ref.shape[1]
+    for b in range(field_ref.shape[0]):
+        right_ref[b] = field_ref[b, pl.ds(nx - 1, rows // nx, stride=nx), :]
+        left_ref[b] = field_ref[b, pl.ds(0, rows // nx, stride=nx), :]
+
+
 def pack_y_kernel(nx, field_ref, cour_ref, right_ref, left_ref):
-    bins, rows, _ = field_ref.shape
+    _, rows, _ = field_ref.shape
     per_bin = rows // SUB
     blocks = rows // (SUB * nx)
     lane = lax.broadcasted_iota(jnp.int32, (SUB, LANES), 1)
@@ -36,25 +43,28 @@
         return packed
 
     zero = jnp.zeros((SUB, LANES), jnp.float32)
-
-    def group(g, _):
+    step = pl.program_id(0)
+    final = pl.num_programs(0) - 1
+
+    @pl.when(step < final)
+    def _():
         packed = (zero, zero)
         for k in range(GROUP):
-            packed = one(lambda r: field_ref[g * GROUP + k, r, :], k * per_bin, packed)
-        right_ref[g] = packed[0]
-        left_ref[g] = packed[1]
-        return 0
-
-    lax.fori_loop(0, bins // GROUP, group, 0)
-    right_ref[bins // GROUP] = one(lambda r: cour_ref[r, :], 0, (zero, zero))[0]
+            packed = one(lambda r: field_ref[k, r, :], k * per_bin, packed)
+        right_ref[0] = packed[0]
+        left_ref[0] = packed[1]
+
+    @pl.when(step == final)
+    def _():
+        right_ref[0] = one(lambda r: cour_ref[r, :], 0, (zero, zero))[0]
 
 
 def advect_settle_kernel(nx, xs, halos, *refs):
     if halos:
-        scal, field, cx, cy, yl, yr, table, xl, xr, out, bottom = refs
+        scal, field, cx, cy, yl, yr, table, cl, xl, xr, out, bottom = refs
     else:
         scal, field, cx, cy, yl, yr, table, out, bottom = refs
-        xl = xr = None
+        cl = xl = xr = None
     bins, rows, _ = field.shape
     blocks = rows // (SUB * nx)
     per_bin = nx * blocks
@@ -66,7 +76,7 @@
             spot = x * blocks + q
             zrows = pl.ds(q * SUB, SUB)
             c_here = cx[span(x), :]
-            c_left = cx[span(x - 1), :] if x > 0 else xl[bins, zrows, :]
+            c_left = cx[span(x - 1), :] if x > 0 else cl[zrows, :]
             y_here = cy[span(x), :]
             y_left = jnp.where(
                 first, roll_to(yl[bins // GROUP], spot, 0), pltpu.roll(y_here, 1, 1)
@@ -86,6 +96,7 @@
             def group(g, _):
                 down_pack = yl[g]
                 up_pack = yr[g]
+                moved, falls = [], []
                 for k in range(GROUP):
                     b = g * GROUP + k
                     here = field[b, span(x), :]
@@ -96,23 +107,28 @@
                     up = jnp.where(
                         last, roll_to(up_pack, at, LANES - 1), pltpu.roll(here, LANES - 1, 1)
                     )
-                    moved = (
+                    moved.append(
                         stay * here
                         + from_right * right
                         + from_left * left
                         + from_up * up
                         + from_down * down
                     )
-                    fall = moved * scal[b]
+                for k in range(GROUP):
+                    b = g * GROUP + k
+                    fall = moved[k] * scal[b]
                     fall = fall + table[b, 0] * pltpu.roll(fall, SUB - 1, 0)
                     fall = fall + table[b, 1] * pltpu.roll(fall, SUB - 2, 0)
                     fall = fall + table[b, 2] * pltpu.roll(fall, SUB - 4, 0)
                     if q < blocks - 1:
                         above = out[b, xi * blocks + q + 1, pl.ds(0, 1), :]
                         fall = fall + table[b, 3] * above
-                    out[b, xi * blocks + q] = fall
+                    falls.append(fall)
+                for k in range(GROUP):
+                    b = g * GROUP + k
+                    out[b, xi * blocks + q] = falls[k]
                     if q == 0:
-                        bottom[xi, pl.ds(b, 1), :] = fall[0:1, :]
+                        bottom[xi, pl.ds(b, 1), :] = falls[k][0:1, :]
                 return 0
 
             lax.fori_loop(0, bins // GROUP, group, 0)
@@ -263,24 +279,42 @@
         a.reshape(depth * nx, ny) for a in (courant_x, courant_y, supersat, cloud_mask)
     )
 
-    to_right = jnp.concatenate([field[:, :, nx - 1, :], courant_x[None, :, nx - 1, :]], 0)
-    to_left = field[:, :, 0, :]
+    groups = bins // GROUP
+    face = jax.ShapeDtypeStruct((bins, depth, ny), f32)
+    to_right, to_left = pl.pallas_call(
+        functools.partial(pack_x_kernel, nx),
+        grid=(groups,),
+        out_shape=(face, face),
+        in_specs=[pl.BlockSpec((GROUP, depth * nx, ny), lambda g: (g, 0, 0))],
+        out_specs=(pl.BlockSpec((GROUP, depth, ny), lambda g: (g, 0, 0)),) * 2,
+        compiler_params=PARAMS,
+        cost_estimate=cost(1 << 20, 6 << 20),
+        name="pack_x",
+    )(flat)
     x_left = shift_up(to_right, "gx")
     x_right = shift_down(to_left, "gx")
-
-    groups = bins // GROUP
+    cx_left = shift_up(courant_x[:, nx - 1, :], "gx")
+    flat_y, _, _ = lax.optimization_barrier((flat, to_right, to_left))
+
     y_to_right, y_to_left = pl.pallas_call(
         functools.partial(pack_y_kernel, nx),
+        grid=(groups + 1,),
         out_shape=(
             jax.ShapeDtypeStruct((groups + 1, SUB, LANES), f32),
             jax.ShapeDtypeStruct((groups, SUB, LANES), f32),
         ),
-        in_specs=[VMEM, VMEM],
-        out_specs=(VMEM, VMEM),
+        in_specs=[
+            pl.BlockSpec((GROUP, depth * nx, ny), lambda g: (jnp.minimum(g, groups - 1), 0, 0)),
+            pl.BlockSpec((depth * nx, ny), lambda g: (0, 0)),
+        ],
+        out_specs=(
+            pl.BlockSpec((1, SUB, LANES), lambda g: (g, 0, 0)),
+            pl.BlockSpec((1, SUB, LANES), lambda g: (jnp.minimum(g, groups - 1), 0, 0)),
+        ),
         compiler_params=PARAMS,
         cost_estimate=cost(1 << 22, 1 << 22),
         name="pack_y",
-    )(flat, cy)
+    )(flat_y, cy)
     y_left = shift_up(y_to_right, "gy")
     y_right = shift_down(y_to_left, "gy")
 
@@ -356,7 +390,8 @@
 
     settled, bottom = settle_part(inner_x, ())
     inner = micro_part(inner_x, settled, inflow(bottom), ())
-    settled, bottom = settle_part(edge_x, (x_left, x_right))
+    x_left, x_right, inner = lax.optimization_barrier((x_left, x_right, inner))
+    settled, bottom = settle_part(edge_x, (cx_left, x_left, x_right))
     out = micro_part(edge_x, settled, inflow(bottom), (inner,))
     return out.reshape(field.shape)
 

time: 63.6 us -> 70 us (1.10)
  the two profiles are of different devices: /device:TPU:6 before, /device:TPU:0 now
where the time goes in v2:
time: 70 us; the launch traced here: 69.7 us
  Pallas kernels  41.5 us (59%)
  waiting for transfers between devices  13.6 us (19%)
  starting transfers between devices  9.54 us (14%)
  local copies, waits for them, and re-layouts  3.67 us (5%)
  other arithmetic  1.07 us (2%)
    pallas_call x2, Pallas kernels, settle_part(): pl.pallas_call(functools.partial(advect_settle_kernel, nx, xs, bool(halos...  20 us
    pallas_call x2, Pallas kernels, micro_part(): pl.pallas_call(functools.partial(micro_kernel, nx, xs, slots, bool(inner)...  12.4 us
    ppermute x2, waiting for transfers between devices, inflow(): carry = lax.ppermute(sent, 'gz', [(i + 1, i) for i in range(count - 1)])  9.71 us
    pallas_call x1, Pallas kernels, shards(): pl.pallas_call(functools.partial(pack_x_kernel, nx), grid=(groups,), out_...  6.2 us
    ppermute x3, waiting for transfers between devices, shift_up(): lax.ppermute(value, axis, [(i, (i + 1) % count) for i in range(count)])  3.92 us
    ppermute x2, starting transfers between devices, shift_down(): lax.ppermute(value, axis, [((i + 1) % count, i) for i in range(count)])  3.82 us
    ppermute x3, starting transfers between devices, shift_up(): lax.ppermute(value, axis, [(i, (i + 1) % count) for i in range(count)])  3.14 us
    pallas_call x1, Pallas kernels, shards(): pl.pallas_call(functools.partial(pack_y_kernel, nx), grid=(groups + 1,),...  2.91 us
  transfers between devices with their start and end apart: 7, of which 3 were waited for; matrix products, arithmetic and copies ran while one was open for 4% of the time, Pallas kernels for 35%

profile of v2, /device:TPU:0, one launch (start us, length us, event | category | flops | bytes accessed | tf_op | source)
XLA Modules:
  0.0 69.7 jit_solution(441110808529364465)
XLA Ops:
  0.0 0.9 %slice.3 = f32[32,1,128]{2,1,0:T(1,128)S(1)} slice(f32[32,4,128]{2,1,0:T(4,128)} %param.12), slice={[0:32], [3:4], [0:128]} | slice | bytes 32768 | tf_op jit(solution)/shard_map/slice | solution.py:296
  0.9 0.5 collective-permute-start.2
  1.4 0.0 copy-start
  1.4 6.2 %pack_x.1 = (f32[64,32,128]{2,1,0:T(8,128)}, f32[64,32,128]{2,1,0:T(8,128)S(1)}) custom-call(f32[64,128,128]{2,1,0:T(8,128)} %bitcast.11), custom_call_target="tpu_custom_call" | custom-call | flops 1048576 | bytes 6291456 | tf_op jit(solution)/shard_map/pack_x/pallas_call | solution.py:284
  7.6 2.6 %collective-permute-start.3 = (f32[64,32,128]{2,1,0:T(8,128)}, f32[64,32,128]{2,1,0:T(8,128)S(1)}, u32[]{:S(2)}, u32[]{:S(2)}) collective-permute-start(f32[64,32,128]{2,1,0:T(8,128)} %get-tuple-element.17), channel_id=1, source_target_pairs={{0,8},{8,16},{16,24},{24,0},{1,9},{9,17},{17,25},{25,1},{2,10},{10... | collective-permute-start | bytes 3145736 | tf_op jit(solution)/shard_map/ppermute | solution.py:252
  10.2 0.0 collective-permute-start.4
  10.2 0.0 copy-done
  10.2 0.0 copy-start.1
  10.2 0.8 %copy-done.1 = f32[32,4,128]{2,1,0:T(4,128)S(1)} copy-done((f32[32,4,128]{2,1,0:T(4,128)S(1)}, f32[32,4,128]{2,1,0:T(4,128)}, u32[]{:S(2)}) %copy-start.1) | copy-done | bytes 65560
  11.0 0.0 copy-start.11
  11.0 0.0 copy-start.6
  11.1 0.0 copy-start.7
  11.1 0.0 copy-start.8
  11.1 0.0 copy-start.9
  11.1 0.0 copy-start.10
  11.1 0.0 copy-start.2
  11.1 0.0 copy-start.3
  11.1 2.9 %pack_y.1 = (f32[9,8,128]{2,1,0:T(8,128)S(1)}, f32[8,8,128]{2,1,0:T(8,128)S(1)}) custom-call(f32[64,128,128]{2,1,0:T(8,128)S(1)} %bitcast.14, f32[128,128]{1,0:T(8,128)S(1)} %bitcast.15), custom_call_target="tpu_custom_call" | custom-call | flops 4194304 | bytes 4194304 | tf_op jit(solution)/shard_map/pack_y/pallas_call | solution.py:299
  14.0 3.8 %collective-permute-start.1 = (f32[8,8,128]{2,1,0:T(8,128)S(1)}, f32[8,8,128]{2,1,0:T(8,128)S(1)}, u32[]{:S(2)}, u32[]{:S(2)}) collective-permute-start(f32[8,8,128]{2,1,0:T(8,128)S(1)} %get-tuple-element.21), channel_id=1, source_target_pairs={{2,0},{4,2},{6,4},{0,6},{3,1},{5,3},{7,5},{1,7},{10,8},{12,10},{14... | collective-permute-start | bytes 98312 | tf_op jit(solution)/shard_map/ppermute | solution.py:257
  17.8 0.0 collective-permute-start
  17.9 0.0 copy-done.11
  17.9 0.1 pad_maximum_fusion.1
  18.0 0.0 copy-done.6
  18.0 0.1 copy.14
  18.1 0.1 reshape.80
  18.2 0.1 pad_maximum_fusion
  18.3 0.1 multiply_exponential_fusion
  18.3 0.8 %exponential_select_fusion = f32[64,4,8]{2,1,0:T(4,128)} fusion(f32[4,8]{1,0:T(4,128)S(1)} %pad_maximum_fusion, f32[64]{0:T(128)S(1)} %get-tuple-element.29, pred[4,8]{1,0:T(4,128)(4,1)S(1)} %pad_add_fusion), kind=kLoop, calls=%fused_computation | loop fusion | flops 4096 | bytes 8608 | tf_op jit(solution)/shard_map/jit(_where)/select_n | solution.py:326
  19.1 0.1 exp.15
  19.2 0.0 copy-done.7
  19.2 0.1 copy.13
  19.3 0.1 reshape.79
  19.4 0.0 copy-done.8
  19.4 0.1 copy.15
  19.5 0.1 reshape.81
  19.6 0.0 copy-done.9
  19.6 0.0 copy-done.10
  19.6 0.1 concatenate.6.refs_0_
  19.7 0.0 collective-permute-done.1.refs_5_
  19.7 3.9 %collective-permute-done.refs_4_ = f32[9,8,128]{2,1,0:T(8,128)S(1)} collective-permute-done((f32[9,8,128]{2,1,0:T(8,128)S(1)}, f32[9,8,128]{2,1,0:T(8,128)S(1)}, u32[]{:S(2)}, u32[]{:S(2)}) %collective-permute-start) | collective-permute-done | bytes 36896 | tf_op jit(solution)/shard_map/ppermute | solution.py:252
  23.6 1.2 %broadcast_in_dim.20.refs_6_.refs_4_ = f32[64,4,8,128]{3,2,1,0:T(8,128)S(1)} broadcast(f32[64,4,8]{2,1,0:T(4,128)} %exponential_select_fusion), dimensions={0,1,2} | broadcast | bytes 1056768 | tf_op jit(solution)/shard_map/broadcast_in_dim | solution.py:327
  24.8 0.0 copy-done.2
  24.8 0.0 copy-done.3
  24.9 0.0 copy-start.4
  24.9 0.0 copy-start.5
  24.9 10.0 %settle_inner.1 = (f32[64,8,8,128]{3,2,1,0:T(8,128)S(1)}, f32[2,64,128]{2,1,0:T(8,128)S(1)}) custom-call(f32[768]{0:T(1024)S(1)} %concatenate.6.refs_0_, f32[64,128,128]{2,1,0:T(8,128)} %bitcast.12, f32[128,128]{1,0:T(8,128)S(1)} %bitcast.18, f32[128,128]{1,0:T(8,128)S(1)} %bitcast.16, f32[9,8,128]{2,1,0:T(8,128)S(1)} %collective-permute-done.refs_4_, ...), custom_call_target="tpu_custom_call" | custom-call | flops 16777216 | bytes 8388608 | tf_op jit(solution)/shard_map/settle_inner/pallas_call | solution.py:347
  34.9 1.3 %collective-permute-start.5 = (f32[2,64,128]{2,1,0:T(8,128)S(1)}, f32[2,64,128]{2,1,0:T(8,128)S(1)}, u32[]{:S(2)}, u32[]{:S(2)}) collective-permute-start(f32[2,64,128]{2,1,0:T(8,128)S(1)} %get-tuple-element.23), channel_id=1, source_target_pairs={{1,0},{3,2},{5,4},{7,6},{9,8},{11,10},{13,12},{15,14},{17,16},{19,... | collective-permute-start | bytes 196616 | tf_op jit(solution)/shard_map/ppermute | solution.py:367
  36.2 4.8 %collective-permute-done.5.refs_3_ = f32[2,64,128]{2,1,0:T(8,128)S(1)} collective-permute-done((f32[2,64,128]{2,1,0:T(8,128)S(1)}, f32[2,64,128]{2,1,0:T(8,128)S(1)}, u32[]{:S(2)}, u32[]{:S(2)}) %collective-permute-start.5) | collective-permute-done | bytes 65568 | tf_op jit(solution)/shard_map/ppermute | solution.py:367
  41.1 0.0 copy-done.4
  41.1 0.0 copy-done.5
  41.1 4.9 %micro_inner.1.refs_7_ = f32[64,8,8,128]{3,2,1,0:T(8,128)S(1)} custom-call(f32[768]{0:T(1024)S(1)} %concatenate.6.refs_0_, s32[768]{0:T(1024)S(1)} %constant_dynamic-update-slice_fusion.refs_1_, f32[64,8,8,128]{3,2,1,0:T(8,128)S(1)} %get-tuple-element.22.refs_2_, f32[2,64,128]{2,1,0:T(8,128)S(1)} %collective-permute-done.5.refs_3_, ...), custom_call_target="tpu_custom_call" | custom-call | flops 16777216 | bytes 8388608 | tf_op jit(solution)/shard_map/micro_inner/pallas_call | solution.py:377
  46.0 0.0 collective-permute-done.3.refs_8_
  46.0 0.0 collective-permute-done.4.refs_9_
  46.0 0.0 collective-permute-done.2.refs_7_
  46.0 10.0 %settle_edge.1 = (f32[64,8,8,128]{3,2,1,0:T(8,128)S(1)}, f32[2,64,128]{2,1,0:T(8,128)S(1)}) custom-call(f32[768]{0:T(1024)S(1)} %concatenate.6.refs_0_, f32[64,128,128]{2,1,0:T(8,128)} %bitcast.13, f32[128,128]{1,0:T(8,128)S(1)} %bitcast.19, f32[128,128]{1,0:T(8,128)S(1)} %bitcast.17, f32[9,8,128]{2,1,0:T(8,128)S(1)} %collective-permute-done.refs_4_, ...), custom_call_target="tpu_custom_call" | custom-call | flops 16777216 | bytes 8388608 | tf_op jit(solution)/shard_map/settle_edge/pallas_call | solution.py:347
  56.0 1.3 %collective-permute-start.6 = (f32[2,64,128]{2,1,0:T(8,128)S(1)}, f32[2,64,128]{2,1,0:T(8,128)S(1)}, u32[]{:S(2)}, u32[]{:S(2)}) collective-permute-start(f32[2,64,128]{2,1,0:T(8,128)S(1)} %get-tuple-element.27), channel_id=1, source_target_pairs={{1,0},{3,2},{5,4},{7,6},{9,8},{11,10},{13,12},{15,14},{17,16},{19,... | collective-permute-start | bytes 196616 | tf_op jit(solution)/shard_map/ppermute | solution.py:367
  57.3 4.9 %collective-permute-done.6.refs_3_ = f32[2,64,128]{2,1,0:T(8,128)S(1)} collective-permute-done((f32[2,64,128]{2,1,0:T(8,128)S(1)}, f32[2,64,128]{2,1,0:T(8,128)S(1)}, u32[]{:S(2)}, u32[]{:S(2)}) %collective-permute-start.6) | collective-permute-done | bytes 65568 | tf_op jit(solution)/shard_map/ppermute | solution.py:367
  62.2 7.5 %micro_edge.1 = f32[64,128,128]{2,1,0:T(8,128)} custom-call(f32[768]{0:T(1024)S(1)} %concatenate.6.refs_0_, s32[768]{0:T(1024)S(1)} %constant_dynamic-update-slice_fusion.refs_1_, f32[64,8,8,128]{3,2,1,0:T(8,128)S(1)} %get-tuple-element.26.refs_2_, f32[2,64,128]{2,1,0:T(8,128)S(1)} %collective-permute-done.6.refs_3_, ...), custom_call_target="tpu_custom_call" | custom-call | flops 16777216 | bytes 8388608 | tf_op jit(solution)/shard_map/micro_edge/pallas_call | solution.py:377
  (10 shorter events, 0.1 us)
Async XLA Ops:
  0.9 45.2 %collective-permute-start.2 = (f32[32,128]{1,0:T(8,128)S(1)}, f32[32,128]{1,0:T(8,128)S(1)}, u32[]{:S(2)}, u32[]{:S(2)}) collective-permute-start(f32[32,128]{1,0:T(8,128)S(1)} %bitcast.24), channel_id=1, source_target_pairs={{0,8},{8,16},{16,24},{24,0},{1,9},{9,17},{17,25},{25,1},{2,10},{10... | collective-permute-start | bytes 49160 | tf_op jit(solution)/shard_map/ppermute | solution.py:252
  1.4 8.8 %copy-start = (f32[64,32,4,128]{3,2,1,0:T(4,128)S(1)}, f32[64,32,4,128]{3,2,1,0:T(4,128)}, u32[]{:S(2)}) copy-start(f32[64,32,4,128]{3,2,1,0:T(4,128)} %param.11) | copy-start | bytes 12582916
  7.6 38.4 %collective-permute-start.3 = (f32[64,32,128]{2,1,0:T(8,128)}, f32[64,32,128]{2,1,0:T(8,128)S(1)}, u32[]{:S(2)}, u32[]{:S(2)}) collective-permute-start(f32[64,32,128]{2,1,0:T(8,128)} %get-tuple-element.17), channel_id=1, source_target_pairs={{0,8},{8,16},{16,24},{24,0},{1,9},{9,17},{17,25},{25,1},{2,10},{10... | collective-permute-start | bytes 3145736 | tf_op jit(solution)/shard_map/ppermute | solution.py:252
  10.2 35.8 %collective-permute-start.4 = (f32[64,32,128]{2,1,0:T(8,128)S(1)}, f32[64,32,128]{2,1,0:T(8,128)S(1)}, u32[]{:S(2)}, u32[]{:S(2)}) collective-permute-start(f32[64,32,128]{2,1,0:T(8,128)S(1)} %get-tuple-element.18), channel_id=1, source_target_pairs={{8,0},{16,8},{24,16},{0,24},{9,1},{17,9},{25,17},{1,25},{10,2},{18... | collective-permute-start | bytes 3145736 | tf_op jit(solution)/shard_map/ppermute | solution.py:257
  10.2 0.8 %copy-start.1 = (f32[32,4,128]{2,1,0:T(4,128)S(1)}, f32[32,4,128]{2,1,0:T(4,128)}, u32[]{:S(2)}) copy-start(f32[32,4,128]{2,1,0:T(4,128)} %param.13) | copy-start | bytes 196612
  11.0 6.8 %copy-start.11 = (f32[64]{0:T(128)S(1)}, f32[64]{0:T(128)}, u32[]{:S(2)}) copy-start(f32[64]{0:T(128)} %param.16) | copy-start | bytes 772
  11.0 6.9 %copy-start.6 = (s32[48,8]{0,1:T(8,128)S(1)}, s32[48,8]{0,1:T(8,128)}, u32[]{:S(2)}) copy-start(s32[48,8]{0,1:T(8,128)} %param.20) | copy-start | bytes 4612
  11.1 8.2 %copy-start.7 = (f32[48,8]{0,1:T(8,128)S(1)}, f32[48,8]{0,1:T(8,128)}, u32[]{:S(2)}) copy-start(f32[48,8]{0,1:T(8,128)} %param.19) | copy-start | bytes 4612
  11.1 8.3 %copy-start.8 = (s32[48,8]{0,1:T(8,128)S(1)}, s32[48,8]{0,1:T(8,128)}, u32[]{:S(2)}) copy-start(s32[48,8]{0,1:T(8,128)} %param.21) | copy-start | bytes 4612
  11.1 8.5 %copy-start.9 = (f32[47]{0:T(128)S(1)}, f32[47]{0:T(128)}, u32[]{:S(2)}) copy-start(f32[47]{0:T(128)} %param.17) | copy-start | bytes 568
  11.1 8.5 %copy-start.10 = (f32[16]{0:T(128)S(1)}, f32[16]{0:T(128)}, u32[]{:S(2)}) copy-start(f32[16]{0:T(128)} %param.18) | copy-start | bytes 196
  11.1 13.8 %copy-start.2 = (f32[32,4,128]{2,1,0:T(4,128)S(1)}, f32[32,4,128]{2,1,0:T(4,128)}, u32[]{:S(2)}) copy-start(f32[32,4,128]{2,1,0:T(4,128)} %param.13) | copy-start | bytes 196612
  11.1 13.8 %copy-start.3 = (f32[32,4,128]{2,1,0:T(4,128)S(1)}, f32[32,4,128]{2,1,0:T(4,128)}, u32[]{:S(2)}) copy-start(f32[32,4,128]{2,1,0:T(4,128)} %param.12) | copy-start | bytes 196612
  14.0 5.7 %collective-permute-start.1 = (f32[8,8,128]{2,1,0:T(8,128)S(1)}, f32[8,8,128]{2,1,0:T(8,128)S(1)}, u32[]{:S(2)}, u32[]{:S(2)}) collective-permute-start(f32[8,8,128]{2,1,0:T(8,128)S(1)} %get-tuple-element.21), channel_id=1, source_target_pairs={{2,0},{4,2},{6,4},{0,6},{3,1},{5,3},{7,5},{1,7},{10,8},{12,10},{14... | collective-permute-start | bytes 98312 | tf_op jit(solution)/shard_map/ppermute | solution.py:257
  17.8 5.8 %collective-permute-start = (f32[9,8,128]{2,1,0:T(8,128)S(1)}, f32[9,8,128]{2,1,0:T(8,128)S(1)}, u32[]{:S(2)}, u32[]{:S(2)}) collective-permute-start(f32[9,8,128]{2,1,0:T(8,128)S(1)} %get-tuple-element.20), channel_id=1, source_target_pairs={{0,2},{2,4},{4,6},{6,0},{1,3},{3,5},{5,7},{7,1},{8,10},{10,12},{12... | collective-permute-start | bytes 110600 | tf_op jit(solution)/shard_map/ppermute | solution.py:252
  24.9 16.2 %copy-start.4 = (f32[32,4,128]{2,1,0:T(4,128)S(1)}, f32[32,4,128]{2,1,0:T(4,128)}, u32[]{:S(2)}) copy-start(f32[32,4,128]{2,1,0:T(4,128)} %param.14) | copy-start | bytes 196612
  24.9 16.2 %copy-start.5 = (s32[32,4,128]{2,1,0:T(4,128)S(1)}, s32[32,4,128]{2,1,0:T(4,128)}, u32[]{:S(2)}) copy-start(s32[32,4,128]{2,1,0:T(4,128)} %param.15) | copy-start | bytes 196612
  34.9 6.2 %collective-permute-start.5 = (f32[2,64,128]{2,1,0:T(8,128)S(1)}, f32[2,64,128]{2,1,0:T(8,128)S(1)}, u32[]{:S(2)}, u32[]{:S(2)}) collective-permute-start(f32[2,64,128]{2,1,0:T(8,128)S(1)} %get-tuple-element.23), channel_id=1, source_target_pairs={{1,0},{3,2},{5,4},{7,6},{9,8},{11,10},{13,12},{15,14},{17,16},{19,... | collective-permute-start | bytes 196616 | tf_op jit(solution)/shard_map/ppermute | solution.py:367
  56.0 6.2 %collective-permute-start.6 = (f32[2,64,128]{2,1,0:T(8,128)S(1)}, f32[2,64,128]{2,1,0:T(8,128)S(1)}, u32[]{:S(2)}, u32[]{:S(2)}) collective-permute-start(f32[2,64,128]{2,1,0:T(8,128)S(1)} %get-tuple-element.27), channel_id=1, source_target_pairs={{1,0},{3,2},{5,4},{7,6},{9,8},{11,10},{13,12},{15,14},{17,16},{19,... | collective-permute-start | bytes 196616 | tf_op jit(solution)/shard_map/ppermute | solution.py:367

commit v3 on v2

--- a/solution.py
+++ b/solution.py
@@ -15,13 +15,6 @@
 def roll_to(value, source, dest):
     shift = (dest - source) % LANES
     return value if shift == 0 else pltpu.roll(value, shift, 1)
-
-
-def pack_x_kernel(nx, field_ref, right_ref, left_ref):
-    rows = field_ref.shape[1]
-    for b in range(field_ref.shape[0]):
-        right_ref[b] = field_ref[b, pl.ds(nx - 1, rows // nx, stride=nx), :]
-        left_ref[b] = field_ref[b, pl.ds(0, rows // nx, stride=nx), :]
 
 
 def pack_y_kernel(nx, field_ref, cour_ref, right_ref, left_ref):
@@ -59,24 +52,28 @@
         right_ref[0] = one(lambda r: cour_ref[r, :], 0, (zero, zero))[0]
 
 
-def advect_settle_kernel(nx, xs, halos, *refs):
-    if halos:
-        scal, field, cx, cy, yl, yr, table, cl, xl, xr, out, bottom = refs
-    else:
-        scal, field, cx, cy, yl, yr, table, out, bottom = refs
-        cl = xl = xr = None
+def scan_levels(value, table, b):
+    value = value + table[b, 0] * pltpu.roll(value, SUB - 1, 0)
+    value = value + table[b, 1] * pltpu.roll(value, SUB - 2, 0)
+    return value + table[b, 2] * pltpu.roll(value, SUB - 4, 0)
+
+
+def settle_kernel(nx, sets, *refs):
+    scal, field, cx, cy, yl, yr, table = refs[:7]
+    outs = refs[7:]
     bins, rows, _ = field.shape
     blocks = rows // (SUB * nx)
     per_bin = nx * blocks
     lane = lax.broadcasted_iota(jnp.int32, (SUB, LANES), 1)
     first, last = lane == 0, lane == LANES - 1
-    for xi, x in enumerate(xs):
+    places = [
+        (x, xi, outs[2 * n], outs[2 * n + 1]) for n, xs in enumerate(sets) for xi, x in enumerate(xs)
+    ]
+    for x, xi, out, bottom in places:
         for q in reversed(range(blocks)):
             span = lambda xx: pl.ds(q * SUB * nx + xx, SUB, stride=nx)
             spot = x * blocks + q
-            zrows = pl.ds(q * SUB, SUB)
             c_here = cx[span(x), :]
-            c_left = cx[span(x - 1), :] if x > 0 else cl[zrows, :]
             y_here = cy[span(x), :]
             y_left = jnp.where(
                 first, roll_to(yl[bins // GROUP], spot, 0), pltpu.roll(y_here, 1, 1)
@@ -84,45 +81,37 @@
             stay = (
                 1.0
                 - jnp.maximum(c_here, 0.0)
-                + jnp.minimum(c_left, 0.0)
                 - jnp.maximum(y_here, 0.0)
                 + jnp.minimum(y_left, 0.0)
             )
+            if x > 0:
+                c_left = cx[span(x - 1), :]
+                stay = stay + jnp.minimum(c_left, 0.0)
+                from_left = jnp.maximum(c_left, 0.0)
             from_right = -jnp.minimum(c_here, 0.0)
-            from_left = jnp.maximum(c_left, 0.0)
             from_up = -jnp.minimum(y_here, 0.0)
             from_down = jnp.maximum(y_left, 0.0)
 
             def group(g, _):
                 down_pack = yl[g]
                 up_pack = yr[g]
-                moved, falls = [], []
+                falls = []
                 for k in range(GROUP):
                     b = g * GROUP + k
                     here = field[b, span(x), :]
-                    left = field[b, span(x - 1), :] if x > 0 else xl[b, zrows, :]
-                    right = field[b, span(x + 1), :] if x < nx - 1 else xr[b, zrows, :]
                     at = k * per_bin + spot
                     down = jnp.where(first, roll_to(down_pack, at, 0), pltpu.roll(here, 1, 1))
                     up = jnp.where(
                         last, roll_to(up_pack, at, LANES - 1), pltpu.roll(here, LANES - 1, 1)
                     )
-                    moved.append(
-                        stay * here
-                        + from_right * right
-                        + from_left * left
-                        + from_up * up
-                        + from_down * down
-                    )
-                for k in range(GROUP):
-                    b = g * GROUP + k
-                    fall = moved[k] * scal[b]
-                    fall = fall + table[b, 0] * pltpu.roll(fall, SUB - 1, 0)
-                    fall = fall + table[b, 1] * pltpu.roll(fall, SUB - 2, 0)
-                    fall = fall + table[b, 2] * pltpu.roll(fall, SUB - 4, 0)
+                    moved = stay * here + from_up * up + from_down * down
+                    if x > 0:
+                        moved = moved + from_left * field[b, span(x - 1), :]
+                    if x < nx - 1:
+                        moved = moved + from_right * field[b, span(x + 1), :]
+                    fall = scan_levels(moved * scal[b], table, b)
                     if q < blocks - 1:
-                        above = out[b, xi * blocks + q + 1, pl.ds(0, 1), :]
-                        fall = fall + table[b, 3] * above
+                        fall = fall + table[b, 3] * out[b, xi * blocks + q + 1, pl.ds(0, 1), :]
                     falls.append(fall)
                 for k in range(GROUP):
                     b = g * GROUP + k
@@ -132,6 +121,44 @@
                 return 0
 
             lax.fori_loop(0, bins // GROUP, group, 0)
+
+
+def edge_kernel(nx, *refs):
+    scal, part, part_bottom, cx, table, cl, own, xl, xr, out, bottom = refs
+    bins, cells = part.shape[:2]
+    blocks = cells // 2
+    leaves = [jnp.minimum(cl[pl.ds(q * SUB, SUB), :], 0.0) for q in range(blocks)]
+    enters = [jnp.maximum(cl[pl.ds(q * SUB, SUB), :], 0.0) for q in range(blocks)]
+    backs = [
+        -jnp.minimum(cx[pl.ds(q * SUB * nx + nx - 1, SUB, stride=nx), :], 0.0)
+        for q in range(blocks)
+    ]
+
+    def group(g, _):
+        values, ends = [], []
+        for k in range(4):
+            b = g * 4 + k
+            for xi in range(2):
+                above = None
+                for q in reversed(range(blocks)):
+                    zrows = pl.ds(q * SUB, SUB)
+                    if xi == 0:
+                        flux = enters[q] * xl[b, zrows, :] + leaves[q] * own[b, zrows, :]
+                    else:
+                        flux = backs[q] * xr[b, zrows, :]
+                    fall = scan_levels(flux * scal[b], table, b)
+                    if above is not None:
+                        fall = fall + table[b, 3] * above
+                    above = fall[0:1, :]
+                    values.append((b, xi * blocks + q, fall + part[b, xi * blocks + q]))
+                ends.append((xi, b, above + part_bottom[xi, pl.ds(b, 1), :]))
+        for b, v, value in values:
+            out[b, v] = value
+        for xi, b, value in ends:
+            bottom[xi, pl.ds(b, 1), :] = value
+        return 0
+
+    lax.fori_loop(0, bins // 4, group, 0)
 
 
 def micro_kernel(nx, xs, slots, merge, *refs):
@@ -280,21 +307,11 @@
     )
 
     groups = bins // GROUP
-    face = jax.ShapeDtypeStruct((bins, depth, ny), f32)
-    to_right, to_left = pl.pallas_call(
-        functools.partial(pack_x_kernel, nx),
-        grid=(groups,),
-        out_shape=(face, face),
-        in_specs=[pl.BlockSpec((GROUP, depth * nx, ny), lambda g: (g, 0, 0))],
-        out_specs=(pl.BlockSpec((GROUP, depth, ny), lambda g: (g, 0, 0)),) * 2,
-        compiler_params=PARAMS,
-        cost_estimate=cost(1 << 20, 6 << 20),
-        name="pack_x",
-    )(flat)
+    to_right, to_left = field[:, :, nx - 1, :], field[:, :, 0, :]
     x_left = shift_up(to_right, "gx")
     x_right = shift_down(to_left, "gx")
-    cx_left = shift_up(courant_x[:, nx - 1, :], "gx")
-    flat_y, _, _ = lax.optimization_barrier((flat, to_right, to_left))
+    flat_y, cx_last, to_right, to_left = lax.optimization_barrier((flat, courant_x, to_right, to_left))
+    cx_left = shift_up(cx_last[:, nx - 1, :], "gx")
 
     y_to_right, y_to_left = pl.pallas_call(
         functools.partial(pack_y_kernel, nx),
@@ -341,21 +358,11 @@
     inner_x = tuple(range(1, nx - 1))
     edge_x = (0, nx - 1)
 
-    def settle_part(xs, halos):
-        cells = len(xs) * blocks
-        args = [scal, flat, cx, cy, y_left, y_right, table] + list(halos)
-        return pl.pallas_call(
-            functools.partial(advect_settle_kernel, nx, xs, bool(halos)),
-            out_shape=(
-                jax.ShapeDtypeStruct((bins, cells, SUB, LANES), f32),
-                jax.ShapeDtypeStruct((len(xs), bins, LANES), f32),
-            ),
-            in_specs=[SMEM] + [VMEM] * (len(args) - 1),
-            out_specs=(VMEM, VMEM),
-            compiler_params=PARAMS,
-            cost_estimate=cost(1 << 24, 8 << 20),
-            name="settle_edge" if halos else "settle_inner",
-        )(*args)
+    def settle_shapes(xs):
+        return (
+            jax.ShapeDtypeStruct((bins, len(xs) * blocks, SUB, LANES), f32),
+            jax.ShapeDtypeStruct((len(xs), bins, LANES), f32),
+        )
 
     count = lax.axis_size("gz")
     whole = jnp.exp(log_ratio * depth)[None, :, None]
@@ -388,11 +395,29 @@
             name="micro_edge" if inner else "micro_inner",
         )(*args)
 
-    settled, bottom = settle_part(inner_x, ())
-    inner = micro_part(inner_x, settled, inflow(bottom), ())
-    x_left, x_right, inner = lax.optimization_barrier((x_left, x_right, inner))
-    settled, bottom = settle_part(edge_x, (cx_left, x_left, x_right))
-    out = micro_part(edge_x, settled, inflow(bottom), (inner,))
+    settled, bottom, part, part_bottom = pl.pallas_call(
+        functools.partial(settle_kernel, nx, (inner_x, edge_x)),
+        out_shape=settle_shapes(inner_x) + settle_shapes(edge_x),
+        in_specs=[SMEM] + [VMEM] * 6,
+        out_specs=(VMEM,) * 4,
+        compiler_params=PARAMS,
+        cost_estimate=cost(1 << 24, 16 << 20),
+        name="settle_all",
+    )(scal, flat_y, cx, cy, y_left, y_right, table)
+    inner_carry = inflow(bottom)
+    edge_settled, edge_bottom = pl.pallas_call(
+        functools.partial(edge_kernel, nx),
+        out_shape=settle_shapes(edge_x),
+        in_specs=[SMEM] + [VMEM] * 8,
+        out_specs=(VMEM,) * 2,
+        compiler_params=PARAMS,
+        cost_estimate=cost(1 << 23, 8 << 20),
+        name="settle_edge",
+    )(scal, part, part_bottom, cx, table, cx_left, to_left, x_left, x_right)
+    settled, edge_bottom = lax.optimization_barrier((settled, edge_bottom))
+    edge_carry = inflow(edge_bottom)
+    inner = micro_part(inner_x, settled, inner_carry, ())
+    out = micro_part(edge_x, edge_settled, edge_carry, (inner,))
     return out.reshape(field.shape)
 
 

time: 70 us -> 61.1 us (0.87)
  the two profiles are of different devices: /device:TPU:0 before, /device:TPU:3 now
where the time goes in v3:
time: 61.1 us; the launch traced here: 60.8 us
  Pallas kernels  37.5 us (61%)
  local copies, waits for them, and re-layouts  11 us (18%)
  starting transfers between devices  10.9 us (18%)
  other arithmetic  1.08 us (2%)
    pallas_call x1, Pallas kernels, shards(): pl.pallas_call(functools.partial(settle_kernel, nx, (inner_x, edge_x)), o...  18 us
    pallas_call x2, Pallas kernels, micro_part(): pl.pallas_call(functools.partial(micro_kernel, nx, xs, slots, bool(inner)...  12.4 us
    slice x1, local copies, waits for them, and re-layouts, shards(): to_right, to_left = (field[:, :, nx - 1, :], field[:, :, 0, :])  6.89 us
    ppermute x3, starting transfers between devices, shift_up(): lax.ppermute(value, axis, [(i, (i + 1) % count) for i in range(count)])  5.38 us
    pallas_call x1, Pallas kernels, shards(): pl.pallas_call(functools.partial(edge_kernel, nx), out_shape=settle_shape...  4.18 us
    ppermute x2, starting transfers between devices, inflow(): carry = lax.ppermute(sent, 'gz', [(i + 1, i) for i in range(count - 1)])  3.43 us
    pallas_call x1, Pallas kernels, shards(): pl.pallas_call(functools.partial(pack_y_kernel, nx), grid=(groups + 1,),...  2.91 us
    unnamed x32, local copies, waits for them, and re-layouts  2.46 us
  transfers between devices with their start and end apart: 7, of which 0 were waited for; matrix products, arithmetic and copies ran while one was open for 5% of the time, Pallas kernels for 49%

profile of v3, /device:TPU:3, one launch (start us, length us, event | category | flops | bytes accessed | tf_op | source)
XLA Modules:
  0.0 60.8 jit_solution(14866258829601441073)
XLA Ops:
  0.0 0.0 copy-start
  0.0 6.9 %fusion.1 = (f32[64,32,1,128]{3,2,1,0:T(1,128)S(1)}, f32[64,32,1,128]{3,2,1,0:T(1,128)}) fusion(f32[64,32,4,128]{3,2,1,0:T(4,128)} %param.11), kind=kLoop, calls=%fused_computation.17 | loop fusion | bytes 4194304 | tf_op jit(solution)/shard_map/slice | solution.py:310
  6.9 1.8 %collective-permute-start.3 = (f32[64,32,128]{2,1,0:T(8,128)}, f32[64,32,128]{2,1,0:T(8,128)S(1)}, u32[]{:S(2)}, u32[]{:S(2)}) collective-permute-start(f32[64,32,128]{2,1,0:T(8,128)} %bitcast.1), channel_id=1, source_target_pairs={{0,8},{8,16},{16,24},{24,0},{1,9},{9,17},{17,25},{25,1},{2,10},{10... | collective-permute-start | bytes 3145736 | tf_op jit(solution)/shard_map/ppermute | solution.py:279
  8.7 0.0 collective-permute-start.4
  8.7 0.0 copy-done
  8.7 0.0 copy-start.4
  8.7 0.8 %copy-done.4 = f32[32,4,128]{2,1,0:T(4,128)S(1)} copy-done((f32[32,4,128]{2,1,0:T(4,128)S(1)}, f32[32,4,128]{2,1,0:T(4,128)}, u32[]{:S(2)}) %copy-start.4) | copy-done | bytes 65560
  9.5 0.0 copy-start.3
  9.5 0.0 copy-start.8
  9.5 0.0 copy-start.13
  9.5 0.0 copy-start.9
  9.5 0.0 copy-start.10
  9.6 0.0 copy-start.11
  9.6 0.0 copy-start.12
  9.6 0.0 copy-start.5
  9.6 2.9 %pack_y.1 = (f32[9,8,128]{2,1,0:T(8,128)S(1)}, f32[8,8,128]{2,1,0:T(8,128)S(1)}) custom-call(f32[64,128,128]{2,1,0:T(8,128)S(1)} %bitcast.17, f32[128,128]{1,0:T(8,128)S(1)} %bitcast.22), custom_call_target="tpu_custom_call" | custom-call | flops 4194304 | bytes 4194304 | tf_op jit(solution)/shard_map/pack_y/pallas_call | solution.py:316
  12.5 1.3 %collective-permute-start = (f32[9,8,128]{2,1,0:T(8,128)S(1)}, f32[9,8,128]{2,1,0:T(8,128)S(1)}, u32[]{:S(2)}, u32[]{:S(2)}) collective-permute-start(f32[9,8,128]{2,1,0:T(8,128)S(1)} %get-tuple-element.19), channel_id=1, source_target_pairs={{0,2},{2,4},{4,6},{6,0},{1,3},{3,5},{5,7},{7,1},{8,10},{10,12},{12... | collective-permute-start | bytes 110600 | tf_op jit(solution)/shard_map/ppermute | solution.py:279
  13.9 2.1 %collective-permute-start.1 = (f32[8,8,128]{2,1,0:T(8,128)S(1)}, f32[8,8,128]{2,1,0:T(8,128)S(1)}, u32[]{:S(2)}, u32[]{:S(2)}) collective-permute-start(f32[8,8,128]{2,1,0:T(8,128)S(1)} %get-tuple-element.20), channel_id=1, source_target_pairs={{2,0},{4,2},{6,4},{0,6},{3,1},{5,3},{7,5},{1,7},{10,8},{12,10},{14... | collective-permute-start | bytes 98312 | tf_op jit(solution)/shard_map/ppermute | solution.py:284
  16.0 0.0 copy-done.3
  16.0 2.2 %collective-permute-start.2 = (f32[32,128]{1,0:T(8,128)S(1)}, f32[32,128]{1,0:T(8,128)S(1)}, u32[]{:S(2)}, u32[]{:S(2)}) collective-permute-start(f32[32,128]{1,0:T(8,128)S(1)} %slice_bitcast_fusion), channel_id=1, source_target_pairs={{0,8},{8,16},{16,24},{24,0},{1,9},{9,17},{17,25},{25,1},{2,10},{10... | collective-permute-start | bytes 49160 | tf_op jit(solution)/shard_map/ppermute | solution.py:279
  18.3 0.1 pad_maximum_fusion.1
  18.4 0.0 copy-done.8
  18.4 0.1 copy.16
  18.4 0.1 reshape.80
  18.5 0.0 copy-done.13
  18.6 0.1 pad_maximum_fusion
  18.6 0.1 multiply_exponential_fusion
  18.7 0.8 %exponential_select_fusion = f32[64,4,8]{2,1,0:T(4,128)} fusion(f32[4,8]{1,0:T(4,128)S(1)} %pad_maximum_fusion, f32[64]{0:T(128)S(1)} %get-tuple-element.33, pred[4,8]{1,0:T(4,128)(4,1)S(1)} %pad_add_fusion), kind=kLoop, calls=%fused_computation | loop fusion | flops 4096 | bytes 8608 | tf_op jit(solution)/shard_map/jit(_where)/select_n | solution.py:343
  19.5 0.1 exp.15
  19.6 0.0 copy-done.9
  19.6 0.1 copy.15
  19.7 0.1 reshape.79
  19.8 0.0 copy-done.10
  19.8 0.1 copy.17
  19.9 0.1 reshape.81
  20.0 0.0 copy-done.11
  20.0 0.0 copy-done.12
  20.0 0.1 concatenate.6.refs_0_
  20.1 0.0 collective-permute-done.1.refs_5_
  20.1 0.0 collective-permute-done.refs_4_
  20.1 1.2 %broadcast_in_dim.20.refs_6_.refs_4_ = f32[64,4,8,128]{3,2,1,0:T(8,128)S(1)} broadcast(f32[64,4,8]{2,1,0:T(4,128)} %exponential_select_fusion), dimensions={0,1,2} | broadcast | bytes 1056768 | tf_op jit(solution)/shard_map/broadcast_in_dim | solution.py:344
  21.3 0.0 copy-done.5
  21.3 18.0 %settle_all.1 = (f32[64,8,8,128]{3,2,1,0:T(8,128)S(1)}, f32[2,64,128]{2,1,0:T(8,128)S(1)}, f32[64,8,8,128]{3,2,1,0:T(8,128)S(1)}, f32[2,64,128]{2,1,0:T(8,128)S(1)}) custom-call(f32[768]{0:T(1024)S(1)} %concatenate.6.refs_0_, f32[64,128,128]{2,1,0:T(8,128)} %bitcast.16, f32[128,128]{1,0:T(8,128)S(1)} %bitcast.20, f32[128,128]{1,0:T(8,128)S(1)} %bitcast.23, ...), custom_call_target="tpu_custom_call" | custom-call | flops 16777216 | bytes 16777216 | tf_op jit(solution)/shard_map/settle_all/pallas_call | solution.py:398
  39.4 0.0 copy-start.2
  39.4 1.3 %copy-done.2 = f32[64,8,8,128]{3,2,1,0:T(8,128)} copy-done((f32[64,8,8,128]{3,2,1,0:T(8,128)}, f32[64,8,8,128]{3,2,1,0:T(8,128)S(1)}, u32[]{:S(2)}) %copy-start.2) | copy-done | bytes 2097176
  40.7 2.1 %collective-permute-start.6 = (f32[2,64,128]{2,1,0:T(8,128)S(1)}, f32[2,64,128]{2,1,0:T(8,128)S(1)}, u32[]{:S(2)}, u32[]{:S(2)}) collective-permute-start(f32[2,64,128]{2,1,0:T(8,128)S(1)} %get-tuple-element.30), channel_id=1, source_target_pairs={{1,0},{3,2},{5,4},{7,6},{9,8},{11,10},{13,12},{15,14},{17,16},{19,... | collective-permute-start | bytes 196616 | tf_op jit(solution)/shard_map/ppermute | solution.py:374
  42.8 0.0 collective-permute-done.2.refs_5_
  42.8 0.0 collective-permute-done.3.refs_7_
  42.9 0.0 collective-permute-done.4.refs_8_
  42.9 0.0 copy-start.6
  42.9 0.0 copy-start.7
  42.9 4.2 %settle_edge.1 = (f32[64,8,8,128]{3,2,1,0:T(8,128)}, f32[2,64,128]{2,1,0:T(8,128)S(1)}) custom-call(f32[768]{0:T(1024)S(1)} %concatenate.6.refs_0_, f32[64,8,8,128]{3,2,1,0:T(8,128)} %copy-done.2, f32[2,64,128]{2,1,0:T(8,128)S(1)} %get-tuple-element.22.refs_2_, f32[128,128]{1,0:T(8,128)S(1)} %bitcast.21, ...), custom_call_target="tpu_custom_call" | custom-call | flops 8388608 | bytes 8388608 | tf_op jit(solution)/shard_map/settle_edge/pallas_call | solution.py:408
  47.1 1.3 %collective-permute-start.5 = (f32[2,64,128]{2,1,0:T(8,128)S(1)}, f32[2,64,128]{2,1,0:T(8,128)S(1)}, u32[]{:S(2)}, u32[]{:S(2)}) collective-permute-start(f32[2,64,128]{2,1,0:T(8,128)S(1)} %get-tuple-element.28), channel_id=1, source_target_pairs={{1,0},{3,2},{5,4},{7,6},{9,8},{11,10},{13,12},{15,14},{17,16},{19,... | collective-permute-start | bytes 196616 | tf_op jit(solution)/shard_map/ppermute | solution.py:374
  48.4 0.0 collective-permute-done.6.refs_3_
  48.4 0.0 copy-done.6
  48.4 0.0 copy-done.7
  48.4 0.0 copy-start.1
  48.4 4.9 %micro_inner.1.refs_7_ = f32[64,8,8,128]{3,2,1,0:T(8,128)S(1)} custom-call(f32[768]{0:T(1024)S(1)} %concatenate.6.refs_0_, s32[768]{0:T(1024)S(1)} %constant_dynamic-update-slice_fusion.refs_1_, f32[64,8,8,128]{3,2,1,0:T(8,128)S(1)} %get-tuple-element.29.refs_2_, f32[2,64,128]{2,1,0:T(8,128)S(1)} %collective-permute-done.6.refs_3_, ...), custom_call_target="tpu_custom_call" | custom-call | flops 16777216 | bytes 8388608 | tf_op jit(solution)/shard_map/micro_inner/pallas_call | solution.py:384
  53.3 0.0 collective-permute-done.5.refs_3_
  53.4 0.0 copy-done.1
  53.4 7.5 %micro_edge.1 = f32[64,128,128]{2,1,0:T(8,128)} custom-call(f32[768]{0:T(1024)S(1)} %concatenate.6.refs_0_, s32[768]{0:T(1024)S(1)} %constant_dynamic-update-slice_fusion.refs_1_, f32[64,8,8,128]{3,2,1,0:T(8,128)S(1)} %copy-done.1, f32[2,64,128]{2,1,0:T(8,128)S(1)} %collective-permute-done.5.refs_3_, f32[64,4,8,128]{3,2,1,0:T(8,128)S(1)} %broadcast_in_dim.20.refs_6_.refs_4_, ...), custom_call_target="tpu_custom_call" | custom-call | flops 16777216 | bytes 8388608 | tf_op jit(solution)/shard_map/micro_edge/pallas_call | solution.py:384
  (12 shorter events, 0.1 us)
Async XLA Ops:
  0.0 8.7 %copy-start = (f32[64,32,4,128]{3,2,1,0:T(4,128)S(1)}, f32[64,32,4,128]{3,2,1,0:T(4,128)}, u32[]{:S(2)}) copy-start(f32[64,32,4,128]{3,2,1,0:T(4,128)} %param.11) | copy-start | bytes 12582916
  6.9 36.0 %collective-permute-start.3 = (f32[64,32,128]{2,1,0:T(8,128)}, f32[64,32,128]{2,1,0:T(8,128)S(1)}, u32[]{:S(2)}, u32[]{:S(2)}) collective-permute-start(f32[64,32,128]{2,1,0:T(8,128)} %bitcast.1), channel_id=1, source_target_pairs={{0,8},{8,16},{16,24},{24,0},{1,9},{9,17},{17,25},{25,1},{2,10},{10... | collective-permute-start | bytes 3145736 | tf_op jit(solution)/shard_map/ppermute | solution.py:279
  8.7 34.2 %collective-permute-start.4 = (f32[64,32,128]{2,1,0:T(8,128)S(1)}, f32[64,32,128]{2,1,0:T(8,128)S(1)}, u32[]{:S(2)}, u32[]{:S(2)}) collective-permute-start(f32[64,32,128]{2,1,0:T(8,128)S(1)} %bitcast.18), channel_id=1, source_target_pairs={{8,0},{16,8},{24,16},{0,24},{9,1},{17,9},{25,17},{1,25},{10,2},{18... | collective-permute-start | bytes 3145736 | tf_op jit(solution)/shard_map/ppermute | solution.py:284
  8.7 0.8 %copy-start.4 = (f32[32,4,128]{2,1,0:T(4,128)S(1)}, f32[32,4,128]{2,1,0:T(4,128)}, u32[]{:S(2)}) copy-start(f32[32,4,128]{2,1,0:T(4,128)} %param.13) | copy-start | bytes 196612
  9.5 6.4 %copy-start.3 = (f32[32,4,128]{2,1,0:T(4,128)S(1)}, f32[32,4,128]{2,1,0:T(4,128)}, u32[]{:S(2)}) copy-start(f32[32,4,128]{2,1,0:T(4,128)} %param.12) | copy-start | bytes 196612
  9.5 8.8 %copy-start.8 = (s32[48,8]{0,1:T(8,128)S(1)}, s32[48,8]{0,1:T(8,128)}, u32[]{:S(2)}) copy-start(s32[48,8]{0,1:T(8,128)} %param.20) | copy-start | bytes 4612
  9.5 9.0 %copy-start.13 = (f32[64]{0:T(128)S(1)}, f32[64]{0:T(128)}, u32[]{:S(2)}) copy-start(f32[64]{0:T(128)} %param.16) | copy-start | bytes 772
  9.5 10.1 %copy-start.9 = (f32[48,8]{0,1:T(8,128)S(1)}, f32[48,8]{0,1:T(8,128)}, u32[]{:S(2)}) copy-start(f32[48,8]{0,1:T(8,128)} %param.19) | copy-start | bytes 4612
  9.5 10.2 %copy-start.10 = (s32[48,8]{0,1:T(8,128)S(1)}, s32[48,8]{0,1:T(8,128)}, u32[]{:S(2)}) copy-start(s32[48,8]{0,1:T(8,128)} %param.21) | copy-start | bytes 4612
  9.6 10.4 %copy-start.11 = (f32[47]{0:T(128)S(1)}, f32[47]{0:T(128)}, u32[]{:S(2)}) copy-start(f32[47]{0:T(128)} %param.17) | copy-start | bytes 568
  9.6 10.4 %copy-start.12 = (f32[16]{0:T(128)S(1)}, f32[16]{0:T(128)}, u32[]{:S(2)}) copy-start(f32[16]{0:T(128)} %param.18) | copy-start | bytes 196
  9.6 11.7 %copy-start.5 = (f32[32,4,128]{2,1,0:T(4,128)S(1)}, f32[32,4,128]{2,1,0:T(4,128)}, u32[]{:S(2)}) copy-start(f32[32,4,128]{2,1,0:T(4,128)} %param.13) | copy-start | bytes 196612
  12.5 7.6 %collective-permute-start = (f32[9,8,128]{2,1,0:T(8,128)S(1)}, f32[9,8,128]{2,1,0:T(8,128)S(1)}, u32[]{:S(2)}, u32[]{:S(2)}) collective-permute-start(f32[9,8,128]{2,1,0:T(8,128)S(1)} %get-tuple-element.19), channel_id=1, source_target_pairs={{0,2},{2,4},{4,6},{6,0},{1,3},{3,5},{5,7},{7,1},{8,10},{10,12},{12... | collective-permute-start | bytes 110600 | tf_op jit(solution)/shard_map/ppermute | solution.py:279
  13.9 6.2 %collective-permute-start.1 = (f32[8,8,128]{2,1,0:T(8,128)S(1)}, f32[8,8,128]{2,1,0:T(8,128)S(1)}, u32[]{:S(2)}, u32[]{:S(2)}) collective-permute-start(f32[8,8,128]{2,1,0:T(8,128)S(1)} %get-tuple-element.20), channel_id=1, source_target_pairs={{2,0},{4,2},{6,4},{0,6},{3,1},{5,3},{7,5},{1,7},{10,8},{12,10},{14... | collective-permute-start | bytes 98312 | tf_op jit(solution)/shard_map/ppermute | solution.py:284
  16.0 26.9 %collective-permute-start.2 = (f32[32,128]{1,0:T(8,128)S(1)}, f32[32,128]{1,0:T(8,128)S(1)}, u32[]{:S(2)}, u32[]{:S(2)}) collective-permute-start(f32[32,128]{1,0:T(8,128)S(1)} %slice_bitcast_fusion), channel_id=1, source_target_pairs={{0,8},{8,16},{16,24},{24,0},{1,9},{9,17},{17,25},{25,1},{2,10},{10... | collective-permute-start | bytes 49160 | tf_op jit(solution)/shard_map/ppermute | solution.py:279
  39.4 1.3 %copy-start.2 = (f32[64,8,8,128]{3,2,1,0:T(8,128)}, f32[64,8,8,128]{3,2,1,0:T(8,128)S(1)}, u32[]{:S(2)}) copy-start(f32[64,8,8,128]{3,2,1,0:T(8,128)S(1)} %get-tuple-element.21.refs_1_) | copy-start | bytes 6291460
  40.7 7.7 %collective-permute-start.6 = (f32[2,64,128]{2,1,0:T(8,128)S(1)}, f32[2,64,128]{2,1,0:T(8,128)S(1)}, u32[]{:S(2)}, u32[]{:S(2)}) collective-permute-start(f32[2,64,128]{2,1,0:T(8,128)S(1)} %get-tuple-element.30), channel_id=1, source_target_pairs={{1,0},{3,2},{5,4},{7,6},{9,8},{11,10},{13,12},{15,14},{17,16},{19,... | collective-permute-start | bytes 196616 | tf_op jit(solution)/shard_map/ppermute | solution.py:374
  42.9 5.5 %copy-start.6 = (f32[32,4,128]{2,1,0:T(4,128)S(1)}, f32[32,4,128]{2,1,0:T(4,128)}, u32[]{:S(2)}) copy-start(f32[32,4,128]{2,1,0:T(4,128)} %param.14) | copy-start | bytes 196612
  42.9 5.5 %copy-start.7 = (s32[32,4,128]{2,1,0:T(4,128)S(1)}, s32[32,4,128]{2,1,0:T(4,128)}, u32[]{:S(2)}) copy-start(s32[32,4,128]{2,1,0:T(4,128)} %param.15) | copy-start | bytes 196612
  47.1 6.3 %collective-permute-start.5 = (f32[2,64,128]{2,1,0:T(8,128)S(1)}, f32[2,64,128]{2,1,0:T(8,128)S(1)}, u32[]{:S(2)}, u32[]{:S(2)}) collective-permute-start(f32[2,64,128]{2,1,0:T(8,128)S(1)} %get-tuple-element.28), channel_id=1, source_target_pairs={{1,0},{3,2},{5,4},{7,6},{9,8},{11,10},{13,12},{15,14},{17,16},{19,... | collective-permute-start | bytes 196616 | tf_op jit(solution)/shard_map/ppermute | solution.py:374
  48.4 5.0 %copy-start.1 = (f32[64,8,8,128]{3,2,1,0:T(8,128)S(1)}, f32[64,8,8,128]{3,2,1,0:T(8,128)}, u32[]{:S(2)}) copy-start(f32[64,8,8,128]{3,2,1,0:T(8,128)} %get-tuple-element.25.refs_2_) | copy-start | bytes 6291460

commit v4 on v3

--- a/solution.py
+++ b/solution.py
@@ -17,8 +17,12 @@
     return value if shift == 0 else pltpu.roll(value, shift, 1)
 
 
+def lane_of(at):
+    return 2 * (at % (LANES // 2)) + at // (LANES // 2)
+
+
 def pack_y_kernel(nx, field_ref, cour_ref, right_ref, left_ref):
-    _, rows, _ = field_ref.shape
+    bins, rows, _ = field_ref.shape
     per_bin = rows // SUB
     blocks = rows // (SUB * nx)
     lane = lax.broadcasted_iota(jnp.int32, (SUB, LANES), 1)
@@ -26,30 +30,27 @@
     def one(load, offset, packed):
         for x in range(nx):
             for q in range(blocks):
-                at = offset + x * blocks + q
+                at = lane_of(offset + x * blocks + q)
+                under = (at - 1) % LANES
                 value = load(pl.ds(q * SUB * nx + x, SUB, stride=nx))
-                hit = lane == at
                 packed = (
-                    jnp.where(hit, roll_to(value, LANES - 1, at), packed[0]),
-                    jnp.where(hit, roll_to(value, 0, at), packed[1]),
+                    jnp.where(lane == at, roll_to(value, LANES - 1, at), packed[0]),
+                    jnp.where(lane == under, roll_to(value, 0, under), packed[1]),
                 )
         return packed
 
     zero = jnp.zeros((SUB, LANES), jnp.float32)
-    step = pl.program_id(0)
-    final = pl.num_programs(0) - 1
-
-    @pl.when(step < final)
-    def _():
+
+    def group(g, _):
         packed = (zero, zero)
         for k in range(GROUP):
-            packed = one(lambda r: field_ref[k, r, :], k * per_bin, packed)
-        right_ref[0] = packed[0]
-        left_ref[0] = packed[1]
-
-    @pl.when(step == final)
-    def _():
-        right_ref[0] = one(lambda r: cour_ref[r, :], 0, (zero, zero))[0]
+            packed = one(lambda r: field_ref[g * GROUP + k, r, :], k * per_bin, packed)
+        right_ref[g] = packed[0]
+        left_ref[g] = packed[1]
+        return 0
+
+    lax.fori_loop(0, bins // GROUP, group, 0)
+    right_ref[bins // GROUP] = one(lambda r: cour_ref[r, :], 0, (zero, zero))[0]
 
 
 def scan_levels(value, table, b):
@@ -66,61 +67,61 @@
     per_bin = nx * blocks
     lane = lax.broadcasted_iota(jnp.int32, (SUB, LANES), 1)
     first, last = lane == 0, lane == LANES - 1
-    places = [
-        (x, xi, outs[2 * n], outs[2 * n + 1]) for n, xs in enumerate(sets) for xi, x in enumerate(xs)
-    ]
-    for x, xi, out, bottom in places:
-        for q in reversed(range(blocks)):
-            span = lambda xx: pl.ds(q * SUB * nx + xx, SUB, stride=nx)
-            spot = x * blocks + q
-            c_here = cx[span(x), :]
-            y_here = cy[span(x), :]
-            y_left = jnp.where(
-                first, roll_to(yl[bins // GROUP], spot, 0), pltpu.roll(y_here, 1, 1)
-            )
-            stay = (
+    even = lane % 2 == 0
+    place = {x: (n, xi) for n, xs in enumerate(sets) for xi, x in enumerate(xs)}
+    half = GROUP // 2
+    for q in reversed(range(blocks)):
+        spans = [pl.ds(q * SUB * nx + x, SUB, stride=nx) for x in range(nx)]
+        c_all = [cx[spans[x], :] for x in range(nx)]
+        stay, from_up, from_down = [], [], []
+        for x in range(nx):
+            y_here = cy[spans[x], :]
+            edge = roll_to(yl[bins // GROUP], lane_of(x * blocks + q), 0)
+            y_left = jnp.where(first, edge, pltpu.roll(y_here, 1, 1))
+            kept = (
                 1.0
-                - jnp.maximum(c_here, 0.0)
+                - jnp.maximum(c_all[x], 0.0)
                 - jnp.maximum(y_here, 0.0)
                 + jnp.minimum(y_left, 0.0)
             )
             if x > 0:
-                c_left = cx[span(x - 1), :]
-                stay = stay + jnp.minimum(c_left, 0.0)
-                from_left = jnp.maximum(c_left, 0.0)
-            from_right = -jnp.minimum(c_here, 0.0)
-            from_up = -jnp.minimum(y_here, 0.0)
-            from_down = jnp.maximum(y_left, 0.0)
-
-            def group(g, _):
-                down_pack = yl[g]
-                up_pack = yr[g]
+                kept = kept + jnp.minimum(c_all[x - 1], 0.0)
+            stay.append(kept)
+            from_up.append(-jnp.minimum(y_here, 0.0))
+            from_down.append(jnp.maximum(y_left, 0.0))
+        enters = [jnp.maximum(c, 0.0) for c in c_all]
+        backs = [-jnp.minimum(c, 0.0) for c in c_all]
+
+        def group(g, _):
+            packs = (jnp.where(even, yl[g], yr[g]), jnp.where(even, yr[g], yl[g]))
+            for part in range(2):
                 falls = []
-                for k in range(GROUP):
+                for k in range(part * half, (part + 1) * half):
                     b = g * GROUP + k
-                    here = field[b, span(x), :]
-                    at = k * per_bin + spot
-                    down = jnp.where(first, roll_to(down_pack, at, 0), pltpu.roll(here, 1, 1))
-                    up = jnp.where(
-                        last, roll_to(up_pack, at, LANES - 1), pltpu.roll(here, LANES - 1, 1)
-                    )
-                    moved = stay * here + from_up * up + from_down * down
-                    if x > 0:
-                        moved = moved + from_left * field[b, span(x - 1), :]
-                    if x < nx - 1:
-                        moved = moved + from_right * field[b, span(x + 1), :]
-                    fall = scan_levels(moved * scal[b], table, b)
-                    if q < blocks - 1:
-                        fall = fall + table[b, 3] * out[b, xi * blocks + q + 1, pl.ds(0, 1), :]
-                    falls.append(fall)
-                for k in range(GROUP):
-                    b = g * GROUP + k
-                    out[b, xi * blocks + q] = falls[k]
+                    row = [field[b, spans[x], :] for x in range(nx)]
+                    for x in range(nx):
+                        n, xi = place[x]
+                        at = k * per_bin + x * blocks + q
+                        halo = roll_to(packs[at // (LANES // 2)], lane_of(at), 0)
+                        down = jnp.where(first, halo, pltpu.roll(row[x], 1, 1))
+                        up = jnp.where(last, halo, pltpu.roll(row[x], LANES - 1, 1))
+                        moved = stay[x] * row[x] + from_up[x] * up + from_down[x] * down
+                        if x > 0:
+                            moved = moved + enters[x - 1] * row[x - 1]
+                        if x < nx - 1:
+                            moved = moved + backs[x] * row[x + 1]
+                        fall = scan_levels(moved * scal[b], table, b)
+                        if q < blocks - 1:
+                            above = outs[2 * n][b, xi * blocks + q + 1, pl.ds(0, 1), :]
+                            fall = fall + table[b, 3] * above
+                        falls.append((n, xi, b, fall))
+                for n, xi, b, fall in falls:
+                    outs[2 * n][b, xi * blocks + q] = fall
                     if q == 0:
-                        bottom[xi, pl.ds(b, 1), :] = falls[k][0:1, :]
-                return 0
-
-            lax.fori_loop(0, bins // GROUP, group, 0)
+                        outs[2 * n + 1][xi, pl.ds(b, 1), :] = fall[0:1, :]
+            return 0
+
+        lax.fori_loop(0, bins // GROUP, group, 0)
 
 
 def edge_kernel(nx, *refs):
@@ -267,7 +268,7 @@
 
 VMEM = pl.BlockSpec(memory_space=pltpu.VMEM)
 SMEM = pl.BlockSpec(memory_space=pltpu.SMEM)
-PARAMS = pltpu.CompilerParams(vmem_limit_bytes=48 * 1024 * 1024)
+PARAMS = pltpu.CompilerParams(vmem_limit_bytes=24 * 1024 * 1024)
 
 
 def cost(flops, bytes_accessed):
@@ -310,28 +311,21 @@
     to_right, to_left = field[:, :, nx - 1, :], field[:, :, 0, :]
     x_left = shift_up(to_right, "gx")
     x_right = shift_down(to_left, "gx")
-    flat_y, cx_last, to_right, to_left = lax.optimization_barrier((flat, courant_x, to_right, to_left))
+    cy, cx_last, to_right, to_left = lax.optimization_barrier((cy, courant_x, to_right, to_left))
     cx_left = shift_up(cx_last[:, nx - 1, :], "gx")
 
     y_to_right, y_to_left = pl.pallas_call(
         functools.partial(pack_y_kernel, nx),
-        grid=(groups + 1,),
         out_shape=(
             jax.ShapeDtypeStruct((groups + 1, SUB, LANES), f32),
             jax.ShapeDtypeStruct((groups, SUB, LANES), f32),
         ),
-        in_specs=[
-            pl.BlockSpec((GROUP, depth * nx, ny), lambda g: (jnp.minimum(g, groups - 1), 0, 0)),
-            pl.BlockSpec((depth * nx, ny), lambda g: (0, 0)),
-        ],
-        out_specs=(
-            pl.BlockSpec((1, SUB, LANES), lambda g: (g, 0, 0)),
-            pl.BlockSpec((1, SUB, LANES), lambda g: (jnp.minimum(g, groups - 1), 0, 0)),
-        ),
+        in_specs=[VMEM, VMEM],
+        out_specs=(VMEM, VMEM),
         compiler_params=PARAMS,
         cost_estimate=cost(1 << 22, 1 << 22),
         name="pack_y",
-    )(flat_y, cy)
+    )(flat, cy)
     y_left = shift_up(y_to_right, "gy")
     y_right = shift_down(y_to_left, "gy")
 
@@ -403,7 +397,7 @@
         compiler_params=PARAMS,
         cost_estimate=cost(1 << 24, 16 << 20),
         name="settle_all",
-    )(scal, flat_y, cx, cy, y_left, y_right, table)
+    )(scal, flat, cx, cy, y_left, y_right, table)
     inner_carry = inflow(bottom)
     edge_settled, edge_bottom = pl.pallas_call(
         functools.partial(edge_kernel, nx),

time: 61.1 us -> 49.5 us (0.81)
  the two profiles are of different devices: /device:TPU:3 before, /device:TPU:6 now
where the time goes in v4:
time: 49.5 us; the launch traced here: 49.2 us
  Pallas kernels  24 us (48%)
  local copies, waits for them, and re-layouts  11.8 us (24%)
  starting transfers between devices  10.7 us (22%)
  waiting for transfers between devices  1.33 us (3%)
  other arithmetic  1.08 us (2%)
    pallas_call x2, Pallas kernels, micro_part(): pl.pallas_call(functools.partial(micro_kernel, nx, xs, slots, bool(inner)...  12.4 us
    pallas_call x1, Pallas kernels, shards(): pl.pallas_call(functools.partial(settle_kernel, nx, (inner_x, edge_x)), o...  7.03 us
    slice x1, local copies, waits for them, and re-layouts, shards(): to_right, to_left = (field[:, :, nx - 1, :], field[:, :, 0, :])  6.85 us
    ppermute x2, starting transfers between devices, inflow(): carry = lax.ppermute(sent, 'gz', [(i + 1, i) for i in range(count - 1)])  5.05 us
    ppermute x2, starting transfers between devices, shift_down(): lax.ppermute(value, axis, [((i + 1) % count, i) for i in range(count)])  3.99 us
    unnamed x30, local copies, waits for them, and re-layouts  3.32 us
    pallas_call x1, Pallas kernels, shards(): pl.pallas_call(functools.partial(pack_y_kernel, nx), out_shape=(jax.Shape...  2.76 us
    pallas_call x1, Pallas kernels, shards(): pl.pallas_call(functools.partial(edge_kernel, nx), out_shape=settle_shape...  1.79 us
  transfers between devices with their start and end apart: 7, of which 2 were waited for; matrix products, arithmetic and copies ran while one was open for 6% of the time, Pallas kernels for 34%

profile of v4, /device:TPU:6, one launch (start us, length us, event | category | flops | bytes accessed | tf_op | source)
XLA Modules:
  0.0 49.2 jit_solution(1857510294733956677)
XLA Ops:
  0.0 0.0 copy-start
  0.0 6.8 %fusion.1 = (f32[64,32,1,128]{3,2,1,0:T(1,128)S(1)}, f32[64,32,1,128]{3,2,1,0:T(1,128)}) fusion(f32[64,32,4,128]{3,2,1,0:T(4,128)} %param.11), kind=kLoop, calls=%fused_computation.17 | loop fusion | bytes 4194304 | tf_op jit(solution)/shard_map/slice | solution.py:311
  6.8 0.0 collective-permute-start.3
  6.9 1.7 %collective-permute-start.4 = (f32[64,32,128]{2,1,0:T(8,128)S(1)}, f32[64,32,128]{2,1,0:T(8,128)S(1)}, u32[]{:S(2)}, u32[]{:S(2)}) collective-permute-start(f32[64,32,128]{2,1,0:T(8,128)S(1)} %bitcast.18), channel_id=1, source_target_pairs={{8,0},{16,8},{24,16},{0,24},{9,1},{17,9},{25,17},{1,25},{10,2},{18... | collective-permute-start | bytes 3145736 | tf_op jit(solution)/shard_map/ppermute | solution.py:285
  8.6 0.0 copy-done
  8.6 0.0 copy-start.3
  8.6 0.8 %copy-done.3 = f32[32,4,128]{2,1,0:T(4,128)S(1)} copy-done((f32[32,4,128]{2,1,0:T(4,128)S(1)}, f32[32,4,128]{2,1,0:T(4,128)}, u32[]{:S(2)}) %copy-start.3) | copy-done | bytes 65560
  9.4 0.0 copy-start.2
  9.4 0.0 copy-start.7
  9.4 0.0 copy-start.12
  9.4 0.0 copy-start.8
  9.4 0.0 copy-start.9
  9.5 0.0 copy-start.10
  9.5 0.0 copy-start.11
  9.5 0.0 copy-start.4
  9.5 2.8 %pack_y.1 = (f32[9,8,128]{2,1,0:T(8,128)S(1)}, f32[8,8,128]{2,1,0:T(8,128)S(1)}) custom-call(f32[64,128,128]{2,1,0:T(8,128)S(1)} %bitcast.16, f32[128,128]{1,0:T(8,128)S(1)} %bitcast.22), custom_call_target="tpu_custom_call" | custom-call | flops 4194304 | bytes 4194304 | tf_op jit(solution)/shard_map/pack_y/pallas_call | solution.py:317
  12.3 1.6 %collective-permute-start = (f32[9,8,128]{2,1,0:T(8,128)S(1)}, f32[9,8,128]{2,1,0:T(8,128)S(1)}, u32[]{:S(2)}, u32[]{:S(2)}) collective-permute-start(f32[9,8,128]{2,1,0:T(8,128)S(1)} %get-tuple-element.19), channel_id=1, source_target_pairs={{0,2},{2,4},{4,6},{6,0},{1,3},{3,5},{5,7},{7,1},{8,10},{10,12},{12... | collective-permute-start | bytes 110600 | tf_op jit(solution)/shard_map/ppermute | solution.py:280
  13.9 2.2 %collective-permute-start.1 = (f32[8,8,128]{2,1,0:T(8,128)S(1)}, f32[8,8,128]{2,1,0:T(8,128)S(1)}, u32[]{:S(2)}, u32[]{:S(2)}) collective-permute-start(f32[8,8,128]{2,1,0:T(8,128)S(1)} %get-tuple-element.20), channel_id=1, source_target_pairs={{2,0},{4,2},{6,4},{0,6},{3,1},{5,3},{7,5},{1,7},{10,8},{12,10},{14... | collective-permute-start | bytes 98312 | tf_op jit(solution)/shard_map/ppermute | solution.py:285
  16.1 0.0 copy-done.2
  16.2 0.1 collective-permute-start.2
  16.3 0.1 pad_maximum_fusion.1
  16.4 0.0 copy-done.7
  16.4 0.1 copy.16
  16.5 0.1 reshape.80
  16.6 0.0 copy-done.12
  16.6 0.1 pad_maximum_fusion
  16.7 0.1 multiply_exponential_fusion
  16.8 0.8 %exponential_select_fusion = f32[64,4,8]{2,1,0:T(4,128)} fusion(f32[4,8]{1,0:T(4,128)S(1)} %pad_maximum_fusion, f32[64]{0:T(128)S(1)} %get-tuple-element.33, pred[4,8]{1,0:T(4,128)(4,1)S(1)} %pad_add_fusion), kind=kLoop, calls=%fused_computation | loop fusion | flops 4096 | bytes 8608 | tf_op jit(solution)/shard_map/jit(_where)/select_n | solution.py:337
  17.6 0.1 exp.15
  17.6 0.0 copy-done.8
  17.6 0.1 copy.15
  17.7 0.1 reshape.79
  17.8 0.0 copy-done.9
  17.8 0.1 copy.17
  17.9 0.1 reshape.81
  18.0 0.0 copy-done.10
  18.0 0.0 copy-done.11
  18.0 0.1 concatenate.6.refs_0_
  18.1 0.1 collective-permute-done.1.refs_5_
  18.2 0.0 collective-permute-done.refs_4_
  18.2 1.2 %broadcast_in_dim.20.refs_6_.refs_4_ = f32[64,4,8,128]{3,2,1,0:T(8,128)S(1)} broadcast(f32[64,4,8]{2,1,0:T(4,128)} %exponential_select_fusion), dimensions={0,1,2} | broadcast | bytes 1056768 | tf_op jit(solution)/shard_map/broadcast_in_dim | solution.py:338
  19.4 0.0 copy-done.4
  19.5 0.0 copy-start.1
  19.5 2.2 %copy-done.1 = f32[64,32,4,128]{3,2,1,0:T(4,128)S(1)} copy-done((f32[64,32,4,128]{3,2,1,0:T(4,128)S(1)}, f32[64,32,4,128]{3,2,1,0:T(4,128)}, u32[]{:S(2)}) %copy-start.1) | copy-done | bytes 4194328
  21.6 7.0 %settle_all.1 = (f32[64,8,8,128]{3,2,1,0:T(8,128)S(1)}, f32[2,64,128]{2,1,0:T(8,128)S(1)}, f32[64,8,8,128]{3,2,1,0:T(8,128)S(1)}, f32[2,64,128]{2,1,0:T(8,128)S(1)}) custom-call(f32[768]{0:T(1024)S(1)} %concatenate.6.refs_0_, f32[64,128,128]{2,1,0:T(8,128)S(1)} %bitcast.17, f32[128,128]{1,0:T(8,128)S(1)} %bitcast.20, f32[128,128]{1,0:T(8,128)S(1)} %bitcast.23, ...), custom_call_target="tpu_custom_call" | custom-call | flops 16777216 | bytes 16777216 | tf_op jit(solution)/shard_map/settle_all/pallas_call | solution.py:392
  28.7 2.4 %collective-permute-start.6 = (f32[2,64,128]{2,1,0:T(8,128)S(1)}, f32[2,64,128]{2,1,0:T(8,128)S(1)}, u32[]{:S(2)}, u32[]{:S(2)}) collective-permute-start(f32[2,64,128]{2,1,0:T(8,128)S(1)} %get-tuple-element.30), channel_id=1, source_target_pairs={{1,0},{3,2},{5,4},{7,6},{9,8},{11,10},{13,12},{15,14},{17,16},{19,... | collective-permute-start | bytes 196616 | tf_op jit(solution)/shard_map/ppermute | solution.py:368
  31.1 1.2 %collective-permute-done.2.refs_5_ = f32[32,128]{1,0:T(8,128)S(1)} collective-permute-done((f32[32,128]{1,0:T(8,128)S(1)}, f32[32,128]{1,0:T(8,128)S(1)}, u32[]{:S(2)}, u32[]{:S(2)}) %collective-permute-start.2) | collective-permute-done | bytes 16416 | tf_op jit(solution)/shard_map/ppermute | solution.py:280
  32.3 0.0 collective-permute-done.3.refs_7_
  32.3 0.0 collective-permute-done.4.refs_8_
  32.3 0.0 copy-start.5
  32.3 0.0 copy-start.6
  32.4 1.8 %settle_edge.1 = (f32[64,8,8,128]{3,2,1,0:T(8,128)S(1)}, f32[2,64,128]{2,1,0:T(8,128)S(1)}) custom-call(f32[768]{0:T(1024)S(1)} %concatenate.6.refs_0_, f32[64,8,8,128]{3,2,1,0:T(8,128)S(1)} %get-tuple-element.21.refs_1_, f32[2,64,128]{2,1,0:T(8,128)S(1)} %get-tuple-element.22.refs_2_, f32[128,128]{1,0:T(8,128)S(1)} %bitcast.21, ...), custom_call_target="tpu_custom_call" | custom-call | flops 8388608 | bytes 8388608 | tf_op jit(solution)/shard_map/settle_edge/pallas_call | solution.py:402
  34.2 2.6 %collective-permute-start.5 = (f32[2,64,128]{2,1,0:T(8,128)S(1)}, f32[2,64,128]{2,1,0:T(8,128)S(1)}, u32[]{:S(2)}, u32[]{:S(2)}) collective-permute-start(f32[2,64,128]{2,1,0:T(8,128)S(1)} %get-tuple-element.28), channel_id=1, source_target_pairs={{1,0},{3,2},{5,4},{7,6},{9,8},{11,10},{13,12},{15,14},{17,16},{19,... | collective-permute-start | bytes 196616 | tf_op jit(solution)/shard_map/ppermute | solution.py:368
  36.8 0.0 collective-permute-done.6.refs_3_
  36.8 0.0 copy-done.5
  36.8 0.0 copy-done.6
  36.8 4.9 %micro_inner.1.refs_7_ = f32[64,8,8,128]{3,2,1,0:T(8,128)S(1)} custom-call(f32[768]{0:T(1024)S(1)} %concatenate.6.refs_0_, s32[768]{0:T(1024)S(1)} %constant_dynamic-update-slice_fusion.refs_1_, f32[64,8,8,128]{3,2,1,0:T(8,128)S(1)} %get-tuple-element.29.refs_2_, f32[2,64,128]{2,1,0:T(8,128)S(1)} %collective-permute-done.6.refs_3_, ...), custom_call_target="tpu_custom_call" | custom-call | flops 16777216 | bytes 8388608 | tf_op jit(solution)/shard_map/micro_inner/pallas_call | solution.py:378
  41.7 0.0 collective-permute-done.5.refs_3_
  41.8 7.5 %micro_edge.1 = f32[64,128,128]{2,1,0:T(8,128)} custom-call(f32[768]{0:T(1024)S(1)} %concatenate.6.refs_0_, s32[768]{0:T(1024)S(1)} %constant_dynamic-update-slice_fusion.refs_1_, f32[64,8,8,128]{3,2,1,0:T(8,128)S(1)} %get-tuple-element.25.refs_2_, f32[2,64,128]{2,1,0:T(8,128)S(1)} %collective-permute-done.5.refs_3_, ...), custom_call_target="tpu_custom_call" | custom-call | flops 16777216 | bytes 8388608 | tf_op jit(solution)/shard_map/micro_edge/pallas_call | solution.py:378
  (12 shorter events, 0.1 us)
Async XLA Ops:
  0.0 8.6 %copy-start = (f32[64,32,4,128]{3,2,1,0:T(4,128)S(1)}, f32[64,32,4,128]{3,2,1,0:T(4,128)}, u32[]{:S(2)}) copy-start(f32[64,32,4,128]{3,2,1,0:T(4,128)} %param.11) | copy-start | bytes 12582916
  6.8 25.5 %collective-permute-start.3 = (f32[64,32,128]{2,1,0:T(8,128)}, f32[64,32,128]{2,1,0:T(8,128)S(1)}, u32[]{:S(2)}, u32[]{:S(2)}) collective-permute-start(f32[64,32,128]{2,1,0:T(8,128)} %bitcast.3), channel_id=1, source_target_pairs={{0,8},{8,16},{16,24},{24,0},{1,9},{9,17},{17,25},{25,1},{2,10},{10... | collective-permute-start | bytes 3145736 | tf_op jit(solution)/shard_map/ppermute | solution.py:280
  6.9 25.5 %collective-permute-start.4 = (f32[64,32,128]{2,1,0:T(8,128)S(1)}, f32[64,32,128]{2,1,0:T(8,128)S(1)}, u32[]{:S(2)}, u32[]{:S(2)}) collective-permute-start(f32[64,32,128]{2,1,0:T(8,128)S(1)} %bitcast.18), channel_id=1, source_target_pairs={{8,0},{16,8},{24,16},{0,24},{9,1},{17,9},{25,17},{1,25},{10,2},{18... | collective-permute-start | bytes 3145736 | tf_op jit(solution)/shard_map/ppermute | solution.py:285
  8.6 0.8 %copy-start.3 = (f32[32,4,128]{2,1,0:T(4,128)S(1)}, f32[32,4,128]{2,1,0:T(4,128)}, u32[]{:S(2)}) copy-start(f32[32,4,128]{2,1,0:T(4,128)} %param.13) | copy-start | bytes 196612
  9.4 6.7 %copy-start.2 = (f32[32,4,128]{2,1,0:T(4,128)S(1)}, f32[32,4,128]{2,1,0:T(4,128)}, u32[]{:S(2)}) copy-start(f32[32,4,128]{2,1,0:T(4,128)} %param.12) | copy-start | bytes 196612
  9.4 6.9 %copy-start.7 = (s32[48,8]{0,1:T(8,128)S(1)}, s32[48,8]{0,1:T(8,128)}, u32[]{:S(2)}) copy-start(s32[48,8]{0,1:T(8,128)} %param.20) | copy-start | bytes 4612
  9.4 7.1 %copy-start.12 = (f32[64]{0:T(128)S(1)}, f32[64]{0:T(128)}, u32[]{:S(2)}) copy-start(f32[64]{0:T(128)} %param.16) | copy-start | bytes 772
  9.4 8.2 %copy-start.8 = (f32[48,8]{0,1:T(8,128)S(1)}, f32[48,8]{0,1:T(8,128)}, u32[]{:S(2)}) copy-start(f32[48,8]{0,1:T(8,128)} %param.19) | copy-start | bytes 4612
  9.4 8.4 %copy-start.9 = (s32[48,8]{0,1:T(8,128)S(1)}, s32[48,8]{0,1:T(8,128)}, u32[]{:S(2)}) copy-start(s32[48,8]{0,1:T(8,128)} %param.21) | copy-start | bytes 4612
  9.5 8.5 %copy-start.10 = (f32[47]{0:T(128)S(1)}, f32[47]{0:T(128)}, u32[]{:S(2)}) copy-start(f32[47]{0:T(128)} %param.17) | copy-start | bytes 568
  9.5 8.5 %copy-start.11 = (f32[16]{0:T(128)S(1)}, f32[16]{0:T(128)}, u32[]{:S(2)}) copy-start(f32[16]{0:T(128)} %param.18) | copy-start | bytes 196
  9.5 10.0 %copy-start.4 = (f32[32,4,128]{2,1,0:T(4,128)S(1)}, f32[32,4,128]{2,1,0:T(4,128)}, u32[]{:S(2)}) copy-start(f32[32,4,128]{2,1,0:T(4,128)} %param.13) | copy-start | bytes 196612
  12.3 5.9 %collective-permute-start = (f32[9,8,128]{2,1,0:T(8,128)S(1)}, f32[9,8,128]{2,1,0:T(8,128)S(1)}, u32[]{:S(2)}, u32[]{:S(2)}) collective-permute-start(f32[9,8,128]{2,1,0:T(8,128)S(1)} %get-tuple-element.19), channel_id=1, source_target_pairs={{0,2},{2,4},{4,6},{6,0},{1,3},{3,5},{5,7},{7,1},{8,10},{10,12},{12... | collective-permute-start | bytes 110600 | tf_op jit(solution)/shard_map/ppermute | solution.py:280
  13.9 4.3 %collective-permute-start.1 = (f32[8,8,128]{2,1,0:T(8,128)S(1)}, f32[8,8,128]{2,1,0:T(8,128)S(1)}, u32[]{:S(2)}, u32[]{:S(2)}) collective-permute-start(f32[8,8,128]{2,1,0:T(8,128)S(1)} %get-tuple-element.20), channel_id=1, source_target_pairs={{2,0},{4,2},{6,4},{0,6},{3,1},{5,3},{7,5},{1,7},{10,8},{12,10},{14... | collective-permute-start | bytes 98312 | tf_op jit(solution)/shard_map/ppermute | solution.py:285
  16.2 16.2 %collective-permute-start.2 = (f32[32,128]{1,0:T(8,128)S(1)}, f32[32,128]{1,0:T(8,128)S(1)}, u32[]{:S(2)}, u32[]{:S(2)}) collective-permute-start(f32[32,128]{1,0:T(8,128)S(1)} %slice_bitcast_fusion), channel_id=1, source_target_pairs={{0,8},{8,16},{16,24},{24,0},{1,9},{9,17},{17,25},{25,1},{2,10},{10... | collective-permute-start | bytes 49160 | tf_op jit(solution)/shard_map/ppermute | solution.py:280
  19.5 2.2 %copy-start.1 = (f32[64,32,4,128]{3,2,1,0:T(4,128)S(1)}, f32[64,32,4,128]{3,2,1,0:T(4,128)}, u32[]{:S(2)}) copy-start(f32[64,32,4,128]{3,2,1,0:T(4,128)} %param.11) | copy-start | bytes 12582916
  28.7 8.1 %collective-permute-start.6 = (f32[2,64,128]{2,1,0:T(8,128)S(1)}, f32[2,64,128]{2,1,0:T(8,128)S(1)}, u32[]{:S(2)}, u32[]{:S(2)}) collective-permute-start(f32[2,64,128]{2,1,0:T(8,128)S(1)} %get-tuple-element.30), channel_id=1, source_target_pairs={{1,0},{3,2},{5,4},{7,6},{9,8},{11,10},{13,12},{15,14},{17,16},{19,... | collective-permute-start | bytes 196616 | tf_op jit(solution)/shard_map/ppermute | solution.py:368
  32.3 4.5 %copy-start.5 = (f32[32,4,128]{2,1,0:T(4,128)S(1)}, f32[32,4,128]{2,1,0:T(4,128)}, u32[]{:S(2)}) copy-start(f32[32,4,128]{2,1,0:T(4,128)} %param.14) | copy-start | bytes 196612
  32.3 4.5 %copy-start.6 = (s32[32,4,128]{2,1,0:T(4,128)S(1)}, s32[32,4,128]{2,1,0:T(4,128)}, u32[]{:S(2)}) copy-start(s32[32,4,128]{2,1,0:T(4,128)} %param.15) | copy-start | bytes 196612
  34.2 7.6 %collective-permute-start.5 = (f32[2,64,128]{2,1,0:T(8,128)S(1)}, f32[2,64,128]{2,1,0:T(8,128)S(1)}, u32[]{:S(2)}, u32[]{:S(2)}) collective-permute-start(f32[2,64,128]{2,1,0:T(8,128)S(1)} %get-tuple-element.28), channel_id=1, source_target_pairs={{1,0},{3,2},{5,4},{7,6},{9,8},{11,10},{13,12},{15,14},{17,16},{19,... | collective-permute-start | bytes 196616 | tf_op jit(solution)/shard_map/ppermute | solution.py:368

commit v5 on v4

--- a/solution.py
+++ b/solution.py
@@ -19,6 +19,22 @@
 
 def lane_of(at):
     return 2 * (at % (LANES // 2)) + at // (LANES // 2)
+
+
+def pack_x_kernel(nx, field_ref, right_ref, left_ref):
+    bins, rows, _ = field_ref.shape
+
+    def group(g, _):
+        for k in range(GROUP):
+            b = g * GROUP + k
+            for q in range(rows // (SUB * nx)):
+                start = q * SUB * nx
+                zrows = pl.ds(q * SUB, SUB)
+                right_ref[b, zrows, :] = field_ref[b, pl.ds(start + nx - 1, SUB, stride=nx), :]
+                left_ref[b, zrows, :] = field_ref[b, pl.ds(start, SUB, stride=nx), :]
+        return 0
+
+    lax.fori_loop(0, bins // GROUP, group, 0)
 
 
 def pack_y_kernel(nx, field_ref, cour_ref, right_ref, left_ref):
@@ -308,7 +324,16 @@
     )
 
     groups = bins // GROUP
-    to_right, to_left = field[:, :, nx - 1, :], field[:, :, 0, :]
+    face = jax.ShapeDtypeStruct((bins, depth, ny), f32)
+    to_right, to_left = pl.pallas_call(
+        functools.partial(pack_x_kernel, nx),
+        out_shape=(face, face),
+        in_specs=[VMEM],
+        out_specs=(VMEM, VMEM),
+        compiler_params=PARAMS,
+        cost_estimate=cost(1 << 20, 6 << 20),
+        name="pack_x",
+    )(flat)
     x_left = shift_up(to_right, "gx")
     x_right = shift_down(to_left, "gx")
     cy, cx_last, to_right, to_left = lax.optimization_barrier((cy, courant_x, to_right, to_left))

time: 49.5 us -> 45.9 us (0.927)
  local copies, waits for them, and re-layouts: 11.8 us -> 6.35 us
  Pallas kernels: 24 us -> 25.1 us
  waiting for transfers between devices: 1.33 us -> 2.19 us
    slice x1 -> x0, local copies, waits for them, and re-layouts: 6.85 us -> none  [shards(): to_right, to_left = (field[:, :, nx - 1, :], field[:, :, 0, :])]
    unnamed x30 -> x28, local copies, waits for them, and re-layouts: 3.32 us -> 4.67 us
    pallas_call x0 -> x1, Pallas kernels: none -> 1.13 us  [shards(): pl.pallas_call(functools.partial(pack_x_kernel, nx), out_shape=(face, fac...]
    ppermute x3, waiting for transfers between devices: 1.21 us -> 2.06 us  [shift_up(): lax.ppermute(value, axis, [(i, (i + 1) % count) for i in range(count)])]
  transfers between devices with their start and end apart: 7 -> 7, of which waited for: 2 -> 2; matrix products, arithmetic and copies ran while one was open for 6% -> 7% of each run, Pallas kernels for 34% -> 36%
where the time goes in v5:
time: 45.9 us; the launch traced here: 45.7 us
  Pallas kernels  25.1 us (55%)
  starting transfers between devices  10.7 us (23%)
  local copies, waits for them, and re-layouts  6.35 us (14%)
  waiting for transfers between devices  2.19 us (5%)
  other arithmetic  1.07 us (2%)
    pallas_call x2, Pallas kernels, micro_part(): pl.pallas_call(functools.partial(micro_kernel, nx, xs, slots, bool(inner)...  12.4 us
    pallas_call x1, Pallas kernels, shards(): pl.pallas_call(functools.partial(settle_kernel, nx, (inner_x, edge_x)), o...  7.03 us
    ppermute x2, starting transfers between devices, inflow(): carry = lax.ppermute(sent, 'gz', [(i + 1, i) for i in range(count - 1)])  5.05 us
    unnamed x28, local copies, waits for them, and re-layouts  4.67 us
    ppermute x2, starting transfers between devices, shift_down(): lax.ppermute(value, axis, [((i + 1) % count, i) for i in range(count)])  3.99 us
    pallas_call x1, Pallas kernels, shards(): pl.pallas_call(functools.partial(pack_y_kernel, nx), out_shape=(jax.Shape...  2.76 us
    ppermute x3, waiting for transfers between devices, shift_up(): lax.ppermute(value, axis, [(i, (i + 1) % count) for i in range(count)])  2.06 us
    pallas_call x1, Pallas kernels, shards(): pl.pallas_call(functools.partial(edge_kernel, nx), out_shape=settle_shape...  1.79 us
  transfers between devices with their start and end apart: 7, of which 2 were waited for; matrix products, arithmetic and copies ran while one was open for 7% of the time, Pallas kernels for 36%

profile of v5, /device:TPU:6, one launch (start us, length us, event | category | flops | bytes accessed | tf_op | source)
XLA Modules:
  0.0 45.7 jit_solution(13763823203260217424)
XLA Ops:
  0.0 0.0 copy-start
  0.0 2.2 %copy-done = f32[64,32,4,128]{3,2,1,0:T(4,128)S(1)} copy-done((f32[64,32,4,128]{3,2,1,0:T(4,128)S(1)}, f32[64,32,4,128]{3,2,1,0:T(4,128)}, u32[]{:S(2)}) %copy-start) | copy-done | bytes 4194328
  2.2 0.0 copy-start.3
  2.2 1.1 %pack_x.1 = (f32[64,32,128]{2,1,0:T(8,128)}, f32[64,32,128]{2,1,0:T(8,128)S(1)}) custom-call(f32[64,128,128]{2,1,0:T(8,128)S(1)} %bitcast.10), custom_call_target="tpu_custom_call" | custom-call | flops 1048576 | bytes 6291456 | tf_op jit(solution)/shard_map/pack_x/pallas_call | solution.py:328
  3.3 0.0 collective-permute-start.3
  3.3 1.7 %collective-permute-start.4 = (f32[64,32,128]{2,1,0:T(8,128)S(1)}, f32[64,32,128]{2,1,0:T(8,128)S(1)}, u32[]{:S(2)}, u32[]{:S(2)}) collective-permute-start(f32[64,32,128]{2,1,0:T(8,128)S(1)} %get-tuple-element.28.refs_6_), channel_id=1, source_target_pairs={{8,0},{16,8},{24,16},{0,24},{9,1},{17,9},{25,17},{1,25},{10,2},{18... | collective-permute-start | bytes 3145736 | tf_op jit(solution)/shard_map/ppermute | solution.py:301
  5.1 0.0 copy-done.3
  5.1 0.0 copy-start.2
  5.1 0.0 copy-start.6
  5.1 0.0 copy-start.11
  5.1 0.0 copy-start.7
  5.1 0.0 copy-start.8
  5.1 0.0 copy-start.9
  5.1 0.0 copy-start.10
  5.1 2.8 %pack_y.1 = (f32[9,8,128]{2,1,0:T(8,128)S(1)}, f32[8,8,128]{2,1,0:T(8,128)S(1)}) custom-call(f32[64,128,128]{2,1,0:T(8,128)S(1)} %bitcast.11, f32[128,128]{1,0:T(8,128)S(1)} %bitcast.15), custom_call_target="tpu_custom_call" | custom-call | flops 4194304 | bytes 4194304 | tf_op jit(solution)/shard_map/pack_y/pallas_call | solution.py:342
  7.9 1.6 %collective-permute-start = (f32[9,8,128]{2,1,0:T(8,128)S(1)}, f32[9,8,128]{2,1,0:T(8,128)S(1)}, u32[]{:S(2)}, u32[]{:S(2)}) collective-permute-start(f32[9,8,128]{2,1,0:T(8,128)S(1)} %get-tuple-element.23), channel_id=1, source_target_pairs={{0,2},{2,4},{4,6},{6,0},{1,3},{3,5},{5,7},{7,1},{8,10},{10,12},{12... | collective-permute-start | bytes 110600 | tf_op jit(solution)/shard_map/ppermute | solution.py:296
  9.5 2.2 %collective-permute-start.1 = (f32[8,8,128]{2,1,0:T(8,128)S(1)}, f32[8,8,128]{2,1,0:T(8,128)S(1)}, u32[]{:S(2)}, u32[]{:S(2)}) collective-permute-start(f32[8,8,128]{2,1,0:T(8,128)S(1)} %get-tuple-element.24), channel_id=1, source_target_pairs={{2,0},{4,2},{6,4},{0,6},{3,1},{5,3},{7,5},{1,7},{10,8},{12,10},{14... | collective-permute-start | bytes 98312 | tf_op jit(solution)/shard_map/ppermute | solution.py:301
  11.8 0.0 copy-done.2
  11.8 0.1 collective-permute-start.2
  11.9 0.1 pad_maximum_fusion.1
  12.0 0.0 copy-done.6
  12.0 0.1 copy.14
  12.1 0.1 reshape.80
  12.2 0.0 copy-done.11
  12.2 0.1 pad_maximum_fusion
  12.3 0.1 multiply_exponential_fusion
  12.4 0.8 %exponential_select_fusion = f32[64,4,8]{2,1,0:T(4,128)} fusion(f32[4,8]{1,0:T(4,128)S(1)} %pad_maximum_fusion, f32[64]{0:T(128)S(1)} %get-tuple-element.35, pred[4,8]{1,0:T(4,128)(4,1)S(1)} %pad_add_fusion), kind=kLoop, calls=%fused_computation | loop fusion | flops 4096 | bytes 8608 | tf_op jit(solution)/shard_map/jit(_where)/select_n | solution.py:362
  13.2 0.1 exp.15
  13.3 0.0 copy-done.7
  13.3 0.1 copy.13
  13.3 0.1 reshape.79
  13.4 0.0 copy-done.8
  13.4 0.1 copy.15
  13.5 0.1 reshape.81
  13.6 0.0 copy-done.9
  13.6 0.0 copy-done.10
  13.6 0.1 concatenate.6.refs_0_
  13.7 0.1 collective-permute-done.1.refs_5_
  13.8 0.0 collective-permute-done.refs_4_
  13.8 1.2 %broadcast_in_dim.20.refs_6_.refs_4_ = f32[64,4,8,128]{3,2,1,0:T(8,128)S(1)} broadcast(f32[64,4,8]{2,1,0:T(4,128)} %exponential_select_fusion), dimensions={0,1,2} | broadcast | bytes 1056768 | tf_op jit(solution)/shard_map/broadcast_in_dim | solution.py:363
  15.1 0.0 copy-start.1
  15.1 2.2 %copy-done.1 = f32[64,32,4,128]{3,2,1,0:T(4,128)S(1)} copy-done((f32[64,32,4,128]{3,2,1,0:T(4,128)S(1)}, f32[64,32,4,128]{3,2,1,0:T(4,128)}, u32[]{:S(2)}) %copy-start.1) | copy-done | bytes 4194328
  17.3 7.0 %settle_all.1 = (f32[64,8,8,128]{3,2,1,0:T(8,128)S(1)}, f32[2,64,128]{2,1,0:T(8,128)S(1)}, f32[64,8,8,128]{3,2,1,0:T(8,128)S(1)}, f32[2,64,128]{2,1,0:T(8,128)S(1)}) custom-call(f32[768]{0:T(1024)S(1)} %concatenate.6.refs_0_, f32[64,128,128]{2,1,0:T(8,128)S(1)} %bitcast.12, f32[128,128]{1,0:T(8,128)S(1)} %bitcast.13, f32[128,128]{1,0:T(8,128)S(1)} %bitcast.16, ...), custom_call_target="tpu_custom_call" | custom-call | flops 16777216 | bytes 16777216 | tf_op jit(solution)/shard_map/settle_all/pallas_call | solution.py:417
  24.3 2.4 %collective-permute-start.6 = (f32[2,64,128]{2,1,0:T(8,128)S(1)}, f32[2,64,128]{2,1,0:T(8,128)S(1)}, u32[]{:S(2)}, u32[]{:S(2)}) collective-permute-start(f32[2,64,128]{2,1,0:T(8,128)S(1)} %get-tuple-element.34), channel_id=1, source_target_pairs={{1,0},{3,2},{5,4},{7,6},{9,8},{11,10},{13,12},{15,14},{17,16},{19,... | collective-permute-start | bytes 196616 | tf_op jit(solution)/shard_map/ppermute | solution.py:393
  26.8 2.1 %collective-permute-done.2.refs_5_ = f32[32,128]{1,0:T(8,128)S(1)} collective-permute-done((f32[32,128]{1,0:T(8,128)S(1)}, f32[32,128]{1,0:T(8,128)S(1)}, u32[]{:S(2)}, u32[]{:S(2)}) %collective-permute-start.2) | collective-permute-done | bytes 16416 | tf_op jit(solution)/shard_map/ppermute | solution.py:296
  28.8 0.0 collective-permute-done.3.refs_7_
  28.8 0.0 collective-permute-done.4.refs_8_
  28.8 0.0 copy-start.4
  28.8 0.0 copy-start.5
  28.8 1.8 %settle_edge.1 = (f32[64,8,8,128]{3,2,1,0:T(8,128)S(1)}, f32[2,64,128]{2,1,0:T(8,128)S(1)}) custom-call(f32[768]{0:T(1024)S(1)} %concatenate.6.refs_0_, f32[64,8,8,128]{3,2,1,0:T(8,128)S(1)} %get-tuple-element.25.refs_1_, f32[2,64,128]{2,1,0:T(8,128)S(1)} %get-tuple-element.26.refs_2_, f32[128,128]{1,0:T(8,128)S(1)} %bitcast.14, ...), custom_call_target="tpu_custom_call" | custom-call | flops 8388608 | bytes 8388608 | tf_op jit(solution)/shard_map/settle_edge/pallas_call | solution.py:427
  30.6 2.6 %collective-permute-start.5 = (f32[2,64,128]{2,1,0:T(8,128)S(1)}, f32[2,64,128]{2,1,0:T(8,128)S(1)}, u32[]{:S(2)}, u32[]{:S(2)}) collective-permute-start(f32[2,64,128]{2,1,0:T(8,128)S(1)} %get-tuple-element.32), channel_id=1, source_target_pairs={{1,0},{3,2},{5,4},{7,6},{9,8},{11,10},{13,12},{15,14},{17,16},{19,... | collective-permute-start | bytes 196616 | tf_op jit(solution)/shard_map/ppermute | solution.py:393
  33.3 0.0 collective-permute-done.6.refs_3_
  33.3 0.0 copy-done.4
  33.3 0.0 copy-done.5
  33.3 4.9 %micro_inner.1.refs_7_ = f32[64,8,8,128]{3,2,1,0:T(8,128)S(1)} custom-call(f32[768]{0:T(1024)S(1)} %concatenate.6.refs_0_, s32[768]{0:T(1024)S(1)} %constant_dynamic-update-slice_fusion.refs_1_, f32[64,8,8,128]{3,2,1,0:T(8,128)S(1)} %get-tuple-element.33.refs_2_, f32[2,64,128]{2,1,0:T(8,128)S(1)} %collective-permute-done.6.refs_3_, ...), custom_call_target="tpu_custom_call" | custom-call | flops 16777216 | bytes 8388608 | tf_op jit(solution)/shard_map/micro_inner/pallas_call | solution.py:403
  38.2 0.0 collective-permute-done.5.refs_3_
  38.2 7.5 %micro_edge.1 = f32[64,128,128]{2,1,0:T(8,128)} custom-call(f32[768]{0:T(1024)S(1)} %concatenate.6.refs_0_, s32[768]{0:T(1024)S(1)} %constant_dynamic-update-slice_fusion.refs_1_, f32[64,8,8,128]{3,2,1,0:T(8,128)S(1)} %get-tuple-element.29.refs_2_, f32[2,64,128]{2,1,0:T(8,128)S(1)} %collective-permute-done.5.refs_3_, ...), custom_call_target="tpu_custom_call" | custom-call | flops 16777216 | bytes 8388608 | tf_op jit(solution)/shard_map/micro_edge/pallas_call | solution.py:403
  (12 shorter events, 0.1 us)
Async XLA Ops:
  0.0 2.2 %copy-start = (f32[64,32,4,128]{3,2,1,0:T(4,128)S(1)}, f32[64,32,4,128]{3,2,1,0:T(4,128)}, u32[]{:S(2)}) copy-start(f32[64,32,4,128]{3,2,1,0:T(4,128)} %param.11) | copy-start | bytes 12582916
  2.2 2.9 %copy-start.3 = (f32[32,4,128]{2,1,0:T(4,128)S(1)}, f32[32,4,128]{2,1,0:T(4,128)}, u32[]{:S(2)}) copy-start(f32[32,4,128]{2,1,0:T(4,128)} %param.13) | copy-start | bytes 196612
  3.3 25.5 %collective-permute-start.3 = (f32[64,32,128]{2,1,0:T(8,128)}, f32[64,32,128]{2,1,0:T(8,128)S(1)}, u32[]{:S(2)}, u32[]{:S(2)}) collective-permute-start(f32[64,32,128]{2,1,0:T(8,128)} %get-tuple-element.20), channel_id=1, source_target_pairs={{0,8},{8,16},{16,24},{24,0},{1,9},{9,17},{17,25},{25,1},{2,10},{10... | collective-permute-start | bytes 3145736 | tf_op jit(solution)/shard_map/ppermute | solution.py:296
  3.3 25.5 %collective-permute-start.4 = (f32[64,32,128]{2,1,0:T(8,128)S(1)}, f32[64,32,128]{2,1,0:T(8,128)S(1)}, u32[]{:S(2)}, u32[]{:S(2)}) collective-permute-start(f32[64,32,128]{2,1,0:T(8,128)S(1)} %get-tuple-element.28.refs_6_), channel_id=1, source_target_pairs={{8,0},{16,8},{24,16},{0,24},{9,1},{17,9},{25,17},{1,25},{10,2},{18... | collective-permute-start | bytes 3145736 | tf_op jit(solution)/shard_map/ppermute | solution.py:301
  5.1 6.7 %copy-start.2 = (f32[32,4,128]{2,1,0:T(4,128)S(1)}, f32[32,4,128]{2,1,0:T(4,128)}, u32[]{:S(2)}) copy-start(f32[32,4,128]{2,1,0:T(4,128)} %param.12) | copy-start | bytes 196612
  5.1 6.9 %copy-start.6 = (s32[48,8]{0,1:T(8,128)S(1)}, s32[48,8]{0,1:T(8,128)}, u32[]{:S(2)}) copy-start(s32[48,8]{0,1:T(8,128)} %param.20) | copy-start | bytes 4612
  5.1 7.1 %copy-start.11 = (f32[64]{0:T(128)S(1)}, f32[64]{0:T(128)}, u32[]{:S(2)}) copy-start(f32[64]{0:T(128)} %param.16) | copy-start | bytes 772
  5.1 8.2 %copy-start.7 = (f32[48,8]{0,1:T(8,128)S(1)}, f32[48,8]{0,1:T(8,128)}, u32[]{:S(2)}) copy-start(f32[48,8]{0,1:T(8,128)} %param.19) | copy-start | bytes 4612
  5.1 8.3 %copy-start.8 = (s32[48,8]{0,1:T(8,128)S(1)}, s32[48,8]{0,1:T(8,128)}, u32[]{:S(2)}) copy-start(s32[48,8]{0,1:T(8,128)} %param.21) | copy-start | bytes 4612
  5.1 8.5 %copy-start.9 = (f32[47]{0:T(128)S(1)}, f32[47]{0:T(128)}, u32[]{:S(2)}) copy-start(f32[47]{0:T(128)} %param.17) | copy-start | bytes 568
  5.1 8.5 %copy-start.10 = (f32[16]{0:T(128)S(1)}, f32[16]{0:T(128)}, u32[]{:S(2)}) copy-start(f32[16]{0:T(128)} %param.18) | copy-start | bytes 196
  7.9 5.9 %collective-permute-start = (f32[9,8,128]{2,1,0:T(8,128)S(1)}, f32[9,8,128]{2,1,0:T(8,128)S(1)}, u32[]{:S(2)}, u32[]{:S(2)}) collective-permute-start(f32[9,8,128]{2,1,0:T(8,128)S(1)} %get-tuple-element.23), channel_id=1, source_target_pairs={{0,2},{2,4},{4,6},{6,0},{1,3},{3,5},{5,7},{7,1},{8,10},{10,12},{12... | collective-permute-start | bytes 110600 | tf_op jit(solution)/shard_map/ppermute | solution.py:296
  9.5 4.3 %collective-permute-start.1 = (f32[8,8,128]{2,1,0:T(8,128)S(1)}, f32[8,8,128]{2,1,0:T(8,128)S(1)}, u32[]{:S(2)}, u32[]{:S(2)}) collective-permute-start(f32[8,8,128]{2,1,0:T(8,128)S(1)} %get-tuple-element.24), channel_id=1, source_target_pairs={{2,0},{4,2},{6,4},{0,6},{3,1},{5,3},{7,5},{1,7},{10,8},{12,10},{14... | collective-permute-start | bytes 98312 | tf_op jit(solution)/shard_map/ppermute | solution.py:301
  11.8 17.0 %collective-permute-start.2 = (f32[32,128]{1,0:T(8,128)S(1)}, f32[32,128]{1,0:T(8,128)S(1)}, u32[]{:S(2)}, u32[]{:S(2)}) collective-permute-start(f32[32,128]{1,0:T(8,128)S(1)} %slice_bitcast_fusion), channel_id=1, source_target_pairs={{0,8},{8,16},{16,24},{24,0},{1,9},{9,17},{17,25},{25,1},{2,10},{10... | collective-permute-start | bytes 49160 | tf_op jit(solution)/shard_map/ppermute | solution.py:296
  15.1 2.2 %copy-start.1 = (f32[64,32,4,128]{3,2,1,0:T(4,128)S(1)}, f32[64,32,4,128]{3,2,1,0:T(4,128)}, u32[]{:S(2)}) copy-start(f32[64,32,4,128]{3,2,1,0:T(4,128)} %param.11) | copy-start | bytes 12582916
  24.3 9.0 %collective-permute-start.6 = (f32[2,64,128]{2,1,0:T(8,128)S(1)}, f32[2,64,128]{2,1,0:T(8,128)S(1)}, u32[]{:S(2)}, u32[]{:S(2)}) collective-permute-start(f32[2,64,128]{2,1,0:T(8,128)S(1)} %get-tuple-element.34), channel_id=1, source_target_pairs={{1,0},{3,2},{5,4},{7,6},{9,8},{11,10},{13,12},{15,14},{17,16},{19,... | collective-permute-start | bytes 196616 | tf_op jit(solution)/shard_map/ppermute | solution.py:393
  28.8 4.5 %copy-start.4 = (f32[32,4,128]{2,1,0:T(4,128)S(1)}, f32[32,4,128]{2,1,0:T(4,128)}, u32[]{:S(2)}) copy-start(f32[32,4,128]{2,1,0:T(4,128)} %param.14) | copy-start | bytes 196612
  28.8 4.5 %copy-start.5 = (s32[32,4,128]{2,1,0:T(4,128)S(1)}, s32[32,4,128]{2,1,0:T(4,128)}, u32[]{:S(2)}) copy-start(s32[32,4,128]{2,1,0:T(4,128)} %param.15) | copy-start | bytes 196612
  30.6 7.6 %collective-permute-start.5 = (f32[2,64,128]{2,1,0:T(8,128)S(1)}, f32[2,64,128]{2,1,0:T(8,128)S(1)}, u32[]{:S(2)}, u32[]{:S(2)}) collective-permute-start(f32[2,64,128]{2,1,0:T(8,128)S(1)} %get-tuple-element.32), channel_id=1, source_target_pairs={{1,0},{3,2},{5,4},{7,6},{9,8},{11,10},{13,12},{15,14},{17,16},{19,... | collective-permute-start | bytes 196616 | tf_op jit(solution)/shard_map/ppermute | solution.py:393

commit v6 on v5

--- a/solution.py
+++ b/solution.py
@@ -10,6 +10,7 @@
 LANES = 128
 SUB = 8
 GROUP = 8
+WRITES = 4
 
 
 def roll_to(value, source, dest):
@@ -180,7 +181,8 @@
 
 def micro_kernel(nx, xs, slots, merge, *refs):
     if merge:
-        scal, index, settled, carry, table, sat_ref, mask_ref, inner, out, grown, change = refs
+        scal, index, settled, carry, table, sat_ref, mask_ref, inner, final = refs[:9]
+        grown, change, out, sems = refs[9:]
     else:
         scal, index, settled, carry, table, sat_ref, mask_ref, out, grown, change = refs
     bins = settled.shape[0]
@@ -226,7 +228,25 @@
             fresh.append(gained[v] + active)
         return tuple(fresh)
 
+    def fill(b, _):
+        others = [x for x in range(nx) if x not in xs]
+        for xi, x in enumerate(others):
+            for q in range(blocks):
+                out[b, pl.ds(q * SUB * nx + x, SUB, stride=nx), :] = inner[b, xi * blocks + q]
+        return 0
+
+    copies = []
+
+    def send(begin, size):
+        part = pl.ds(begin, size)
+        copy = pltpu.make_async_copy(out.at[part], final.at[part], sems.at[len(copies)])
+        copy.start()
+        copies.append(copy)
+
     gained = lax.fori_loop(0, aero, activate, (zero,) * cells)
+    if merge:
+        lax.fori_loop(drops, bins, fill, 0)
+        send(drops, aero)
 
     def condense(b, state):
         current, below = state
@@ -268,18 +288,18 @@
             put(b, v, grown[b, v] + mask[v] * change[b, v])
         return 0
 
-    lax.fori_loop(0, drops, finish, 0)
-
     if merge:
-        others = [x for x in range(nx) if x not in xs]
-
-        def fill(b, _):
-            for xi, x in enumerate(others):
-                for q in range(blocks):
-                    out[b, pl.ds(q * SUB * nx + x, SUB, stride=nx), :] = inner[b, xi * blocks + q]
-            return 0
-
-        lax.fori_loop(0, bins, fill, 0)
+        lax.fori_loop(0, drops, fill, 0)
+        size = drops // WRITES
+        for n in range(WRITES):
+            begin = n * size
+            end = begin + size if n < WRITES - 1 else drops
+            lax.fori_loop(begin, end, finish, 0)
+            send(begin, end - begin)
+        for copy in copies:
+            copy.wait()
+    else:
+        lax.fori_loop(0, drops, finish, 0)
 
 
 VMEM = pl.BlockSpec(memory_space=pltpu.VMEM)
@@ -404,11 +424,12 @@
             functools.partial(micro_kernel, nx, xs, slots, bool(inner)),
             out_shape=out,
             in_specs=[SMEM, SMEM] + [VMEM] * (len(args) - 2),
-            out_specs=VMEM,
+            out_specs=pl.BlockSpec(memory_space=pl.ANY) if inner else VMEM,
             scratch_shapes=[
                 pltpu.VMEM((drops, cells, SUB, LANES), f32),
                 pltpu.VMEM((drops, cells, SUB, LANES), f32),
-            ],
+            ]
+            + ([pltpu.VMEM(out.shape, f32), pltpu.SemaphoreType.DMA((WRITES + 1,))] if inner else []),
             compiler_params=PARAMS,
             cost_estimate=cost(1 << 24, 8 << 20),
             name="micro_edge" if inner else "micro_inner",

time: 45.9 us -> 45.3 us (0.987)
  Pallas kernels: 25.1 us -> 24.5 us
    pallas_call x2, Pallas kernels: 12.4 us -> 11.8 us  [micro_part(): pl.pallas_call(functools.partial(micro_kernel, nx, xs, slots, bool(inner)...]
  transfers between devices with their start and end apart: 7 -> 7, of which waited for: 2 -> 2; matrix products, arithmetic and copies ran while one was open for 7% -> 7% of each run, Pallas kernels for 36% -> 37%
where the time goes in v6:
time: 45.3 us; the launch traced here: 45.1 us
  Pallas kernels  24.5 us (54%)
  starting transfers between devices  10.7 us (24%)
  local copies, waits for them, and re-layouts  6.35 us (14%)
  waiting for transfers between devices  2.19 us (5%)
  other arithmetic  1.07 us (2%)
    pallas_call x2, Pallas kernels, micro_part(): pl.pallas_call(functools.partial(micro_kernel, nx, xs, slots, bool(inner)...  11.8 us
    pallas_call x1, Pallas kernels, shards(): pl.pallas_call(functools.partial(settle_kernel, nx, (inner_x, edge_x)), o...  7.03 us
    ppermute x2, starting transfers between devices, inflow(): carry = lax.ppermute(sent, 'gz', [(i + 1, i) for i in range(count - 1)])  5.05 us
    unnamed x28, local copies, waits for them, and re-layouts  4.67 us
    ppermute x2, starting transfers between devices, shift_down(): lax.ppermute(value, axis, [((i + 1) % count, i) for i in range(count)])  3.99 us
    pallas_call x1, Pallas kernels, shards(): pl.pallas_call(functools.partial(pack_y_kernel, nx), out_shape=(jax.Shape...  2.76 us
    ppermute x3, waiting for transfers between devices, shift_up(): lax.ppermute(value, axis, [(i, (i + 1) % count) for i in range(count)])  2.06 us
    pallas_call x1, Pallas kernels, shards(): pl.pallas_call(functools.partial(edge_kernel, nx), out_shape=settle_shape...  1.79 us
  transfers between devices with their start and end apart: 7, of which 2 were waited for; matrix products, arithmetic and copies ran while one was open for 7% of the time, Pallas kernels for 37%

profile of v6, /device:TPU:6, one launch (start us, length us, event | category | flops | bytes accessed | tf_op | source)
XLA Modules:
  0.0 45.1 jit_solution(9327662988556498535)
XLA Ops:
  0.0 0.0 copy-start
  0.0 2.2 %copy-done = f32[64,32,4,128]{3,2,1,0:T(4,128)S(1)} copy-done((f32[64,32,4,128]{3,2,1,0:T(4,128)S(1)}, f32[64,32,4,128]{3,2,1,0:T(4,128)}, u32[]{:S(2)}) %copy-start) | copy-done | bytes 4194328
  2.2 0.0 copy-start.3
  2.2 1.1 %pack_x.1 = (f32[64,32,128]{2,1,0:T(8,128)}, f32[64,32,128]{2,1,0:T(8,128)S(1)}) custom-call(f32[64,128,128]{2,1,0:T(8,128)S(1)} %bitcast.10), custom_call_target="tpu_custom_call" | custom-call | flops 1048576 | bytes 6291456 | tf_op jit(solution)/shard_map/pack_x/pallas_call | solution.py:348
  3.3 0.0 collective-permute-start.3
  3.3 1.7 %collective-permute-start.4 = (f32[64,32,128]{2,1,0:T(8,128)S(1)}, f32[64,32,128]{2,1,0:T(8,128)S(1)}, u32[]{:S(2)}, u32[]{:S(2)}) collective-permute-start(f32[64,32,128]{2,1,0:T(8,128)S(1)} %get-tuple-element.28.refs_6_), channel_id=1, source_target_pairs={{8,0},{16,8},{24,16},{0,24},{9,1},{17,9},{25,17},{1,25},{10,2},{18... | collective-permute-start | bytes 3145736 | tf_op jit(solution)/shard_map/ppermute | solution.py:321
  5.1 0.0 copy-done.3
  5.1 0.0 copy-start.2
  5.1 0.0 copy-start.6
  5.1 0.0 copy-start.11
  5.1 0.0 copy-start.7
  5.1 0.0 copy-start.8
  5.1 0.0 copy-start.9
  5.1 0.0 copy-start.10
  5.1 2.8 %pack_y.1 = (f32[9,8,128]{2,1,0:T(8,128)S(1)}, f32[8,8,128]{2,1,0:T(8,128)S(1)}) custom-call(f32[64,128,128]{2,1,0:T(8,128)S(1)} %bitcast.11, f32[128,128]{1,0:T(8,128)S(1)} %bitcast.15), custom_call_target="tpu_custom_call" | custom-call | flops 4194304 | bytes 4194304 | tf_op jit(solution)/shard_map/pack_y/pallas_call | solution.py:362
  7.9 1.6 %collective-permute-start = (f32[9,8,128]{2,1,0:T(8,128)S(1)}, f32[9,8,128]{2,1,0:T(8,128)S(1)}, u32[]{:S(2)}, u32[]{:S(2)}) collective-permute-start(f32[9,8,128]{2,1,0:T(8,128)S(1)} %get-tuple-element.23), channel_id=1, source_target_pairs={{0,2},{2,4},{4,6},{6,0},{1,3},{3,5},{5,7},{7,1},{8,10},{10,12},{12... | collective-permute-start | bytes 110600 | tf_op jit(solution)/shard_map/ppermute | solution.py:316
  9.5 2.2 %collective-permute-start.1 = (f32[8,8,128]{2,1,0:T(8,128)S(1)}, f32[8,8,128]{2,1,0:T(8,128)S(1)}, u32[]{:S(2)}, u32[]{:S(2)}) collective-permute-start(f32[8,8,128]{2,1,0:T(8,128)S(1)} %get-tuple-element.24), channel_id=1, source_target_pairs={{2,0},{4,2},{6,4},{0,6},{3,1},{5,3},{7,5},{1,7},{10,8},{12,10},{14... | collective-permute-start | bytes 98312 | tf_op jit(solution)/shard_map/ppermute | solution.py:321
  11.8 0.0 copy-done.2
  11.8 0.1 collective-permute-start.2
  11.9 0.1 pad_maximum_fusion.1
  12.0 0.0 copy-done.6
  12.0 0.1 copy.14
  12.1 0.1 reshape.80
  12.2 0.0 copy-done.11
  12.2 0.1 pad_maximum_fusion
  12.3 0.1 multiply_exponential_fusion
  12.4 0.8 %exponential_select_fusion = f32[64,4,8]{2,1,0:T(4,128)} fusion(f32[4,8]{1,0:T(4,128)S(1)} %pad_maximum_fusion, f32[64]{0:T(128)S(1)} %get-tuple-element.35, pred[4,8]{1,0:T(4,128)(4,1)S(1)} %pad_add_fusion), kind=kLoop, calls=%fused_computation | loop fusion | flops 4096 | bytes 8608 | tf_op jit(solution)/shard_map/jit(_where)/select_n | solution.py:382
  13.2 0.1 exp.15
  13.3 0.0 copy-done.7
  13.3 0.1 copy.13
  13.3 0.1 reshape.79
  13.4 0.0 copy-done.8
  13.4 0.1 copy.15
  13.5 0.1 reshape.81
  13.6 0.0 copy-done.9
  13.6 0.0 copy-done.10
  13.6 0.1 concatenate.6.refs_0_
  13.7 0.1 collective-permute-done.1.refs_5_
  13.8 0.0 collective-permute-done.refs_4_
  13.8 1.2 %broadcast_in_dim.20.refs_6_.refs_4_ = f32[64,4,8,128]{3,2,1,0:T(8,128)S(1)} broadcast(f32[64,4,8]{2,1,0:T(4,128)} %exponential_select_fusion), dimensions={0,1,2} | broadcast | bytes 1056768 | tf_op jit(solution)/shard_map/broadcast_in_dim | solution.py:383
  15.1 0.0 copy-start.1
  15.1 2.2 %copy-done.1 = f32[64,32,4,128]{3,2,1,0:T(4,128)S(1)} copy-done((f32[64,32,4,128]{3,2,1,0:T(4,128)S(1)}, f32[64,32,4,128]{3,2,1,0:T(4,128)}, u32[]{:S(2)}) %copy-start.1) | copy-done | bytes 4194328
  17.3 7.0 %settle_all.1 = (f32[64,8,8,128]{3,2,1,0:T(8,128)S(1)}, f32[2,64,128]{2,1,0:T(8,128)S(1)}, f32[64,8,8,128]{3,2,1,0:T(8,128)S(1)}, f32[2,64,128]{2,1,0:T(8,128)S(1)}) custom-call(f32[768]{0:T(1024)S(1)} %concatenate.6.refs_0_, f32[64,128,128]{2,1,0:T(8,128)S(1)} %bitcast.12, f32[128,128]{1,0:T(8,128)S(1)} %bitcast.13, f32[128,128]{1,0:T(8,128)S(1)} %bitcast.16, ...), custom_call_target="tpu_custom_call" | custom-call | flops 16777216 | bytes 16777216 | tf_op jit(solution)/shard_map/settle_all/pallas_call | solution.py:438
  24.3 2.4 %collective-permute-start.6 = (f32[2,64,128]{2,1,0:T(8,128)S(1)}, f32[2,64,128]{2,1,0:T(8,128)S(1)}, u32[]{:S(2)}, u32[]{:S(2)}) collective-permute-start(f32[2,64,128]{2,1,0:T(8,128)S(1)} %get-tuple-element.34), channel_id=1, source_target_pairs={{1,0},{3,2},{5,4},{7,6},{9,8},{11,10},{13,12},{15,14},{17,16},{19,... | collective-permute-start | bytes 196616 | tf_op jit(solution)/shard_map/ppermute | solution.py:413
  26.8 2.1 %collective-permute-done.2.refs_5_ = f32[32,128]{1,0:T(8,128)S(1)} collective-permute-done((f32[32,128]{1,0:T(8,128)S(1)}, f32[32,128]{1,0:T(8,128)S(1)}, u32[]{:S(2)}, u32[]{:S(2)}) %collective-permute-start.2) | collective-permute-done | bytes 16416 | tf_op jit(solution)/shard_map/ppermute | solution.py:316
  28.8 0.0 collective-permute-done.3.refs_7_
  28.8 0.0 collective-permute-done.4.refs_8_
  28.8 0.0 copy-start.4
  28.8 0.0 copy-start.5
  28.8 1.8 %settle_edge.1 = (f32[64,8,8,128]{3,2,1,0:T(8,128)S(1)}, f32[2,64,128]{2,1,0:T(8,128)S(1)}) custom-call(f32[768]{0:T(1024)S(1)} %concatenate.6.refs_0_, f32[64,8,8,128]{3,2,1,0:T(8,128)S(1)} %get-tuple-element.25.refs_1_, f32[2,64,128]{2,1,0:T(8,128)S(1)} %get-tuple-element.26.refs_2_, f32[128,128]{1,0:T(8,128)S(1)} %bitcast.14, ...), custom_call_target="tpu_custom_call" | custom-call | flops 8388608 | bytes 8388608 | tf_op jit(solution)/shard_map/settle_edge/pallas_call | solution.py:448
  30.6 2.6 %collective-permute-start.5 = (f32[2,64,128]{2,1,0:T(8,128)S(1)}, f32[2,64,128]{2,1,0:T(8,128)S(1)}, u32[]{:S(2)}, u32[]{:S(2)}) collective-permute-start(f32[2,64,128]{2,1,0:T(8,128)S(1)} %get-tuple-element.32), channel_id=1, source_target_pairs={{1,0},{3,2},{5,4},{7,6},{9,8},{11,10},{13,12},{15,14},{17,16},{19,... | collective-permute-start | bytes 196616 | tf_op jit(solution)/shard_map/ppermute | solution.py:413
  33.3 0.0 collective-permute-done.6.refs_3_
  33.3 0.0 copy-done.4
  33.3 0.0 copy-done.5
  33.3 4.9 %micro_inner.1.refs_7_ = f32[64,8,8,128]{3,2,1,0:T(8,128)S(1)} custom-call(f32[768]{0:T(1024)S(1)} %concatenate.6.refs_0_, s32[768]{0:T(1024)S(1)} %constant_dynamic-update-slice_fusion.refs_1_, f32[64,8,8,128]{3,2,1,0:T(8,128)S(1)} %get-tuple-element.33.refs_2_, f32[2,64,128]{2,1,0:T(8,128)S(1)} %collective-permute-done.6.refs_3_, ...), custom_call_target="tpu_custom_call" | custom-call | flops 16777216 | bytes 8388608 | tf_op jit(solution)/shard_map/micro_inner/pallas_call | solution.py:423
  38.2 0.0 collective-permute-done.5.refs_3_
  38.2 6.9 %micro_edge.1 = f32[64,128,128]{2,1,0:T(8,128)} custom-call(f32[768]{0:T(1024)S(1)} %concatenate.6.refs_0_, s32[768]{0:T(1024)S(1)} %constant_dynamic-update-slice_fusion.refs_1_, f32[64,8,8,128]{3,2,1,0:T(8,128)S(1)} %get-tuple-element.29.refs_2_, f32[2,64,128]{2,1,0:T(8,128)S(1)} %collective-permute-done.5.refs_3_, ...), custom_call_target="tpu_custom_call" | custom-call | flops 16777216 | bytes 8388608 | tf_op jit(solution)/shard_map/micro_edge/pallas_call | solution.py:423
  (12 shorter events, 0.1 us)
Async XLA Ops:
  0.0 2.2 %copy-start = (f32[64,32,4,128]{3,2,1,0:T(4,128)S(1)}, f32[64,32,4,128]{3,2,1,0:T(4,128)}, u32[]{:S(2)}) copy-start(f32[64,32,4,128]{3,2,1,0:T(4,128)} %param.11) | copy-start | bytes 12582916
  2.2 2.9 %copy-start.3 = (f32[32,4,128]{2,1,0:T(4,128)S(1)}, f32[32,4,128]{2,1,0:T(4,128)}, u32[]{:S(2)}) copy-start(f32[32,4,128]{2,1,0:T(4,128)} %param.13) | copy-start | bytes 196612
  3.3 25.5 %collective-permute-start.3 = (f32[64,32,128]{2,1,0:T(8,128)}, f32[64,32,128]{2,1,0:T(8,128)S(1)}, u32[]{:S(2)}, u32[]{:S(2)}) collective-permute-start(f32[64,32,128]{2,1,0:T(8,128)} %get-tuple-element.20), channel_id=1, source_target_pairs={{0,8},{8,16},{16,24},{24,0},{1,9},{9,17},{17,25},{25,1},{2,10},{10... | collective-permute-start | bytes 3145736 | tf_op jit(solution)/shard_map/ppermute | solution.py:316
  3.3 25.5 %collective-permute-start.4 = (f32[64,32,128]{2,1,0:T(8,128)S(1)}, f32[64,32,128]{2,1,0:T(8,128)S(1)}, u32[]{:S(2)}, u32[]{:S(2)}) collective-permute-start(f32[64,32,128]{2,1,0:T(8,128)S(1)} %get-tuple-element.28.refs_6_), channel_id=1, source_target_pairs={{8,0},{16,8},{24,16},{0,24},{9,1},{17,9},{25,17},{1,25},{10,2},{18... | collective-permute-start | bytes 3145736 | tf_op jit(solution)/shard_map/ppermute | solution.py:321
  5.1 6.7 %copy-start.2 = (f32[32,4,128]{2,1,0:T(4,128)S(1)}, f32[32,4,128]{2,1,0:T(4,128)}, u32[]{:S(2)}) copy-start(f32[32,4,128]{2,1,0:T(4,128)} %param.12) | copy-start | bytes 196612
  5.1 6.9 %copy-start.6 = (s32[48,8]{0,1:T(8,128)S(1)}, s32[48,8]{0,1:T(8,128)}, u32[]{:S(2)}) copy-start(s32[48,8]{0,1:T(8,128)} %param.20) | copy-start | bytes 4612
  5.1 7.1 %copy-start.11 = (f32[64]{0:T(128)S(1)}, f32[64]{0:T(128)}, u32[]{:S(2)}) copy-start(f32[64]{0:T(128)} %param.16) | copy-start | bytes 772
  5.1 8.2 %copy-start.7 = (f32[48,8]{0,1:T(8,128)S(1)}, f32[48,8]{0,1:T(8,128)}, u32[]{:S(2)}) copy-start(f32[48,8]{0,1:T(8,128)} %param.19) | copy-start | bytes 4612
  5.1 8.3 %copy-start.8 = (s32[48,8]{0,1:T(8,128)S(1)}, s32[48,8]{0,1:T(8,128)}, u32[]{:S(2)}) copy-start(s32[48,8]{0,1:T(8,128)} %param.21) | copy-start | bytes 4612
  5.1 8.5 %copy-start.9 = (f32[47]{0:T(128)S(1)}, f32[47]{0:T(128)}, u32[]{:S(2)}) copy-start(f32[47]{0:T(128)} %param.17) | copy-start | bytes 568
  5.1 8.5 %copy-start.10 = (f32[16]{0:T(128)S(1)}, f32[16]{0:T(128)}, u32[]{:S(2)}) copy-start(f32[16]{0:T(128)} %param.18) | copy-start | bytes 196
  7.9 5.9 %collective-permute-start = (f32[9,8,128]{2,1,0:T(8,128)S(1)}, f32[9,8,128]{2,1,0:T(8,128)S(1)}, u32[]{:S(2)}, u32[]{:S(2)}) collective-permute-start(f32[9,8,128]{2,1,0:T(8,128)S(1)} %get-tuple-element.23), channel_id=1, source_target_pairs={{0,2},{2,4},{4,6},{6,0},{1,3},{3,5},{5,7},{7,1},{8,10},{10,12},{12... | collective-permute-start | bytes 110600 | tf_op jit(solution)/shard_map/ppermute | solution.py:316
  9.5 4.3 %collective-permute-start.1 = (f32[8,8,128]{2,1,0:T(8,128)S(1)}, f32[8,8,128]{2,1,0:T(8,128)S(1)}, u32[]{:S(2)}, u32[]{:S(2)}) collective-permute-start(f32[8,8,128]{2,1,0:T(8,128)S(1)} %get-tuple-element.24), channel_id=1, source_target_pairs={{2,0},{4,2},{6,4},{0,6},{3,1},{5,3},{7,5},{1,7},{10,8},{12,10},{14... | collective-permute-start | bytes 98312 | tf_op jit(solution)/shard_map/ppermute | solution.py:321
  11.8 17.0 %collective-permute-start.2 = (f32[32,128]{1,0:T(8,128)S(1)}, f32[32,128]{1,0:T(8,128)S(1)}, u32[]{:S(2)}, u32[]{:S(2)}) collective-permute-start(f32[32,128]{1,0:T(8,128)S(1)} %slice_bitcast_fusion), channel_id=1, source_target_pairs={{0,8},{8,16},{16,24},{24,0},{1,9},{9,17},{17,25},{25,1},{2,10},{10... | collective-permute-start | bytes 49160 | tf_op jit(solution)/shard_map/ppermute | solution.py:316
  15.1 2.2 %copy-start.1 = (f32[64,32,4,128]{3,2,1,0:T(4,128)S(1)}, f32[64,32,4,128]{3,2,1,0:T(4,128)}, u32[]{:S(2)}) copy-start(f32[64,32,4,128]{3,2,1,0:T(4,128)} %param.11) | copy-start | bytes 12582916
  24.3 9.0 %collective-permute-start.6 = (f32[2,64,128]{2,1,0:T(8,128)S(1)}, f32[2,64,128]{2,1,0:T(8,128)S(1)}, u32[]{:S(2)}, u32[]{:S(2)}) collective-permute-start(f32[2,64,128]{2,1,0:T(8,128)S(1)} %get-tuple-element.34), channel_id=1, source_target_pairs={{1,0},{3,2},{5,4},{7,6},{9,8},{11,10},{13,12},{15,14},{17,16},{19,... | collective-permute-start | bytes 196616 | tf_op jit(solution)/shard_map/ppermute | solution.py:413
  28.8 4.5 %copy-start.4 = (f32[32,4,128]{2,1,0:T(4,128)S(1)}, f32[32,4,128]{2,1,0:T(4,128)}, u32[]{:S(2)}) copy-start(f32[32,4,128]{2,1,0:T(4,128)} %param.14) | copy-start | bytes 196612
  28.8 4.5 %copy-start.5 = (s32[32,4,128]{2,1,0:T(4,128)S(1)}, s32[32,4,128]{2,1,0:T(4,128)}, u32[]{:S(2)}) copy-start(s32[32,4,128]{2,1,0:T(4,128)} %param.15) | copy-start | bytes 196612
  30.6 7.6 %collective-permute-start.5 = (f32[2,64,128]{2,1,0:T(8,128)S(1)}, f32[2,64,128]{2,1,0:T(8,128)S(1)}, u32[]{:S(2)}, u32[]{:S(2)}) collective-permute-start(f32[2,64,128]{2,1,0:T(8,128)S(1)} %get-tuple-element.32), channel_id=1, source_target_pairs={{1,0},{3,2},{5,4},{7,6},{9,8},{11,10},{13,12},{15,14},{17,16},{19,... | collective-permute-start | bytes 196616 | tf_op jit(solution)/shard_map/ppermute | solution.py:413

commit v7 on v6

--- a/solution.py
+++ b/solution.py
@@ -245,7 +245,7 @@
 
     gained = lax.fori_loop(0, aero, activate, (zero,) * cells)
     if merge:
-        lax.fori_loop(drops, bins, fill, 0)
+        lax.fori_loop(drops, bins, fill, 0, unroll=4)
         send(drops, aero)
 
     def condense(b, state):
@@ -279,7 +279,7 @@
         change[i] = change[i] - loss
         return 0
 
-    lax.fori_loop(0, drops, collide, 0)
+    lax.fori_loop(0, drops, collide, 0, unroll=2)
 
     mask = [mask_ref[spans(v), :].astype(jnp.float32) for v in range(cells)]
 
@@ -289,17 +289,17 @@
         return 0
 
     if merge:
-        lax.fori_loop(0, drops, fill, 0)
+        lax.fori_loop(0, drops, fill, 0, unroll=4)
         size = drops // WRITES
         for n in range(WRITES):
             begin = n * size
             end = begin + size if n < WRITES - 1 else drops
-            lax.fori_loop(begin, end, finish, 0)
+            lax.fori_loop(begin, end, finish, 0, unroll=4)
             send(begin, end - begin)
         for copy in copies:
             copy.wait()
     else:
-        lax.fori_loop(0, drops, finish, 0)
+        lax.fori_loop(0, drops, finish, 0, unroll=4)
 
 
 VMEM = pl.BlockSpec(memory_space=pltpu.VMEM)

time: 45.3 us -> 44.9 us (level)
  Pallas kernels: 24.5 us -> 24 us
    pallas_call x2, Pallas kernels: 11.8 us -> 11.3 us  [micro_part(): pl.pallas_call(functools.partial(micro_kernel, nx, xs, slots, bool(inner)...]
where the time goes in v7:
time: 44.9 us; the launch traced here: 44.6 us
  Pallas kernels  24 us (53%)
  starting transfers between devices  10.7 us (24%)
  local copies, waits for them, and re-layouts  6.35 us (14%)
  waiting for transfers between devices  2.19 us (5%)
  other arithmetic  1.07 us (2%)
    pallas_call x2, Pallas kernels, micro_part(): pl.pallas_call(functools.partial(micro_kernel, nx, xs, slots, bool(inner)...  11.3 us
    pallas_call x1, Pallas kernels, shards(): pl.pallas_call(functools.partial(settle_kernel, nx, (inner_x, edge_x)), o...  7.03 us
    ppermute x2, starting transfers between devices, inflow(): carry = lax.ppermute(sent, 'gz', [(i + 1, i) for i in range(count - 1)])  5.05 us
    unnamed x28, local copies, waits for them, and re-layouts  4.67 us
    ppermute x2, starting transfers between devices, shift_down(): lax.ppermute(value, axis, [((i + 1) % count, i) for i in range(count)])  3.99 us
    pallas_call x1, Pallas kernels, shards(): pl.pallas_call(functools.partial(pack_y_kernel, nx), out_shape=(jax.Shape...  2.76 us
    ppermute x3, waiting for transfers between devices, shift_up(): lax.ppermute(value, axis, [(i, (i + 1) % count) for i in range(count)])  2.06 us
    pallas_call x1, Pallas kernels, shards(): pl.pallas_call(functools.partial(edge_kernel, nx), out_shape=settle_shape...  1.79 us
  transfers between devices with their start and end apart: 7, of which 2 were waited for; matrix products, arithmetic and copies ran while one was open for 7% of the time, Pallas kernels for 37%

profile of v7, /device:TPU:6, one launch (start us, length us, event | category | flops | bytes accessed | tf_op | source)
XLA Modules:
  0.0 44.6 jit_solution(1228165752878851235)
XLA Ops:
  0.0 0.0 copy-start
  0.0 2.2 %copy-done = f32[64,32,4,128]{3,2,1,0:T(4,128)S(1)} copy-done((f32[64,32,4,128]{3,2,1,0:T(4,128)S(1)}, f32[64,32,4,128]{3,2,1,0:T(4,128)}, u32[]{:S(2)}) %copy-start) | copy-done | bytes 4194328
  2.2 0.0 copy-start.3
  2.2 1.1 %pack_x.1 = (f32[64,32,128]{2,1,0:T(8,128)}, f32[64,32,128]{2,1,0:T(8,128)S(1)}) custom-call(f32[64,128,128]{2,1,0:T(8,128)S(1)} %bitcast.10), custom_call_target="tpu_custom_call" | custom-call | flops 1048576 | bytes 6291456 | tf_op jit(solution)/shard_map/pack_x/pallas_call | solution.py:348
  3.3 0.0 collective-permute-start.3
  3.3 1.7 %collective-permute-start.4 = (f32[64,32,128]{2,1,0:T(8,128)S(1)}, f32[64,32,128]{2,1,0:T(8,128)S(1)}, u32[]{:S(2)}, u32[]{:S(2)}) collective-permute-start(f32[64,32,128]{2,1,0:T(8,128)S(1)} %get-tuple-element.28.refs_6_), channel_id=1, source_target_pairs={{8,0},{16,8},{24,16},{0,24},{9,1},{17,9},{25,17},{1,25},{10,2},{18... | collective-permute-start | bytes 3145736 | tf_op jit(solution)/shard_map/ppermute | solution.py:321
  5.1 0.0 copy-done.3
  5.1 0.0 copy-start.2
  5.1 0.0 copy-start.6
  5.1 0.0 copy-start.11
  5.1 0.0 copy-start.7
  5.1 0.0 copy-start.8
  5.1 0.0 copy-start.9
  5.1 0.0 copy-start.10
  5.1 2.8 %pack_y.1 = (f32[9,8,128]{2,1,0:T(8,128)S(1)}, f32[8,8,128]{2,1,0:T(8,128)S(1)}) custom-call(f32[64,128,128]{2,1,0:T(8,128)S(1)} %bitcast.11, f32[128,128]{1,0:T(8,128)S(1)} %bitcast.15), custom_call_target="tpu_custom_call" | custom-call | flops 4194304 | bytes 4194304 | tf_op jit(solution)/shard_map/pack_y/pallas_call | solution.py:362
  7.9 1.6 %collective-permute-start = (f32[9,8,128]{2,1,0:T(8,128)S(1)}, f32[9,8,128]{2,1,0:T(8,128)S(1)}, u32[]{:S(2)}, u32[]{:S(2)}) collective-permute-start(f32[9,8,128]{2,1,0:T(8,128)S(1)} %get-tuple-element.23), channel_id=1, source_target_pairs={{0,2},{2,4},{4,6},{6,0},{1,3},{3,5},{5,7},{7,1},{8,10},{10,12},{12... | collective-permute-start | bytes 110600 | tf_op jit(solution)/shard_map/ppermute | solution.py:316
  9.5 2.2 %collective-permute-start.1 = (f32[8,8,128]{2,1,0:T(8,128)S(1)}, f32[8,8,128]{2,1,0:T(8,128)S(1)}, u32[]{:S(2)}, u32[]{:S(2)}) collective-permute-start(f32[8,8,128]{2,1,0:T(8,128)S(1)} %get-tuple-element.24), channel_id=1, source_target_pairs={{2,0},{4,2},{6,4},{0,6},{3,1},{5,3},{7,5},{1,7},{10,8},{12,10},{14... | collective-permute-start | bytes 98312 | tf_op jit(solution)/shard_map/ppermute | solution.py:321
  11.8 0.0 copy-done.2
  11.8 0.1 collective-permute-start.2
  11.9 0.1 pad_maximum_fusion.1
  12.0 0.0 copy-done.6
  12.0 0.1 copy.14
  12.1 0.1 reshape.80
  12.2 0.0 copy-done.11
  12.2 0.1 pad_maximum_fusion
  12.3 0.1 multiply_exponential_fusion
  12.4 0.8 %exponential_select_fusion = f32[64,4,8]{2,1,0:T(4,128)} fusion(f32[4,8]{1,0:T(4,128)S(1)} %pad_maximum_fusion, f32[64]{0:T(128)S(1)} %get-tuple-element.35, pred[4,8]{1,0:T(4,128)(4,1)S(1)} %pad_add_fusion), kind=kLoop, calls=%fused_computation | loop fusion | flops 4096 | bytes 8608 | tf_op jit(solution)/shard_map/jit(_where)/select_n | solution.py:382
  13.2 0.1 exp.15
  13.3 0.0 copy-done.7
  13.3 0.1 copy.13
  13.3 0.1 reshape.79
  13.4 0.0 copy-done.8
  13.4 0.1 copy.15
  13.5 0.1 reshape.81
  13.6 0.0 copy-done.9
  13.6 0.0 copy-done.10
  13.6 0.1 concatenate.6.refs_0_
  13.7 0.1 collective-permute-done.1.refs_5_
  13.8 0.0 collective-permute-done.refs_4_
  13.8 1.2 %broadcast_in_dim.20.refs_6_.refs_4_ = f32[64,4,8,128]{3,2,1,0:T(8,128)S(1)} broadcast(f32[64,4,8]{2,1,0:T(4,128)} %exponential_select_fusion), dimensions={0,1,2} | broadcast | bytes 1056768 | tf_op jit(solution)/shard_map/broadcast_in_dim | solution.py:383
  15.1 0.0 copy-start.1
  15.1 2.2 %copy-done.1 = f32[64,32,4,128]{3,2,1,0:T(4,128)S(1)} copy-done((f32[64,32,4,128]{3,2,1,0:T(4,128)S(1)}, f32[64,32,4,128]{3,2,1,0:T(4,128)}, u32[]{:S(2)}) %copy-start.1) | copy-done | bytes 4194328
  17.3 7.0 %settle_all.1 = (f32[64,8,8,128]{3,2,1,0:T(8,128)S(1)}, f32[2,64,128]{2,1,0:T(8,128)S(1)}, f32[64,8,8,128]{3,2,1,0:T(8,128)S(1)}, f32[2,64,128]{2,1,0:T(8,128)S(1)}) custom-call(f32[768]{0:T(1024)S(1)} %concatenate.6.refs_0_, f32[64,128,128]{2,1,0:T(8,128)S(1)} %bitcast.12, f32[128,128]{1,0:T(8,128)S(1)} %bitcast.13, f32[128,128]{1,0:T(8,128)S(1)} %bitcast.16, ...), custom_call_target="tpu_custom_call" | custom-call | flops 16777216 | bytes 16777216 | tf_op jit(solution)/shard_map/settle_all/pallas_call | solution.py:438
  24.3 2.4 %collective-permute-start.6 = (f32[2,64,128]{2,1,0:T(8,128)S(1)}, f32[2,64,128]{2,1,0:T(8,128)S(1)}, u32[]{:S(2)}, u32[]{:S(2)}) collective-permute-start(f32[2,64,128]{2,1,0:T(8,128)S(1)} %get-tuple-element.34), channel_id=1, source_target_pairs={{1,0},{3,2},{5,4},{7,6},{9,8},{11,10},{13,12},{15,14},{17,16},{19,... | collective-permute-start | bytes 196616 | tf_op jit(solution)/shard_map/ppermute | solution.py:413
  26.8 2.1 %collective-permute-done.2.refs_5_ = f32[32,128]{1,0:T(8,128)S(1)} collective-permute-done((f32[32,128]{1,0:T(8,128)S(1)}, f32[32,128]{1,0:T(8,128)S(1)}, u32[]{:S(2)}, u32[]{:S(2)}) %collective-permute-start.2) | collective-permute-done | bytes 16416 | tf_op jit(solution)/shard_map/ppermute | solution.py:316
  28.8 0.0 collective-permute-done.3.refs_7_
  28.8 0.0 collective-permute-done.4.refs_8_
  28.8 0.0 copy-start.4
  28.8 0.0 copy-start.5
  28.8 1.8 %settle_edge.1 = (f32[64,8,8,128]{3,2,1,0:T(8,128)S(1)}, f32[2,64,128]{2,1,0:T(8,128)S(1)}) custom-call(f32[768]{0:T(1024)S(1)} %concatenate.6.refs_0_, f32[64,8,8,128]{3,2,1,0:T(8,128)S(1)} %get-tuple-element.25.refs_1_, f32[2,64,128]{2,1,0:T(8,128)S(1)} %get-tuple-element.26.refs_2_, f32[128,128]{1,0:T(8,128)S(1)} %bitcast.14, ...), custom_call_target="tpu_custom_call" | custom-call | flops 8388608 | bytes 8388608 | tf_op jit(solution)/shard_map/settle_edge/pallas_call | solution.py:448
  30.6 2.6 %collective-permute-start.5 = (f32[2,64,128]{2,1,0:T(8,128)S(1)}, f32[2,64,128]{2,1,0:T(8,128)S(1)}, u32[]{:S(2)}, u32[]{:S(2)}) collective-permute-start(f32[2,64,128]{2,1,0:T(8,128)S(1)} %get-tuple-element.32), channel_id=1, source_target_pairs={{1,0},{3,2},{5,4},{7,6},{9,8},{11,10},{13,12},{15,14},{17,16},{19,... | collective-permute-start | bytes 196616 | tf_op jit(solution)/shard_map/ppermute | solution.py:413
  33.3 0.0 collective-permute-done.6.refs_3_
  33.3 0.0 copy-done.4
  33.3 0.0 copy-done.5
  33.3 4.8 %micro_inner.1.refs_7_ = f32[64,8,8,128]{3,2,1,0:T(8,128)S(1)} custom-call(f32[768]{0:T(1024)S(1)} %concatenate.6.refs_0_, s32[768]{0:T(1024)S(1)} %constant_dynamic-update-slice_fusion.refs_1_, f32[64,8,8,128]{3,2,1,0:T(8,128)S(1)} %get-tuple-element.33.refs_2_, f32[2,64,128]{2,1,0:T(8,128)S(1)} %collective-permute-done.6.refs_3_, ...), custom_call_target="tpu_custom_call" | custom-call | flops 16777216 | bytes 8388608 | tf_op jit(solution)/shard_map/micro_inner/pallas_call | solution.py:423
  38.1 0.0 collective-permute-done.5.refs_3_
  38.1 6.5 %micro_edge.1 = f32[64,128,128]{2,1,0:T(8,128)} custom-call(f32[768]{0:T(1024)S(1)} %concatenate.6.refs_0_, s32[768]{0:T(1024)S(1)} %constant_dynamic-update-slice_fusion.refs_1_, f32[64,8,8,128]{3,2,1,0:T(8,128)S(1)} %get-tuple-element.29.refs_2_, f32[2,64,128]{2,1,0:T(8,128)S(1)} %collective-permute-done.5.refs_3_, ...), custom_call_target="tpu_custom_call" | custom-call | flops 16777216 | bytes 8388608 | tf_op jit(solution)/shard_map/micro_edge/pallas_call | solution.py:423
  (12 shorter events, 0.1 us)
Async XLA Ops:
  0.0 2.2 %copy-start = (f32[64,32,4,128]{3,2,1,0:T(4,128)S(1)}, f32[64,32,4,128]{3,2,1,0:T(4,128)}, u32[]{:S(2)}) copy-start(f32[64,32,4,128]{3,2,1,0:T(4,128)} %param.11) | copy-start | bytes 12582916
  2.2 2.9 %copy-start.3 = (f32[32,4,128]{2,1,0:T(4,128)S(1)}, f32[32,4,128]{2,1,0:T(4,128)}, u32[]{:S(2)}) copy-start(f32[32,4,128]{2,1,0:T(4,128)} %param.13) | copy-start | bytes 196612
  3.3 25.5 %collective-permute-start.3 = (f32[64,32,128]{2,1,0:T(8,128)}, f32[64,32,128]{2,1,0:T(8,128)S(1)}, u32[]{:S(2)}, u32[]{:S(2)}) collective-permute-start(f32[64,32,128]{2,1,0:T(8,128)} %get-tuple-element.20), channel_id=1, source_target_pairs={{0,8},{8,16},{16,24},{24,0},{1,9},{9,17},{17,25},{25,1},{2,10},{10... | collective-permute-start | bytes 3145736 | tf_op jit(solution)/shard_map/ppermute | solution.py:316
  3.3 25.5 %collective-permute-start.4 = (f32[64,32,128]{2,1,0:T(8,128)S(1)}, f32[64,32,128]{2,1,0:T(8,128)S(1)}, u32[]{:S(2)}, u32[]{:S(2)}) collective-permute-start(f32[64,32,128]{2,1,0:T(8,128)S(1)} %get-tuple-element.28.refs_6_), channel_id=1, source_target_pairs={{8,0},{16,8},{24,16},{0,24},{9,1},{17,9},{25,17},{1,25},{10,2},{18... | collective-permute-start | bytes 3145736 | tf_op jit(solution)/shard_map/ppermute | solution.py:321
  5.1 6.7 %copy-start.2 = (f32[32,4,128]{2,1,0:T(4,128)S(1)}, f32[32,4,128]{2,1,0:T(4,128)}, u32[]{:S(2)}) copy-start(f32[32,4,128]{2,1,0:T(4,128)} %param.12) | copy-start | bytes 196612
  5.1 6.9 %copy-start.6 = (s32[48,8]{0,1:T(8,128)S(1)}, s32[48,8]{0,1:T(8,128)}, u32[]{:S(2)}) copy-start(s32[48,8]{0,1:T(8,128)} %param.20) | copy-start | bytes 4612
  5.1 7.1 %copy-start.11 = (f32[64]{0:T(128)S(1)}, f32[64]{0:T(128)}, u32[]{:S(2)}) copy-start(f32[64]{0:T(128)} %param.16) | copy-start | bytes 772
  5.1 8.2 %copy-start.7 = (f32[48,8]{0,1:T(8,128)S(1)}, f32[48,8]{0,1:T(8,128)}, u32[]{:S(2)}) copy-start(f32[48,8]{0,1:T(8,128)} %param.19) | copy-start | bytes 4612
  5.1 8.3 %copy-start.8 = (s32[48,8]{0,1:T(8,128)S(1)}, s32[48,8]{0,1:T(8,128)}, u32[]{:S(2)}) copy-start(s32[48,8]{0,1:T(8,128)} %param.21) | copy-start | bytes 4612
  5.1 8.5 %copy-start.9 = (f32[47]{0:T(128)S(1)}, f32[47]{0:T(128)}, u32[]{:S(2)}) copy-start(f32[47]{0:T(128)} %param.17) | copy-start | bytes 568
  5.1 8.5 %copy-start.10 = (f32[16]{0:T(128)S(1)}, f32[16]{0:T(128)}, u32[]{:S(2)}) copy-start(f32[16]{0:T(128)} %param.18) | copy-start | bytes 196
  7.9 5.9 %collective-permute-start = (f32[9,8,128]{2,1,0:T(8,128)S(1)}, f32[9,8,128]{2,1,0:T(8,128)S(1)}, u32[]{:S(2)}, u32[]{:S(2)}) collective-permute-start(f32[9,8,128]{2,1,0:T(8,128)S(1)} %get-tuple-element.23), channel_id=1, source_target_pairs={{0,2},{2,4},{4,6},{6,0},{1,3},{3,5},{5,7},{7,1},{8,10},{10,12},{12... | collective-permute-start | bytes 110600 | tf_op jit(solution)/shard_map/ppermute | solution.py:316
  9.5 4.3 %collective-permute-start.1 = (f32[8,8,128]{2,1,0:T(8,128)S(1)}, f32[8,8,128]{2,1,0:T(8,128)S(1)}, u32[]{:S(2)}, u32[]{:S(2)}) collective-permute-start(f32[8,8,128]{2,1,0:T(8,128)S(1)} %get-tuple-element.24), channel_id=1, source_target_pairs={{2,0},{4,2},{6,4},{0,6},{3,1},{5,3},{7,5},{1,7},{10,8},{12,10},{14... | collective-permute-start | bytes 98312 | tf_op jit(solution)/shard_map/ppermute | solution.py:321
  11.8 17.0 %collective-permute-start.2 = (f32[32,128]{1,0:T(8,128)S(1)}, f32[32,128]{1,0:T(8,128)S(1)}, u32[]{:S(2)}, u32[]{:S(2)}) collective-permute-start(f32[32,128]{1,0:T(8,128)S(1)} %slice_bitcast_fusion), channel_id=1, source_target_pairs={{0,8},{8,16},{16,24},{24,0},{1,9},{9,17},{17,25},{25,1},{2,10},{10... | collective-permute-start | bytes 49160 | tf_op jit(solution)/shard_map/ppermute | solution.py:316
  15.1 2.2 %copy-start.1 = (f32[64,32,4,128]{3,2,1,0:T(4,128)S(1)}, f32[64,32,4,128]{3,2,1,0:T(4,128)}, u32[]{:S(2)}) copy-start(f32[64,32,4,128]{3,2,1,0:T(4,128)} %param.11) | copy-start | bytes 12582916
  24.3 9.0 %collective-permute-start.6 = (f32[2,64,128]{2,1,0:T(8,128)S(1)}, f32[2,64,128]{2,1,0:T(8,128)S(1)}, u32[]{:S(2)}, u32[]{:S(2)}) collective-permute-start(f32[2,64,128]{2,1,0:T(8,128)S(1)} %get-tuple-element.34), channel_id=1, source_target_pairs={{1,0},{3,2},{5,4},{7,6},{9,8},{11,10},{13,12},{15,14},{17,16},{19,... | collective-permute-start | bytes 196616 | tf_op jit(solution)/shard_map/ppermute | solution.py:413
  28.8 4.5 %copy-start.4 = (f32[32,4,128]{2,1,0:T(4,128)S(1)}, f32[32,4,128]{2,1,0:T(4,128)}, u32[]{:S(2)}) copy-start(f32[32,4,128]{2,1,0:T(4,128)} %param.14) | copy-start | bytes 196612
  28.8 4.5 %copy-start.5 = (s32[32,4,128]{2,1,0:T(4,128)S(1)}, s32[32,4,128]{2,1,0:T(4,128)}, u32[]{:S(2)}) copy-start(s32[32,4,128]{2,1,0:T(4,128)} %param.15) | copy-start | bytes 196612
  30.6 7.4 %collective-permute-start.5 = (f32[2,64,128]{2,1,0:T(8,128)S(1)}, f32[2,64,128]{2,1,0:T(8,128)S(1)}, u32[]{:S(2)}, u32[]{:S(2)}) collective-permute-start(f32[2,64,128]{2,1,0:T(8,128)S(1)} %get-tuple-element.32), channel_id=1, source_target_pairs={{1,0},{3,2},{5,4},{7,6},{9,8},{11,10},{13,12},{15,14},{17,16},{19,... | collective-permute-start | bytes 196616 | tf_op jit(solution)/shard_map/ppermute | solution.py:413
